TPU v7x, 32 devices: a whole 2x2x4 slice. The times are simulated.
32 devices in a mesh: grp: 4 (over z), cp: 2 (over x), tp: 4 (over y, core).
Axes of the slice: x: 2, y: 2, z: 4, core: 2. Of those that a mesh axis runs over, the one named last changes fastest.
Arguments:
- inputs: bfloat16 [8, 896, 2048], P('grp', 'cp', 'tp'), may hold values from -6 to 6
- cotangent: bfloat16 [8, 896, 2048], P('grp', 'cp', 'tp'), may hold values from -6 to 6
- attn_gain: bfloat16 [2048], P('cp'), may hold values from 0.25 to 1.75
- query_weight: bfloat16 [2048, 2048], P('cp', 'tp'), may hold values from -0.5 to 0.5
- key_weight: bfloat16 [2048, 512], P('cp', 'tp'), may hold values from -0.5 to 0.5
- value_weight: bfloat16 [2048, 512], P('cp', 'tp'), may hold values from -0.125 to 0.125
- out_weight: bfloat16 [2048, 2048], P('tp', 'cp'), may hold values from -2 to 2
- ffn_gain: bfloat16 [2048], P('cp'), may hold values from 0.25 to 1.75
- gate_weight: bfloat16 [2048, 8192], P('cp', 'tp'), may hold values from -0.125 to 0.125
- up_weight: bfloat16 [2048, 8192], P('cp', 'tp'), may hold values from -0.125 to 0.125
- down_weight: bfloat16 [8192, 2048], P('tp', 'cp'), may hold values from -0.5 to 0.5
- seg_parent: int32 [8, 9], P('grp'), may hold values from 0 to 8, as said below
- seg_start: int32 [8, 9], P('grp'), may hold values from 0 to 832, as said below
- seg_len: int32 [8, 9], P('grp'), may hold values from 64 to 384, as said below
- positions: int32 [8, 896], P('grp'), may hold values from 0 to 511, as said below
Outputs:
- output: bfloat16 [8, 896, 2048], P('grp', 'cp', 'tp')
- input_grad: float32 [8, 896, 2048], P('grp', 'cp', 'tp')
- attn_gain_grad: float32 [2048], P('cp')
- query_grad: float32 [2048, 2048], P('cp', 'tp')
- key_grad: float32 [2048, 512], P('cp', 'tp')
- value_grad: float32 [2048, 512], P('cp', 'tp')
- out_grad: float32 [2048, 2048], P('tp', 'cp')
- ffn_gain_grad: float32 [2048], P('cp')
- gate_grad: float32 [2048, 8192], P('cp', 'tp')
- up_grad: float32 [2048, 8192], P('cp', 'tp')
- down_grad: float32 [8192, 2048], P('tp', 'cp')
Inputs may be any that keep to these rules, and one draw needn't show every extreme that they name: `seg_parent`: segments are numbered in the order in which they lie in their tree. One segment is the trunk and is its own parent; four have the trunk as parent; each of the other four has one of those four as parent, and each of those four is the parent of exactly one. The segments of a tree lie end to end in the order of their numbers, starting at token 0, so seg_start is the running sum of seg_len. `seg_len`: every segment has 64 tokens except the trunk, which has 384. The trunk's tokens have positions 0 to 383 in order; a segment whose parent is the trunk starts at 384, the others at 448, rising by one a token.
All inputs are finite; a program needn't handle non-finite values.
Results may differ from a plain program's by a relative error of at most 0.025.
Values may be sent and summed in bfloat16 or wider, within the bound.
No kernel may reach another device: no remote copies, remote signals or barrier semaphores. Data moves between devices by JAX's collectives and lax.ppermute only.
A program may use at most 320 MiB of HBM per device.

v0:
```python
import jax
import jax.numpy as jnp
from jax import lax
from jax.sharding import PartitionSpec as P

HD = 64


norm_eps = 1e-05
att_scale = 0.015625
resid_scale = 0.22
rope_base = 10000000.0


def rope_tables(position):
    half_dim = HD // 2
    freq_index = jnp.arange(half_dim, dtype=jnp.float32)
    inverse = jnp.power(jnp.float32(rope_base), freq_index * (-2.0 / HD))
    angles = position.astype(jnp.float32)[..., None] * inverse
    cosine_table = jnp.concatenate([jnp.cos(angles), jnp.cos(angles)], axis=-1)[..., None, :]
    sine_table = jnp.concatenate([jnp.sin(angles), jnp.sin(angles)], axis=-1)[..., None, :]
    return (cosine_table, sine_table)


def rotate(values, cosine_table, sine_table):
    half_dim = values.shape[-1] // 2
    turned = jnp.concatenate([-values[..., half_dim:], values[..., :half_dim]], axis=-1)
    return values * cosine_table + turned * sine_table


def to_items(head_vals, kv_count, halves):
    tree_count, row_count, head_count, head_dim = head_vals.shape
    sub_count = head_count // (kv_count * halves)
    shaped = head_vals.reshape(tree_count, row_count, kv_count, halves, sub_count, head_dim)
    shaped = jnp.transpose(shaped, (0, 2, 3, 4, 1, 5))
    return shaped.reshape(tree_count * kv_count * halves, sub_count, row_count, head_dim)


def from_items(item_set, tree_count, kv_count):
    item_count, sub_count, row_count, head_dim = item_set.shape
    halves = item_count // (tree_count * kv_count)
    shaped = item_set.reshape(tree_count, kv_count, halves, sub_count, row_count, head_dim)
    shaped = jnp.transpose(shaped, (0, 4, 1, 2, 3, 5))
    return shaped.reshape(tree_count, row_count, kv_count * halves * sub_count * head_dim)


def key_items(key_block, kv_count, halves):
    tree_count, key_count, col_count = key_block.shape
    head_dim = col_count // kv_count
    shaped = jnp.transpose(
        key_block.reshape(tree_count, key_count, kv_count, head_dim), (0, 2, 1, 3)
    )
    spread = jnp.broadcast_to(
        shaped[:, :, None], (tree_count, kv_count, halves, key_count, head_dim)
    )
    return spread.reshape(tree_count * kv_count * halves, key_count, head_dim)


def key_merge(item_set, tree_count, kv_count):
    item_count, key_count, head_dim = item_set.shape
    shaped = item_set.reshape(
        tree_count, kv_count, item_count // (tree_count * kv_count), key_count, head_dim
    )
    shaped = jnp.sum(shaped, axis=2)
    return jnp.transpose(shaped, (0, 2, 1, 3)).reshape(tree_count, key_count, kv_count * head_dim)


def masked_scores(queries, key_rows, allowed):
    scores = (
        jnp.einsum("grd,nd->grn", queries, key_rows, preferred_element_type=jnp.float32) * att_scale
    )
    return jnp.where(allowed[None], scores, -1e30)


def attend(block_set):
    queries, key_rows, value_rows, allowed = block_set
    scores = masked_scores(queries, key_rows, allowed)
    row_top = jnp.max(scores, axis=-1, keepdims=True)
    powered = jnp.exp(scores - row_top)
    row_sum = jnp.sum(powered, axis=-1, keepdims=True)
    weights = (powered / row_sum).astype(jnp.bfloat16)
    mixture = jnp.einsum("grn,nd->grd", weights, value_rows, preferred_element_type=jnp.float32)
    return (mixture.astype(jnp.bfloat16), row_top[..., 0] + jnp.log(row_sum[..., 0]))


def attend_back(block_set):
    queries, key_rows, value_rows, allowed, log_total, mix_grad = block_set
    scores = masked_scores(queries, key_rows, allowed)
    prob_full = jnp.exp(scores - log_total[..., None])
    prob_low = prob_full.astype(jnp.bfloat16)
    prob_grad = jnp.einsum("grd,nd->grn", mix_grad, value_rows, preferred_element_type=jnp.float32)
    value_part = jnp.einsum("grn,grd->nd", prob_low, mix_grad, preferred_element_type=jnp.float32)
    score_grad = (
        prob_full * (prob_grad - jnp.sum(prob_full * prob_grad, axis=-1, keepdims=True))
    ).astype(jnp.bfloat16)
    query_part = (
        jnp.einsum("grn,nd->grd", score_grad, key_rows, preferred_element_type=jnp.float32)
        * att_scale
    )
    key_part = (
        jnp.einsum("grn,grd->nd", score_grad, queries, preferred_element_type=jnp.float32)
        * att_scale
    )
    return (query_part, key_part, value_part)


def norm_back(norm_grad, normed_unit, inv_scale, gain_vec):
    scaled = norm_grad * gain_vec
    return inv_scale * (
        scaled - normed_unit * jnp.mean(scaled * normed_unit, axis=-1, keepdims=True)
    )


def per_device(
    inputs,
    cotangent,
    attn_gain,
    query_weight,
    key_weight,
    value_weight,
    out_weight,
    ffn_gain,
    gate_weight,
    up_weight,
    down_weight,
    seg_parent,
    seg_start,
    seg_len,
    positions,
):
    tree_count, row_count, part_width = inputs.shape
    key_count = positions.shape[1]
    head_local = query_weight.shape[1] // HD
    kv_local = key_weight.shape[1] // HD
    halves = 2
    single = 1
    first_row = lax.axis_index("cp") * row_count
    column_first = lax.axis_index("tp") * part_width
    cp_count = lax.axis_size("cp")
    grp_count = lax.axis_size("grp")

    def arrange(values):
        last_dim = values.shape[-1]
        split_view = values.reshape(
            values.shape[:-1] + (cp_count, grp_count, last_dim // (cp_count * grp_count))
        )
        return jnp.swapaxes(split_view, -3, -2).reshape(values.shape)

    input_rows_all, cot_rows_all = (
        lax.all_gather(inputs, "tp", axis=2, tiled=True),
        lax.all_gather(cotangent, "tp", axis=2, tiled=True),
    )
    token_ids = jnp.arange(key_count, dtype=jnp.int32)
    segment_end = seg_start + seg_len
    member = (
        (token_ids[None, :, None] >= seg_start[:, None, :])
        & (token_ids[None, :, None] < segment_end[:, None, :])
    ).astype(jnp.float32)
    slot_ids = jnp.arange(seg_parent.shape[1], dtype=jnp.int32)
    grand_parent = jnp.sum(
        jnp.where(seg_parent[:, :, None] == slot_ids[None, None, :], seg_parent[:, None, :], 0),
        axis=2,
    )
    lineage = (
        (slot_ids[None, :, None] == slot_ids[None, None, :])
        | (seg_parent[:, None, :] == slot_ids[None, :, None])
        | (grand_parent[:, None, :] == slot_ids[None, :, None])
    ).astype(jnp.float32)
    member_mine = lax.dynamic_slice_in_dim(member, first_row, row_count, 1)
    reachable = jnp.einsum("tqb,tab->tqa", member_mine, lineage)
    own_pos_all = lax.dynamic_slice_in_dim(positions, first_row, row_count, 1)
    attn_set = (
        lax.all_gather(query_weight, "cp", axis=0, tiled=True),
        lax.all_gather(key_weight, "cp", axis=0, tiled=True),
        lax.all_gather(value_weight, "cp", axis=0, tiled=True),
        lax.all_gather(out_weight, "cp", axis=1, tiled=True),
        lax.all_gather(attn_gain, "cp", axis=0, tiled=True),
    )
    ffn_set = (
        lax.all_gather(gate_weight, "cp", axis=0, tiled=True),
        lax.all_gather(up_weight, "cp", axis=0, tiled=True),
        lax.all_gather(down_weight, "cp", axis=1, tiled=True),
        lax.all_gather(ffn_gain, "cp", axis=0, tiled=True),
    )
    results = []
    input_parts = []
    keep_act, keep_down, keep_normed_ffn, keep_gate, keep_upper = ([], [], [], [], [])
    keep_mix, keep_attn_in, keep_normed_attn, keep_query, keep_key, keep_value = (
        [],
        [],
        [],
        [],
        [],
        [],
    )
    attn_gain_total = None
    ffn_gain_total = None
    for tree in range(tree_count):
        query_full, key_full, value_full, out_full, attn_gain_low = attn_set
        gain_attn_full = attn_gain_low.astype(jnp.float32)
        linked = jnp.einsum("tqa,tka->tqk", reachable[tree : tree + 1], member[tree : tree + 1])
        own_pos = own_pos_all[tree : tree + 1]
        allowed = (linked > 0.5) & (positions[tree : tree + 1, None, :] <= own_pos[:, :, None])
        mask_items = jnp.broadcast_to(
            allowed[:, None], (single, kv_local * halves, row_count, key_count)
        ).reshape(kv_local * halves, row_count, key_count)
        input_wide = input_rows_all[tree : tree + 1].astype(jnp.float32)
        scale_attn = lax.rsqrt(jnp.mean(input_wide * input_wide, axis=-1, keepdims=True) + norm_eps)
        unit_attn = input_wide * scale_attn
        normed_attn = (unit_attn * gain_attn_full).astype(jnp.bfloat16)
        cosine_table, sine_table = rope_tables(own_pos)
        query_raw = jnp.einsum(
            "tnd,dc->tnc", normed_attn, query_full, preferred_element_type=jnp.float32
        )
        key_raw = jnp.einsum(
            "tnd,dc->tnc", normed_attn, key_full, preferred_element_type=jnp.float32
        )
        value_raw = jnp.einsum(
            "tnd,dc->tnc", normed_attn, value_full, preferred_element_type=jnp.float32
        )
        query_rot = rotate(
            query_raw.reshape(single, row_count, head_local, HD), cosine_table, sine_table
        ).astype(jnp.bfloat16)
        key_rot = (
            rotate(key_raw.reshape(single, row_count, kv_local, HD), cosine_table, sine_table)
            .reshape(single, row_count, kv_local * HD)
            .astype(jnp.bfloat16)
        )
        value_low = value_raw.astype(jnp.bfloat16)
        key_set, value_set = (
            lax.all_gather(key_rot, "cp", axis=1, tiled=True),
            lax.all_gather(value_low, "cp", axis=1, tiled=True),
        )
        query_items = to_items(query_rot, kv_local, halves)
        key_stack = key_items(key_set, kv_local, halves)
        value_stack = key_items(value_set, kv_local, halves)
        mix_items, log_totals = lax.map(attend, (query_items, key_stack, value_stack, mask_items))
        mixture = from_items(mix_items, single, kv_local)
        attn_part = jnp.einsum("tnc,cd->tnd", mixture, out_full, preferred_element_type=jnp.float32)
        attn_total = lax.psum(attn_part.astype(jnp.bfloat16), "tp").astype(jnp.float32)
        hidden = input_wide + resid_scale * attn_total
        gate_full, up_full, down_full, ffn_gain_low = ffn_set
        gain_ffn_full = ffn_gain_low.astype(jnp.float32)
        scale_ffn = lax.rsqrt(jnp.mean(hidden * hidden, axis=-1, keepdims=True) + norm_eps)
        unit_ffn = hidden * scale_ffn
        normed_ffn = (unit_ffn * gain_ffn_full).astype(jnp.bfloat16)
        gate_pre = jnp.einsum(
            "tnd,df->tnf", normed_ffn, gate_full, preferred_element_type=jnp.float32
        )
        up_proj = jnp.einsum("tnd,df->tnf", normed_ffn, up_full, preferred_element_type=jnp.float32)
        gate_sig = jax.nn.sigmoid(gate_pre)
        gate_act = gate_pre * gate_sig
        activation = (gate_act * up_proj).astype(jnp.bfloat16)
        down_part = jnp.einsum(
            "tnf,fd->tnd", activation, down_full, preferred_element_type=jnp.float32
        )
        down_mine = lax.psum_scatter(
            down_part.astype(jnp.bfloat16), "tp", scatter_dimension=2, tiled=True
        ).astype(jnp.float32)
        hidden_mine = lax.dynamic_slice_in_dim(hidden, column_first, part_width, 2)
        results.append((hidden_mine + resid_scale * down_mine).astype(jnp.bfloat16))
        back_set = (query_full, key_full, value_full, out_full, gate_full, up_full, down_full)
        query_back, key_back, value_back, out_back, gate_back, up_back, down_back = back_set
        upstream = cot_rows_all[tree : tree + 1].astype(jnp.float32)
        down_in = (resid_scale * upstream).astype(jnp.bfloat16)
        hidden_grad = jnp.einsum(
            "tnd,fd->tnf", down_in, down_back, preferred_element_type=jnp.float32
        )
        gate_in = (hidden_grad * up_proj * gate_sig * (1.0 + gate_pre * (1.0 - gate_sig))).astype(
            jnp.bfloat16
        )
        upper_in = (hidden_grad * gate_act).astype(jnp.bfloat16)
        ffn_norm_part = jnp.einsum(
            "tnf,df->tnd", gate_in, gate_back, preferred_element_type=jnp.float32
        ) + jnp.einsum("tnf,df->tnd", upper_in, up_back, preferred_element_type=jnp.float32)
        ffn_norm_grad = lax.psum(ffn_norm_part.astype(jnp.bfloat16), "tp").astype(jnp.float32)
        ffn_gain_tree = jnp.sum(ffn_norm_grad * unit_ffn, axis=(0, 1))
        hidden_back = upstream + norm_back(ffn_norm_grad, unit_ffn, scale_ffn, gain_ffn_full)
        attn_in = (resid_scale * hidden_back).astype(jnp.bfloat16)
        mix_grad = jnp.einsum(
            "tnd,cd->tnc", attn_in, out_back, preferred_element_type=jnp.float32
        ).astype(jnp.bfloat16)
        grad_items = to_items(mix_grad.reshape(single, row_count, head_local, HD), kv_local, halves)
        query_parts, key_parts, value_parts = lax.map(
            attend_back, (query_items, key_stack, value_stack, mask_items, log_totals, grad_items)
        )
        key_all = key_merge(key_parts, single, kv_local)
        value_all = key_merge(value_parts, single, kv_local)
        key_mine, value_mine = (
            lax.psum_scatter(
                key_all.astype(jnp.bfloat16), "cp", scatter_dimension=1, tiled=True
            ).astype(jnp.float32),
            lax.psum_scatter(
                value_all.astype(jnp.bfloat16), "cp", scatter_dimension=1, tiled=True
            ).astype(jnp.float32),
        )
        query_turned = from_items(query_parts, single, kv_local)
        query_in = (
            rotate(
                query_turned.reshape(single, row_count, head_local, HD), cosine_table, -sine_table
            )
            .reshape(single, row_count, head_local * HD)
            .astype(jnp.bfloat16)
        )
        key_in = (
            rotate(key_mine.reshape(single, row_count, kv_local, HD), cosine_table, -sine_table)
            .reshape(single, row_count, kv_local * HD)
            .astype(jnp.bfloat16)
        )
        value_in = value_mine.astype(jnp.bfloat16)
        attn_norm_part = (
            jnp.einsum("tnc,dc->tnd", query_in, query_back, preferred_element_type=jnp.float32)
            + jnp.einsum("tnc,dc->tnd", key_in, key_back, preferred_element_type=jnp.float32)
            + jnp.einsum("tnc,dc->tnd", value_in, value_back, preferred_element_type=jnp.float32)
        )
        attn_norm_grad = lax.psum(attn_norm_part.astype(jnp.bfloat16), "tp").astype(jnp.float32)
        attn_gain_tree = jnp.sum(attn_norm_grad * unit_attn, axis=(0, 1))
        input_back = hidden_back + norm_back(attn_norm_grad, unit_attn, scale_attn, gain_attn_full)
        input_parts.append(lax.dynamic_slice_in_dim(input_back, column_first, part_width, 2))
        keep_act.append(activation)
        keep_down.append(down_in)
        keep_normed_ffn.append(normed_ffn)
        keep_gate.append(gate_in)
        keep_upper.append(upper_in)
        keep_mix.append(mixture)
        keep_attn_in.append(attn_in)
        keep_normed_attn.append(normed_attn)
        keep_query.append(query_in)
        keep_key.append(key_in)
        keep_value.append(value_in)
        if attn_gain_total is None:
            attn_gain_total = attn_gain_tree
            ffn_gain_total = ffn_gain_tree
        else:
            attn_gain_total = attn_gain_total + attn_gain_tree
            ffn_gain_total = ffn_gain_total + ffn_gain_tree

    def joined(pieces):
        return jnp.concatenate(pieces, axis=0)

    normed_ffn_sorted = arrange(joined(keep_normed_ffn))
    normed_attn_sorted = arrange(joined(keep_normed_attn))
    down_total = jnp.einsum(
        "tnf,tnd->fd",
        joined(keep_act),
        arrange(joined(keep_down)),
        preferred_element_type=jnp.float32,
    )
    gate_total = jnp.einsum(
        "tnd,tnf->df", normed_ffn_sorted, joined(keep_gate), preferred_element_type=jnp.float32
    )
    upper_total = jnp.einsum(
        "tnd,tnf->df", normed_ffn_sorted, joined(keep_upper), preferred_element_type=jnp.float32
    )
    out_total = jnp.einsum(
        "tnc,tnd->cd",
        joined(keep_mix),
        arrange(joined(keep_attn_in)),
        preferred_element_type=jnp.float32,
    )
    query_total = jnp.einsum(
        "tnd,tnc->dc", normed_attn_sorted, joined(keep_query), preferred_element_type=jnp.float32
    )
    key_total = jnp.einsum(
        "tnd,tnc->dc", normed_attn_sorted, joined(keep_key), preferred_element_type=jnp.float32
    )
    value_total = jnp.einsum(
        "tnd,tnc->dc", normed_attn_sorted, joined(keep_value), preferred_element_type=jnp.float32
    )
    totals = (
        arrange(attn_gain_total),
        query_total,
        key_total,
        value_total,
        out_total,
        arrange(ffn_gain_total),
        gate_total,
        upper_total,
        down_total,
    )
    result = jnp.concatenate(results, axis=0)
    input_mine = jnp.concatenate(input_parts, axis=0)
    (
        attn_gain_share,
        query_share,
        key_share,
        value_share,
        out_share,
        ffn_gain_share,
        gate_share,
        upper_share,
        down_share,
    ) = (
        lax.psum_scatter(
            totals[0].astype(jnp.bfloat16), ("grp", "cp"), scatter_dimension=0, tiled=True
        ).astype(jnp.float32),
        lax.psum_scatter(
            totals[1].astype(jnp.bfloat16), ("grp", "cp"), scatter_dimension=0, tiled=True
        ).astype(jnp.float32),
        lax.psum_scatter(
            totals[2].astype(jnp.bfloat16), ("grp", "cp"), scatter_dimension=0, tiled=True
        ).astype(jnp.float32),
        lax.psum_scatter(
            totals[3].astype(jnp.bfloat16), ("grp", "cp"), scatter_dimension=0, tiled=True
        ).astype(jnp.float32),
        lax.psum_scatter(
            totals[4].astype(jnp.bfloat16), ("grp", "cp"), scatter_dimension=1, tiled=True
        ).astype(jnp.float32),
        lax.psum_scatter(
            totals[5].astype(jnp.bfloat16), ("grp", "cp"), scatter_dimension=0, tiled=True
        ).astype(jnp.float32),
        lax.psum_scatter(
            totals[6].astype(jnp.bfloat16), ("grp", "cp"), scatter_dimension=0, tiled=True
        ).astype(jnp.float32),
        lax.psum_scatter(
            totals[7].astype(jnp.bfloat16), ("grp", "cp"), scatter_dimension=0, tiled=True
        ).astype(jnp.float32),
        lax.psum_scatter(
            totals[8].astype(jnp.bfloat16), ("grp", "cp"), scatter_dimension=1, tiled=True
        ).astype(jnp.float32),
    )
    (
        attn_gain_final,
        query_final,
        key_final,
        value_final,
        out_final,
        ffn_gain_final,
        gate_final,
        upper_final,
        down_final,
    ) = (
        lax.all_gather(attn_gain_share.astype(jnp.bfloat16), "grp", axis=0, tiled=True).astype(
            attn_gain_share.dtype
        ),
        lax.all_gather(query_share.astype(jnp.bfloat16), "grp", axis=0, tiled=True).astype(
            query_share.dtype
        ),
        lax.all_gather(key_share.astype(jnp.bfloat16), "grp", axis=0, tiled=True).astype(
            key_share.dtype
        ),
        lax.all_gather(value_share.astype(jnp.bfloat16), "grp", axis=0, tiled=True).astype(
            value_share.dtype
        ),
        lax.all_gather(out_share.astype(jnp.bfloat16), "grp", axis=1, tiled=True).astype(
            out_share.dtype
        ),
        lax.all_gather(ffn_gain_share.astype(jnp.bfloat16), "grp", axis=0, tiled=True).astype(
            ffn_gain_share.dtype
        ),
        lax.all_gather(gate_share.astype(jnp.bfloat16), "grp", axis=0, tiled=True).astype(
            gate_share.dtype
        ),
        lax.all_gather(upper_share.astype(jnp.bfloat16), "grp", axis=0, tiled=True).astype(
            upper_share.dtype
        ),
        lax.all_gather(down_share.astype(jnp.bfloat16), "grp", axis=1, tiled=True).astype(
            down_share.dtype
        ),
    )
    return (
        result,
        input_mine,
        attn_gain_final,
        query_final,
        key_final,
        value_final,
        out_final,
        ffn_gain_final,
        gate_final,
        upper_final,
        down_final,
    )


def solution(mesh):
    in_specs = (
        P("grp", "cp", "tp"),
        P("grp", "cp", "tp"),
        P("cp"),
        P("cp", "tp"),
        P("cp", "tp"),
        P("cp", "tp"),
        P("tp", "cp"),
        P("cp"),
        P("cp", "tp"),
        P("cp", "tp"),
        P("tp", "cp"),
        P("grp", None),
        P("grp", None),
        P("grp", None),
        P("grp", None),
    )
    out_specs = (
        P("grp", "cp", "tp"),
        P("grp", "cp", "tp"),
        P("cp"),
        P("cp", "tp"),
        P("cp", "tp"),
        P("cp", "tp"),
        P("tp", "cp"),
        P("cp"),
        P("cp", "tp"),
        P("cp", "tp"),
        P("tp", "cp"),
    )
    return jax.shard_map(
        per_device, mesh=mesh, in_specs=in_specs, out_specs=out_specs, check_vma=False
    )
```

profile of v0, /device:TPU:0, one launch (start us, length us, event | category | flops | bytes accessed | tf_op | source)
XLA Modules:
  0.0 2066.8 jit_solution(14838279992698763114)
XLA Ops:
  55.4 23.1 %all-gather.21.cloned.1.call-done = bf16[2048,512]{1,0:T(8,128)(2,1)} async-done(((bf16[1024,512]{1,0:T(8,128)(2,1)}), bf16[2048,512]{1,0:T(8,128)(2,1)}) %all-gather.21.cloned.1.call-update) | async-done | bytes 2097168 | tf_op jit(solution)/shard_map/all_gather | solution.py:173
  119.1 23.1 %while.52 = (s32[]{:T(128)}, bf16[4,2,448,64]{2,3,1,0:T(8,128)(2,1)}, f32[4,2,448]{2,1,0:T(2,128)S(1)}, pred[4,448,896]{2,1,0:T(8,128)(4,1)S(1)}, bf16[4,2,448,6...) while((s32[]{:T(128)}, ...), condition=%wide.region_5.6_spmd, body=%wide.region_2.5_spmd.sunk | while | flops 215211136 | bytes 12164709 | solution.py:237
  164.1 15.6 while.53
  194.0 70.1 %all-reduce.14.cloned.1.call-done = (bf16[1,448,2048]{2,1,0:T(8,128)(2,1)}, bf16[1,448,2048]{2,1,0:T(8,128)(2,1)}) async-done(((bf16[1,448,2048]{2,1,0:T(8,128)(2,1)}, bf16[1,448,2048]{2,1,0:T(8,128)(2,1)}), (bf16[1,448,2048]{2,1,0:T(8,128)(2,1)}, bf16[1,448,2048]{2,1,0:T(8,128)(2,1)})) %all-reduce.14.cloned.1.call-update) | async-done | bytes 3670032 | tf_op jit(solution)/shard_map/psum | solution.py:240
  272.7 96.9 %all-gather.25.cloned.1.call-done = bf16[2048,2048]{1,0:T(8,128)(2,1)} async-done(((bf16[1024,2048]{1,0:T(8,128)(2,1)}), bf16[2048,2048]{1,0:T(8,128)(2,1)}) %all-gather.25.cloned.1.call-update) | async-done | bytes 8388624 | tf_op jit(solution)/shard_map/all_gather | solution.py:180
  379.4 95.6 %all-gather.27.cloned.1.call-done = bf16[2048,2048]{1,0:T(8,128)(2,1)} async-done(((bf16[1024,2048]{1,0:T(8,128)(2,1)}), bf16[2048,2048]{1,0:T(8,128)(2,1)}) %all-gather.27.cloned.1.call-update) | async-done | bytes 8388624 | tf_op jit(solution)/shard_map/all_gather | solution.py:181
  508.1 105.5 %all-gather.29.cloned.1.call-done = bf16[2048,2048]{1,0:T(8,128)(2,1)} async-done(((bf16[2048,1024]{1,0:T(8,128)(2,1)}), bf16[2048,2048]{1,0:T(8,128)(2,1)}) %all-gather.29.cloned.1.call-update) | async-done | bytes 8388624 | tf_op jit(solution)/shard_map/all_gather | solution.py:182
  717.6 34.5 %all-reduce.12.cloned.1.call-done = (bf16[1,448,2048]{2,1,0:T(8,128)(2,1)}, bf16[1,448,2048]{2,1,0:T(8,128)(2,1)}) async-done(((bf16[1,448,2048]{2,1,0:T(8,128)(2,1)}, bf16[1,448,2048]{2,1,0:T(8,128)(2,1)}), (bf16[1,448,2048]{2,1,0:T(8,128)(2,1)}, bf16[1,448,2048]{2,1,0:T(8,128)(2,1)})) %all-reduce.12.cloned.1.call-update) | async-done | bytes 3670032 | tf_op jit(solution)/shard_map/psum | solution.py:276
  772.8 25.2 %while.55 = (s32[]{:T(128)}, f32[4,2,448,64]{2,3,1,0:T(8,128)S(1)}, f32[4,896,64]{1,2,0:T(8,128)}, f32[4,896,64]{1,2,0:T(8,128)}, pred[4,448,896]{2,1,0:T(8,128)...) while((s32[]{:T(128)}, f32[4,2,448,64]{2,3,1,0:T(8,128)S(1)}, ...), condition=%wide.region_32.33_spmd, body=%wide.region_30.32_spmd.sunk | while | flops 521141376 | bytes 30571700 | solution.py:284
  806.2 31.5 %while.54 = (s32[]{:T(128)}, f32[4,2,448,64]{2,3,1,0:T(8,128)S(1)}, f32[4,896,64]{1,2,0:T(8,128)}, f32[4,896,64]{1,2,0:T(8,128)}, pred[4,448,896]{2,1,0:T(8,128)...) while((s32[]{:T(128)}, f32[4,2,448,64]{2,3,1,0:T(8,128)S(1)}, ...), condition=%wide.region_21.22_spmd, body=%wide.region_19.21_spmd.sunk | while | flops 521141376 | bytes 28736664 | solution.py:284
  1048.1 125.9 %reduce-scatter.34.cloned.1.call-done = bf16[256,2048]{1,0:T(8,128)(2,1)} async-done(((bf16[2048,2048]{1,0:T(8,128)(2,1)}), bf16[256,2048]{1,0:T(8,128)(2,1)}) %reduce-scatter.34.cloned.1.call-update) | async-done | bytes 1048592 | tf_op jit(solution)/shard_map/reduce_scatter | solution.py:412
  1174.1 150.6 %reduce-scatter.36.cloned.1.call-done = bf16[256,2048]{1,0:T(8,128)(2,1)} async-done(((bf16[2048,2048]{1,0:T(8,128)(2,1)}), bf16[256,2048]{1,0:T(8,128)(2,1)}) %reduce-scatter.36.cloned.1.call-update) | async-done | bytes 1048592 | tf_op jit(solution)/shard_map/reduce_scatter | solution.py:415
  1324.8 151.0 %reduce-scatter.38.cloned.1.call-done = bf16[2048,256]{1,0:T(8,128)(2,1)} async-done(((bf16[2048,2048]{1,0:T(8,128)(2,1)}), bf16[2048,256]{1,0:T(8,128)(2,1)}) %reduce-scatter.38.cloned.1.call-update) | async-done | bytes 1048592 | tf_op jit(solution)/shard_map/reduce_scatter | solution.py:418
  1477.1 64.3 %reduce-scatter.28.cloned.1.call-done = bf16[256,128]{1,0:T(8,128)(2,1)} async-done(((bf16[2048,128]{1,0:T(8,128)(2,1)}), bf16[256,128]{1,0:T(8,128)(2,1)}) %reduce-scatter.28.cloned.1.call-update) | async-done | bytes 65552 | tf_op jit(solution)/shard_map/reduce_scatter | solution.py:400
  1541.4 14.9 all_gather.89
  1557.1 49.7 %reduce-scatter.30.cloned.1.call-done = bf16[256,128]{1,0:T(8,128)(2,1)} async-done(((bf16[2048,128]{1,0:T(8,128)(2,1)}), bf16[256,128]{1,0:T(8,128)(2,1)}) %reduce-scatter.30.cloned.1.call-update) | async-done | bytes 65552 | tf_op jit(solution)/shard_map/reduce_scatter | solution.py:403
  1606.8 14.5 all_gather.90
  1622.2 16.5 reduce-scatter.16.cloned.1.call-done
  1640.1 30.7 %reduce-scatter.14.cloned.1.call-done = bf16[1,448,512]{2,1,0:T(8,128)(2,1)} async-done(((bf16[1,448,2048]{2,1,0:T(8,128)(2,1)}), bf16[1,448,512]{2,1,0:T(8,128)(2,1)}) %reduce-scatter.14.cloned.1.call-update) | async-done | bytes 458768 | tf_op jit(solution)/shard_map/reduce_scatter | solution.py:257
  1673.3 77.0 %all-reduce.10.cloned.1.call-done = (bf16[1,448,2048]{2,1,0:T(8,128)(2,1)}, bf16[1,448,2048]{2,1,0:T(8,128)(2,1)}) async-done(((bf16[1,448,2048]{2,1,0:T(8,128)(2,1)}, bf16[1,448,2048]{2,1,0:T(8,128)(2,1)}), (bf16[1,448,2048]{2,1,0:T(8,128)(2,1)}, bf16[1,448,2048]{2,1,0:T(8,128)(2,1)})) %all-reduce.10.cloned.1.call-update) | async-done | bytes 3670032 | tf_op jit(solution)/shard_map/psum | solution.py:316
  1757.7 22.9 %all-reduce.2 = (bf16[2048]{0:T(1024)(128)(2,1)S(1)}, bf16[2048]{0:T(1024)(128)(2,1)S(1)}) all-reduce(bf16[2048]{0:T(1024)(128)(2,1)S(1)} %bitcast.629, bf16[2048]{0:T(1024)(128)(2,1)S(1)} %bitcast.628), channel_id=12, replica_groups=mesh['grp'=4,'cp'=2,'tp'=4] {'grp','cp'}, use_global_device_ids=true, to_apply=%region_41.42.clone | all-reduce | flops 4096 | bytes 16384
  1814.1 77.7 %all-gather.37.cloned.1.call-done = bf16[1024,2048]{1,0:T(8,128)(2,1)} async-done(((bf16[256,2048]{1,0:T(8,128)(2,1)}), bf16[1024,2048]{1,0:T(8,128)(2,1)}) %all-gather.37.cloned.1.call-update) | async-done | bytes 4194320 | tf_op jit(solution)/shard_map/all_gather | solution.py:451
  1898.5 74.0 %all-gather.39.cloned.1.call-done = bf16[1024,2048]{1,0:T(8,128)(2,1)} async-done(((bf16[256,2048]{1,0:T(8,128)(2,1)}), bf16[1024,2048]{1,0:T(8,128)(2,1)}) %all-gather.39.cloned.1.call-update) | async-done | bytes 4194320 | tf_op jit(solution)/shard_map/all_gather | solution.py:454
  1979.2 74.0 %all-gather.41.cloned.1.call-done = bf16[2048,1024]{1,0:T(8,128)(2,1)} async-done(((bf16[2048,256]{1,0:T(8,128)(2,1)}), bf16[2048,1024]{1,0:T(8,128)(2,1)}) %all-gather.41.cloned.1.call-update) | async-done | bytes 4194320 | tf_op jit(solution)/shard_map/all_gather | solution.py:457
  (588 shorter events, 680.3 us)
Async XLA Ops:
  9.4 254.7 %all-reduce.14.cloned.1.call-start = ((), (), s32[]{:S(2)}) async-start(), calls=%async_computation.40 | async-start | bytes 7340032 | tf_op jit(solution)/shard_map/psum | solution.py:240
  186.9 182.7 %all-gather.25.cloned.1.call-start = ((), (), s32[]{:S(2)}) async-start(), calls=%async_computation.16 | async-start | bytes 12582912 | tf_op jit(solution)/shard_map/all_gather | solution.py:180
  187.5 287.5 %all-gather.27.cloned.1.call-start = ((), (), s32[]{:S(2)}) async-start(), calls=%async_computation.17 | async-start | bytes 12582912 | tf_op jit(solution)/shard_map/all_gather | solution.py:181
  188.1 320.0 %all-gather.31.cloned.1.call-start = ((), (), s32[]{:S(2)}) async-start(), calls=%async_computation.21 | async-start | bytes 4587520 | tf_op jit(solution)/shard_map/all_gather | solution.py:151
  188.8 424.8 %all-gather.29.cloned.1.call-start = ((), (), s32[]{:S(2)}) async-start(), calls=%async_computation.18 | async-start | bytes 12582912 | tf_op jit(solution)/shard_map/all_gather | solution.py:182
  189.6 562.5 %all-reduce.12.cloned.1.call-start = ((), (), s32[]{:S(2)}) async-start(), calls=%async_computation.39 | async-start | bytes 7340032 | tf_op jit(solution)/shard_map/psum | solution.py:276
  674.9 326.6 %reduce-scatter.22.cloned.1.call-start = ((), (), s32[]{:S(2)}) async-start(), calls=%async_computation.24 | async-start | bytes 344064 | tf_op jit(solution)/shard_map/reduce_scatter | solution.py:290
  800.5 202.9 %reduce-scatter.18.cloned.1.call-start = ((), (), s32[]{:S(2)}) async-start(), calls=%async_computation.22 | async-start | bytes 344064 | tf_op jit(solution)/shard_map/reduce_scatter | solution.py:290
  839.9 172.7 %reduce-scatter.24.cloned.1.call-start = ((), (), s32[]{:S(2)}) async-start(), calls=%async_computation.25 | async-start | bytes 344064 | tf_op jit(solution)/shard_map/reduce_scatter | solution.py:293
  852.9 193.9 %reduce-scatter.26.cloned.1.call-start = ((), (), s32[]{:S(2)}) async-start(), calls=%async_computation.26 | async-start | bytes 2359296 | tf_op jit(solution)/shard_map/reduce_scatter | solution.py:397
  862.1 185.3 %reduce-scatter.32.cloned.1.call-start = ((), (), s32[]{:S(2)}) async-start(), calls=%async_computation.30 | async-start | bytes 2359296 | tf_op jit(solution)/shard_map/reduce_scatter | solution.py:406
  898.4 275.7 %reduce-scatter.34.cloned.1.call-start = ((), (), s32[]{:S(2)}) async-start(), calls=%async_computation.32 | async-start | bytes 9437184 | tf_op jit(solution)/shard_map/reduce_scatter | solution.py:412
  938.7 386.0 %reduce-scatter.36.cloned.1.call-start = ((), (), s32[]{:S(2)}) async-start(), calls=%async_computation.34 | async-start | bytes 9437184 | tf_op jit(solution)/shard_map/reduce_scatter | solution.py:415
  952.6 523.2 %reduce-scatter.38.cloned.1.call-start = ((), (), s32[]{:S(2)}) async-start(), calls=%async_computation.36 | async-start | bytes 9437184 | tf_op jit(solution)/shard_map/reduce_scatter | solution.py:418
  992.9 548.5 %reduce-scatter.28.cloned.1.call-start = ((), (), s32[]{:S(2)}) async-start(), calls=%async_computation.28 | async-start | bytes 589824 | tf_op jit(solution)/shard_map/reduce_scatter | solution.py:400
  1012.2 594.6 %reduce-scatter.30.cloned.1.call-start = ((), (), s32[]{:S(2)}) async-start(), calls=%async_computation.29 | async-start | bytes 589824 | tf_op jit(solution)/shard_map/reduce_scatter | solution.py:403
  1016.8 621.9 %reduce-scatter.16.cloned.1.call-start = ((), (), s32[]{:S(2)}) async-start(), calls=%async_computation.20 | async-start | bytes 2293760 | tf_op jit(solution)/shard_map/reduce_scatter | solution.py:257
  1026.1 644.7 %reduce-scatter.14.cloned.1.call-start = ((), (), s32[]{:S(2)}) async-start(), calls=%async_computation.19 | async-start | bytes 2293760 | tf_op jit(solution)/shard_map/reduce_scatter | solution.py:257
  1035.3 714.9 %all-reduce.10.cloned.1.call-start = ((), (), s32[]{:S(2)}) async-start(), calls=%async_computation.38 | async-start | bytes 7340032 | tf_op jit(solution)/shard_map/psum | solution.py:316
  1046.8 758.2 %all-gather.33.cloned.1.call-start = ((), (), s32[]{:S(2)}) async-start(), calls=%async_computation.27 | async-start | bytes 1310720 | tf_op jit(solution)/shard_map/all_gather | solution.py:436
  1047.3 764.0 %all-gather.35.cloned.1.call-start = ((), (), s32[]{:S(2)}) async-start(), calls=%async_computation.31 | async-start | bytes 1310720 | tf_op jit(solution)/shard_map/all_gather | solution.py:445
  1048.1 843.8 %all-gather.37.cloned.1.call-start = ((), (), s32[]{:S(2)}) async-start(), calls=%async_computation.33 | async-start | bytes 5242880 | tf_op jit(solution)/shard_map/all_gather | solution.py:451
  1174.1 798.4 %all-gather.39.cloned.1.call-start = ((), (), s32[]{:S(2)}) async-start(), calls=%async_computation.35 | async-start | bytes 5242880 | tf_op jit(solution)/shard_map/all_gather | solution.py:454
  1324.7 728.4 %all-gather.41.cloned.1.call-start = ((), (), s32[]{:S(2)}) async-start(), calls=%async_computation.37 | async-start | bytes 5242880 | tf_op jit(solution)/shard_map/all_gather | solution.py:457
  (103 other events, 3333.6 us)
Sparse Core Ops, SparseCore 0:
  9.6 34.1 all-gather.18
  45.4 33.0 all-gather.20
  80.0 37.9 all-gather.22
  187.0 77.0 all-reduce.13
  265.5 104.0 all-gather.24
  371.0 103.9 all-gather.26
  476.6 31.4 all-gather.30
  509.6 103.9 all-gather.28
  675.1 76.9 all-reduce.11
  882.7 68.4 reduce-scatter.25
  955.1 68.2 reduce-scatter.31
  1027.4 146.5 reduce-scatter.33
  1178.1 146.5 reduce-scatter.35
  1328.7 146.9 reduce-scatter.37
  1479.7 61.6 reduce-scatter.27
  1545.1 61.6 reduce-scatter.29
  1609.9 28.6 reduce-scatter.15
  1641.2 29.5 reduce-scatter.13
  1673.2 76.9 all-reduce.9
  1751.7 28.4 all-gather.32
  1781.7 29.6 all-gather.34
  1812.8 79.0 all-gather.36
  1893.3 79.2 all-gather.38
  1974.1 79.0 all-gather.40
  (4 shorter events, 45.5 us)
where the time goes:
time: 2080 us; the launch traced here: 2070 us
  waiting for transfers between devices  1340 us (64%)
  matrix products  280 us (13%)
  local copies, waits for them, and re-layouts  170 us (8%)
  other arithmetic  133 us (6%)
  blocking collectives  124 us (6%)
    reduce_scatter x1, waiting for transfers between devices, per_device(): lax.psum_scatter(totals[8].astype(jnp.bfloat16), ('grp', 'cp'), scatter_d...  151 us
    reduce_scatter x1, waiting for transfers between devices, per_device(): lax.psum_scatter(totals[7].astype(jnp.bfloat16), ('grp', 'cp'), scatter_d...  151 us
    reduce_scatter x1, waiting for transfers between devices, per_device(): lax.psum_scatter(totals[6].astype(jnp.bfloat16), ('grp', 'cp'), scatter_d...  126 us
    all_gather x1, waiting for transfers between devices, per_device(): lax.all_gather(down_weight, 'cp', axis=1, tiled=True)  106 us
    all_gather x1, waiting for transfers between devices, per_device(): lax.all_gather(gate_weight, 'cp', axis=0, tiled=True)  96.9 us
    all_gather x1, waiting for transfers between devices, per_device(): lax.all_gather(up_weight, 'cp', axis=0, tiled=True)  95.6 us
    all_gather x1, waiting for transfers between devices, per_device(): lax.all_gather(gate_share.astype(jnp.bfloat16), 'grp', axis=0, tiled=True)  77.7 us
    psum x1, waiting for transfers between devices, per_device(): lax.psum(attn_norm_part.astype(jnp.bfloat16), 'tp').astype(jnp.float32)  77 us
  transfers between devices with their start and end apart: 28, of which 20 were waited for; matrix products, arithmetic and copies ran while one was open for 22% of the time, Pallas kernels for 0%

commit v1 on v0

v1 whole, which is shorter than its diff:
```python
import functools
import math

import jax
import jax.numpy as jnp
from jax import lax
from jax.experimental import pallas as pl
from jax.experimental.pallas import tpu as pltpu
from jax.sharding import PartitionSpec as P

HD = 64

norm_eps = 1e-05
att_scale = 0.015625
resid_scale = 0.22
rope_base = 10000000.0
masked_score = -1e30

low = jnp.bfloat16
wide = jnp.float32


def tie(value, *earlier):
    return lax.optimization_barrier((value,) + earlier)[0] if earlier else value


class Lane:
    def __init__(self, depth):
        self.depth = depth
        self.done = []

    def move(self, block, axis, pairs, *earlier):
        if len(self.done) >= self.depth:
            earlier = (self.done[-self.depth],) + earlier
        self.done.append(lax.ppermute(tie(block, *earlier), axis, pairs))
        return self.done[-1]


class Clock:
    def __init__(self):
        self.last = ()

    def run(self, function, *given):
        given = lax.optimization_barrier(given + self.last)[: len(given)]
        result = function(*given)
        self.last = (jax.tree.leaves(result)[0],)
        return result


def cp_fetch(lane, block):
    count = lax.axis_size("cp")
    return [
        lane.move(block, "cp", [((i + s) % count, i) for i in range(count)])
        for s in range(1, count)
    ]


def cp_deliver(lane, block, shift):
    count = lax.axis_size("cp")
    return lane.move(block, "cp", [(i, (i + shift) % count) for i in range(count)])


def in_order(flag, first, second):
    return [jnp.where(flag, first, second), jnp.where(flag, second, first)]


class LineGather:
    def __init__(self, lane, block, *earlier):
        self.lane, self.block = lane, block
        self.near = lane.move(block, "grp", [(0, 1), (1, 0), (2, 3), (3, 2)], *earlier)
        self.pair = jnp.concatenate(in_order(lax.axis_index("grp") % 2 == 0, block, self.near), axis=0)

    def across(self, *earlier):
        self.far = self.lane.move(self.pair, "grp", [(1, 2), (2, 1)], *earlier)

    def out(self, *earlier):
        self.passed = self.lane.move(self.far, "grp", [(1, 0), (2, 3)], *earlier)


def assemble_kernel(here_ref, own_ref, *refs, own_blocks, straight_blocks, share_blocks, beside):
    step, here = pl.program_id(0), here_ref[0]
    straight = refs[:1] if straight_blocks else ()
    share_ref, near_ref, far_ref, passed_ref, out_ref = refs[len(straight) :]
    width = own_ref.shape[1]
    at = step if beside else step - own_blocks
    target = out_ref.at[:, width:] if beside else out_ref
    if beside:
        out_ref[:, :width] = own_ref[...]
    else:

        @pl.when(at < 0)
        def _():
            target[...] = own_ref[...]

    if straight:

        @pl.when((at >= 0) & (at < straight_blocks))
        def _():
            target[...] = straight[0][...]

    place = at - straight_blocks
    owner = lax.div(jnp.maximum(place, 0), share_blocks)
    there = place >= 0
    near = owner == here + 1 - 2 * lax.rem(here, 2)
    apart = lax.div(owner, 2) != lax.div(here, 2)
    inner = (here == 1) | (here == 2)

    @pl.when(there & (owner == here))
    def _():
        target[...] = share_ref[...]

    @pl.when(there & near)
    def _():
        target[...] = near_ref[...]

    @pl.when(there & apart & inner)
    def _():
        target[...] = far_ref[...]

    @pl.when(there & apart & jnp.logical_not(inner))
    def _():
        target[...] = passed_ref[...]


def assemble_shared(weight, straight, line, beside):
    share = line.block.shape[0]
    rows, width = weight.shape
    direct = straight[0].shape[0] if straight else 0
    unit = math.gcd(math.gcd(rows, direct), share)
    own_blocks, straight_blocks, share_blocks = rows // unit, direct // unit, share // unit
    offset = straight_blocks + (0 if beside else own_blocks)
    spec = lambda first, count: pl.BlockSpec(
        (unit, width), lambda i, here: (jnp.clip(i - first(here[0]), 0, count - 1), 0)
    )
    own_spec = spec(lambda z: 0, own_blocks)
    straight_spec = [spec(lambda z: offset - straight_blocks, straight_blocks)] if direct else []
    pair_first = lambda z: offset + (2 - 2 * lax.div(z, 2)) * share_blocks
    specs = [own_spec] + straight_spec + [
        spec(lambda z: offset + z * share_blocks, share_blocks),
        spec(lambda z: offset + (z + 1 - 2 * lax.rem(z, 2)) * share_blocks, share_blocks),
        spec(pair_first, 2 * share_blocks),
        spec(pair_first, 2 * share_blocks),
    ]
    out_shape = (rows, 2 * width) if beside else (2 * rows, width)
    return pl.pallas_call(
        functools.partial(
            assemble_kernel,
            own_blocks=own_blocks,
            straight_blocks=straight_blocks,
            share_blocks=share_blocks,
            beside=beside,
        ),
        grid_spec=pltpu.PrefetchScalarGridSpec(
            num_scalar_prefetch=1,
            grid=(out_shape[0] // unit,),
            in_specs=specs,
            out_specs=pl.BlockSpec((unit, out_shape[1]), lambda i, here: (i, 0)),
        ),
        out_shape=jax.ShapeDtypeStruct(out_shape, weight.dtype),
        cost_estimate=pl.CostEstimate(
            flops=0, bytes_accessed=8 * rows * width + 2 * share * width, transcendentals=0
        ),
        name="assemble",
    )(
        lax.axis_index("grp").astype(jnp.int32).reshape(1),
        weight,
        *straight,
        line.block,
        line.near,
        line.far,
        line.passed,
    )


class LineSum:
    lag = 3

    def __init__(self, clock):
        here = lax.axis_index("grp")
        self.inner = (here == 1) | (here == 2)
        self.clock = clock
        self.parts, self.sums, self.totals = [], [], []
        self.ins, self.acrosses, self.outs, self.loads = [], [], [], []

    def load(self, part):
        self.parts.append(part)
        back = len(self.parts) - 1 - self.lag
        total = self.totals[back] if back >= 0 else None
        if part is None or total is None or part.shape[1] != total.shape[1]:
            self.loads.append((part, total))
            return
        height = max(part.shape[0], total.shape[0])

        def choose(part, total):
            fill = lambda v: jnp.pad(v, ((0, height - v.shape[0]), (0, 0)))
            return jnp.where(self.inner, fill(total), fill(part))

        self.loads.append(self.clock.run(choose, part, total))

    def step(self):
        count = len(self.loads) - 1
        before = self.ins[-1:] + self.outs[-1:]
        load = self.loads[count]
        if isinstance(load, tuple):
            part, total = load
            if part is not None:
                self.ins.append(lax.ppermute(tie(part, *before), "grp", [(0, 1), (3, 2)]))
            if total is not None:
                self.outs.append(lax.ppermute(tie(total, *before), "grp", [(1, 0), (2, 3)]))
        else:
            side = lax.ppermute(tie(load, *before), "grp", [(0, 1), (1, 0), (2, 3), (3, 2)])
            self.ins.append(side)
            self.outs.append(side)
        if count >= 1 and self.parts[count - 1] is not None:
            part, got = self.parts[count - 1], self.ins[count - 1]
            total = self.clock.run(lambda p, g: p + g[: p.shape[0]], part, got)
            self.sums.append(total)
            self.acrosses.append(
                lax.ppermute(tie(total, *self.acrosses[-1:]), "grp", [(1, 2), (2, 1)])
            )
        if count >= 2 and self.parts[count - 2] is not None:
            self.totals.append(
                self.clock.run(lambda a, b: a + b, self.sums[count - 2], self.acrosses[count - 2])
            )

    def final(self, index):
        total, got = self.totals[index], self.outs[index]
        return jnp.where(self.inner, total, got[: total.shape[0]]).astype(wide)


def tp_swap(block, bit, *earlier):
    count = lax.axis_size("tp")
    return lax.ppermute(tie(block, *earlier), "tp", [(i, i ^ bit) for i in range(count)])


class TpTotal:
    def __init__(self, part):
        self.plain = None
        if lax.axis_size("tp") != 4:
            self.plain = lax.psum(part.astype(low), "tp")
            return
        half = part.shape[0] // 2
        self.odd = lax.axis_index("tp") % 2
        self.mine = lax.dynamic_slice_in_dim(part, self.odd * half, half, 0)
        theirs = lax.dynamic_slice_in_dim(part, (1 - self.odd) * half, half, 0)
        self.got = tp_swap(theirs.astype(low), 1)

    def across(self, *earlier):
        if self.plain is None:
            self.pair = (self.mine.astype(wide) + self.got.astype(wide)).astype(low)
            self.far = tp_swap(self.pair, 2, *earlier)
            return self.far
        return self.plain

    def back(self, *earlier):
        if self.plain is None:
            self.total = (self.pair.astype(wide) + self.far.astype(wide)).astype(low)
            self.other = tp_swap(self.total, 1, *earlier)
            return self.other
        return self.plain

    def value(self):
        if self.plain is None:
            return jnp.concatenate(in_order(self.odd == 0, self.total, self.other), axis=0)
        return self.plain


def attend_kernel(
    q_ref, k_ref, v_ref, row_ref, col_ref, o_ref, lse_ref, bias_ref, *, per_kv
):
    step = pl.program_id(0)
    group = (2 * step) // per_kv

    @pl.when(step == 0)
    def _():
        seg, par, grand, pos = (row_ref[:, i : i + 1] for i in range(4))
        key_seg, key_pos = col_ref[0:1, :], col_ref[1:2, :]
        linked = (key_seg == seg) | (key_seg == par) | (key_seg == grand)
        bias_ref[...] = jnp.where(linked & (key_pos <= pos), 0.0, masked_score)

    k = jnp.where(group == 0, k_ref[:, :HD], k_ref[:, HD : 2 * HD])
    v = jnp.where(group == 0, v_ref[:, :HD], v_ref[:, HD : 2 * HD])
    outs, totals = [], []
    for h in range(2):
        q = q_ref[:, h * HD : (h + 1) * HD]
        s = lax.dot_general(q, k, (((1,), (1,)), ((), ())), preferred_element_type=wide)
        s = s + bias_ref[...]
        top = jnp.max(s, axis=-1, keepdims=True)
        p = jnp.exp(s - top)
        norm = jnp.sum(p, axis=-1, keepdims=True)
        o = jnp.dot(p.astype(low), v, preferred_element_type=wide)
        outs.append(o / norm)
        totals.append(top + jnp.log(norm))
    o_ref[...] = jnp.concatenate(outs, axis=1).astype(low)
    lse_ref[...] = jnp.concatenate([jnp.broadcast_to(t, (t.shape[0], HD)) for t in totals], axis=1)


def attend(q, k, v, row_meta, col_meta, per_kv):
    rows, width = q.shape
    keys, kv_width = k.shape
    pairs = width // (2 * HD)
    whole = lambda a: pl.BlockSpec(a.shape, lambda j: (0, 0))
    tile = pl.BlockSpec((rows, 2 * HD), lambda j: (0, j))
    heads = 2 * pairs
    return pl.pallas_call(
        functools.partial(attend_kernel, per_kv=per_kv),
        grid=(pairs,),
        in_specs=[tile, whole(k), whole(v), whole(row_meta), whole(col_meta)],
        out_specs=[tile, tile],
        out_shape=[
            jax.ShapeDtypeStruct((rows, width), low),
            jax.ShapeDtypeStruct((rows, width), wide),
        ],
        scratch_shapes=[pltpu.VMEM((rows, keys), wide)],
        cost_estimate=pl.CostEstimate(
            flops=16 * heads * rows * keys * HD,
            bytes_accessed=8 * rows * width + 4 * keys * kv_width,
            transcendentals=heads * rows * keys,
        ),
        name="attend",
    )(q, k, v, row_meta, col_meta)


def attend_back_kernel(
    q_ref, k_ref, v_ref, g_ref, lse_ref, row_ref, col_ref, dq_ref, dk_ref, dv_ref, bias_ref, dk_sum, dv_sum, *, per_kv
):
    step = pl.program_id(0)
    group = (2 * step) // per_kv
    pairs_kv = per_kv // 2

    @pl.when(step == 0)
    def _():
        seg, par, grand, pos = (row_ref[i : i + 1, :] for i in range(4))
        key_seg, key_pos = col_ref[:, 0:1], col_ref[:, 1:2]
        linked = (key_seg == seg) | (key_seg == par) | (key_seg == grand)
        bias_ref[...] = jnp.where(linked & (key_pos <= pos), 0.0, masked_score)

    k = jnp.where(group == 0, k_ref[:, :HD], k_ref[:, HD : 2 * HD])
    v = jnp.where(group == 0, v_ref[:, :HD], v_ref[:, HD : 2 * HD])
    outs = []
    dk = jnp.zeros(k.shape, wide)
    dv = jnp.zeros(k.shape, wide)
    nt = (((1,), (1,)), ((), ()))
    for h in range(2):
        q = q_ref[:, h * HD : (h + 1) * HD]
        g = g_ref[:, h * HD : (h + 1) * HD]
        s = lax.dot_general(k, q, nt, preferred_element_type=wide) + bias_ref[...]
        p = jnp.exp(s - lse_ref[0, h : h + 1, :])
        dp = lax.dot_general(v, g, nt, preferred_element_type=wide)
        dv = dv + jnp.dot(p.astype(low), g, preferred_element_type=wide)
        mean = jnp.sum(p * dp, axis=0, keepdims=True)
        dz = (p * (dp - mean)).astype(low)
        dk = dk + jnp.dot(dz, q, preferred_element_type=wide)
        dq = lax.dot_general(dz, k, (((0,), (0,)), ((), ())), preferred_element_type=wide)
        outs.append(dq * att_scale)
    dq_ref[...] = jnp.concatenate(outs, axis=1)
    first = lax.rem(step, pairs_kv) == 0

    @pl.when(first)
    def _():
        dk_sum[...] = dk
        dv_sum[...] = dv

    @pl.when(jnp.logical_not(first))
    def _():
        dk_sum[...] += dk
        dv_sum[...] += dv

    for which in range(2):

        @pl.when(step == (which + 1) * pairs_kv - 1)
        def _():
            dk_ref[:, which * HD : (which + 1) * HD] = dk_sum[...]
            dv_ref[:, which * HD : (which + 1) * HD] = dv_sum[...]


def attend_back(q, k, v, g, lse, row_meta, col_meta, per_kv):
    rows, width = q.shape
    keys, kv_width = k.shape
    pairs = width // (2 * HD)
    heads = 2 * pairs
    whole = lambda a: pl.BlockSpec(a.shape, lambda j: (0, 0))
    tile = pl.BlockSpec((rows, 2 * HD), lambda j: (0, j))
    return pl.pallas_call(
        functools.partial(attend_back_kernel, per_kv=per_kv),
        grid=(pairs,),
        in_specs=[
            tile,
            whole(k),
            whole(v),
            tile,
            pl.BlockSpec((1, 2, rows), lambda j: (j, 0, 0)),
            whole(row_meta),
            whole(col_meta),
        ],
        out_specs=[tile, whole(k), whole(v)],
        out_shape=[
            jax.ShapeDtypeStruct((rows, width), wide),
            jax.ShapeDtypeStruct((keys, kv_width), wide),
            jax.ShapeDtypeStruct((keys, kv_width), wide),
        ],
        scratch_shapes=[
            pltpu.VMEM((keys, rows), wide),
            pltpu.VMEM((keys, HD), wide),
            pltpu.VMEM((keys, HD), wide),
        ],
        cost_estimate=pl.CostEstimate(
            flops=40 * heads * rows * keys * HD,
            bytes_accessed=8 * rows * width + 12 * keys * kv_width,
            transcendentals=heads * rows * keys,
        ),
        name="attend_back",
    )(q, k, v, g, lse, row_meta, col_meta)


def rope_tables(position, repeats):
    half_dim = HD // 2
    freq_index = jnp.arange(half_dim, dtype=wide)
    inverse = jnp.power(wide(rope_base), freq_index * (-2.0 / HD))
    angles = position.astype(wide)[:, None] * inverse
    tile = lambda table: jnp.tile(table, (1, 2 * repeats))
    return tile(jnp.cos(angles)), tile(jnp.sin(angles))


def turn(values):
    half_dim = HD // 2
    front = lax.broadcasted_iota(jnp.int32, values.shape, 1) % HD < half_dim
    return jnp.where(
        front, -jnp.roll(values, -half_dim, axis=1), jnp.roll(values, half_dim, axis=1)
    )


def norm_back(norm_grad, normed_unit, inv_scale, gain_vec):
    scaled = norm_grad * gain_vec
    return inv_scale * (
        scaled - normed_unit * jnp.mean(scaled * normed_unit, axis=-1, keepdims=True)
    )


def matmul(a, b):
    return jnp.dot(a, b, preferred_element_type=wide)


def matmul_nt(a, b):
    return lax.dot_general(a, b, (((1,), (1,)), ((), ())), preferred_element_type=wide)


def matmul_tn(a, b):
    return lax.dot_general(a, b, (((0,), (0,)), ((), ())), preferred_element_type=wide)


def tree_segments(seg_parent, seg_start, seg_len, key_count):
    token_ids = jnp.arange(key_count, dtype=jnp.int32)
    slot_ids = jnp.arange(seg_parent.shape[1], dtype=jnp.int32)
    member = (token_ids[None, :, None] >= seg_start[:, None, :]) & (
        token_ids[None, :, None] < (seg_start + seg_len)[:, None, :]
    )
    pick = lambda table: jnp.sum(jnp.where(member, table[:, None, :], 0), axis=2)
    grand_parent = jnp.sum(
        jnp.where(seg_parent[:, :, None] == slot_ids[None, None, :], seg_parent[:, None, :], 0),
        axis=2,
    )
    return (
        pick(jnp.broadcast_to(slot_ids[None, :], seg_parent.shape)),
        pick(seg_parent),
        pick(grand_parent),
    )


def per_device(
    inputs,
    cotangent,
    attn_gain,
    query_weight,
    key_weight,
    value_weight,
    out_weight,
    ffn_gain,
    gate_weight,
    up_weight,
    down_weight,
    seg_parent,
    seg_start,
    seg_len,
    positions,
):
    trees, rows, part_width = inputs.shape
    keys = positions.shape[1]
    block = attn_gain.shape[0]
    cp_count, tp_count, grp_count = lax.axis_size("cp"), lax.axis_size("tp"), lax.axis_size("grp")
    model_width = block * cp_count
    q_width, kv_width = query_weight.shape[1], key_weight.shape[1]
    per_kv = q_width // kv_width
    tokens = trees * rows
    cp_here, tp_here = lax.axis_index("cp"), lax.axis_index("tp")

    def rolled(values):
        return lax.dynamic_slice_in_dim(
            jnp.concatenate([values, values], axis=-1), cp_here * block, model_width, values.ndim - 1
        )

    def width_part(values, owner):
        start = (owner * part_width - cp_here * block) % model_width
        if block % part_width:
            values = jnp.concatenate([values, values], axis=-1)
        return lax.dynamic_slice_in_dim(values, start, part_width, 1)

    def tp_width(shard, *earlier):
        shard = tie(shard.reshape(tokens, part_width), *earlier)
        if tp_count != 4:
            return rolled(lax.all_gather(shard, "tp", axis=1, tiled=True)), shard
        far = tp_swap(shard, 2)
        near = tp_swap(jnp.stack([shard, far]), 1)
        pieces = [shard, near[0], far, near[1]]
        picks = [lax.select_n(tp_here, *[pieces[j ^ m] for m in range(4)]) for j in range(4)]
        return rolled(jnp.concatenate(picks, axis=1)), far

    def tp_scatter(part):
        if tp_count != 4:
            natural = lax.dynamic_slice_in_dim(
                jnp.concatenate([part, part], axis=-1),
                (model_width - cp_here * block) % model_width,
                model_width,
                1,
            )
            return lax.psum_scatter(
                natural.astype(low), "tp", scatter_dimension=1, tiled=True
            ).astype(wide)
        sent = jnp.concatenate([width_part(part, tp_here ^ 1), width_part(part, tp_here ^ 3)], axis=1)
        got = tp_swap(sent.astype(low), 1).astype(wide)
        kept = width_part(part, tp_here) + got[:, :part_width]
        passed = width_part(part, tp_here ^ 2) + got[:, part_width:]
        return kept + tp_swap(passed.astype(low), 2).astype(wide)

    lane, line = Lane(2), Lane(2)
    shared = cp_count == 2 and grp_count == 4

    def share_of(weight, direct):
        if not shared:
            return None
        share = (weight.shape[0] - direct) // grp_count
        start = direct + lax.axis_index("grp") * share
        return cp_fetch(lane, lax.dynamic_slice_in_dim(weight, start, share, 0))[0]

    def direct_of(weight, direct):
        if not shared:
            return cp_fetch(lane, weight)
        return cp_fetch(lane, weight[:direct]) if direct else []

    def assemble(weight, straight, gathered, beside):
        if shared:
            return assemble_shared(weight, straight, gathered, beside)
        return jnp.concatenate([weight] + straight, axis=1 if beside else 0)

    qkv_own = jnp.concatenate([query_weight, key_weight, value_weight], axis=1)
    gains_own = jnp.stack([attn_gain, ffn_gain])
    up_direct, down_direct = up_weight.shape[0] // 2, down_weight.shape[0] // 4
    input_rows, input_far = tp_width(inputs)
    gains = jnp.concatenate([gains_own] + cp_fetch(lane, gains_own), axis=1).astype(wide)
    attn_gain_full, ffn_gain_full = gains[0:1], gains[1:2]
    gate_share = share_of(gate_weight, 0)
    qkv_full = jnp.concatenate([qkv_own] + cp_fetch(lane, qkv_own), axis=0)
    up_share = share_of(up_weight, up_direct)
    gate_line = LineGather(line, gate_share) if shared else None
    cot_rows, _ = tp_width(cotangent, input_rows)

    seg, parent, grand = tree_segments(seg_parent, seg_start, seg_len, keys)
    meta = jnp.stack([seg, parent, grand, positions], axis=1)
    first_row = cp_here * rows
    row_meta_t = lax.dynamic_slice_in_dim(meta, first_row, rows, 2)
    key_meta = lax.dynamic_slice_in_dim(
        jnp.concatenate([meta[:, 0::3], meta[:, 0::3]], axis=2), first_row, keys, 2
    )
    row_meta = jnp.swapaxes(row_meta_t, 1, 2)
    key_meta_t = jnp.swapaxes(key_meta, 1, 2)
    own_pos = row_meta_t[:, 3].reshape(tokens)
    cos_qk, sin_qk = rope_tables(own_pos, (q_width + kv_width) // HD)

    input_wide = input_rows.astype(wide)
    scale_attn = lax.rsqrt(jnp.mean(input_wide * input_wide, axis=-1, keepdims=True) + norm_eps)
    unit_attn = input_wide * scale_attn
    normed_attn = (unit_attn * attn_gain_full).astype(low)
    qkv_raw = matmul(normed_attn, qkv_full)
    qk_raw = qkv_raw[:, : q_width + kv_width]
    qk_rot = qk_raw * cos_qk + turn(qk_raw) * sin_qk
    query_low = qk_rot[:, :q_width].astype(low) * low(att_scale)
    key_low = qk_rot[:, q_width:].astype(low)
    kv_own = jnp.concatenate([key_low, qkv_raw[:, q_width + kv_width :].astype(low)], axis=1)
    kv_sets = [
        jnp.concatenate([own] + cp_fetch(lane, own), axis=0)
        for own in (kv_own[t * rows : (t + 1) * rows] for t in range(trees))
    ]
    out_full = jnp.concatenate([out_weight] + cp_fetch(lane, out_weight), axis=1)
    up_straight = direct_of(up_weight, up_direct)
    down_share = share_of(down_weight, down_direct)
    down_straight = direct_of(down_weight, down_direct)
    gate_straight = [] if shared else direct_of(gate_weight, 0)
    clock = Clock()
    up_line = down_line = None
    if shared:
        gate_line.across(query_low)
        up_line = LineGather(line, up_share, query_low)
    mixtures, lses, sums = [], [], []
    for tree in range(trees):
        here = slice(tree * rows, (tree + 1) * rows)
        mixture, lse = clock.run(
            lambda q, kv: attend(
                q, kv[:, :kv_width], kv[:, kv_width:], row_meta[tree], key_meta[tree], per_kv
            ),
            query_low[here],
            kv_sets[tree],
        )
        mixtures.append(mixture)
        lses.append(lse)
        sums.append(TpTotal(clock.run(matmul, mixture, out_full)))
    mixture_all = jnp.concatenate(mixtures, axis=0)
    for one in sums:
        one.across()
    if shared:
        gate_line.out(sums[-1].pair)
        up_line.across(sums[-1].pair)
        up_line.out()
        down_line = LineGather(line, down_share, sums[-1].pair)
        down_line.across()
        down_line.out()
    for one in sums:
        one.back()
    gate_full = assemble(gate_weight, gate_straight, gate_line, False)
    up_full = assemble(up_weight, up_straight, up_line, False)
    down_full = assemble(down_weight, down_straight, down_line, True)
    hidden = input_wide + resid_scale * jnp.concatenate([one.value() for one in sums], axis=0).astype(wide)

    scale_ffn = lax.rsqrt(jnp.mean(hidden * hidden, axis=-1, keepdims=True) + norm_eps)
    unit_ffn = hidden * scale_ffn
    normed_ffn = (unit_ffn * ffn_gain_full).astype(low)
    gate_pre = matmul(normed_ffn, gate_full)
    up_proj = matmul(normed_ffn, up_full)
    activation = (gate_pre * jax.nn.sigmoid(gate_pre) * up_proj).astype(low)

    sums_line = LineSum(clock)
    arrivals, keeps = [], []

    def blocks_of(values):
        return [values[:, s * block : (s + 1) * block] for s in range(cp_count)]

    def send(product, model_side, other_side):
        arrivals.append(
            [
                cp_deliver(
                    lane,
                    clock.run(lambda m, o: product(m, o).astype(low), model_side[s], other_side),
                    s,
                )
                for s in range(1, cp_count)
            ]
        )
        keeps.append((product, model_side[0], other_side))

    def arrive():
        index = sum(part is not None for part in sums_line.parts)
        product, model_side, other_side = keeps[index]

        def total(m, o, *got):
            whole = product(m, o)
            for piece in got:
                whole = whole + piece.astype(wide)
            return whole.astype(low)

        sums_line.load(clock.run(total, model_side, other_side, *arrivals[index]))

    model_last = lambda m, o: matmul_tn(o, m)
    model_first = matmul_tn
    upstream = cot_rows.astype(wide)
    down_in = (resid_scale * upstream).astype(low)
    down_in_blocks = blocks_of(down_in)
    hidden_units = activation.shape[1]
    quarter, half = hidden_units // 4, hidden_units // 2
    send(model_last, down_in_blocks, activation[:, : quarter // 2])
    send(model_last, down_in_blocks, activation[:, quarter // 2 : quarter])
    send(model_last, down_in_blocks, activation[:, quarter:half])

    def unit_grads(down_in, down_full, gate_pre, up_proj):
        hidden_grad = matmul_nt(down_in, down_full)
        gate_sig = jax.nn.sigmoid(gate_pre)
        gate_in = hidden_grad * up_proj * gate_sig * (1.0 + gate_pre * (1.0 - gate_sig))
        return gate_in.astype(low), (hidden_grad * gate_pre * gate_sig).astype(low)

    send(model_last, down_in_blocks, activation[:, half:])
    step = sums_line.step
    arrive()
    step()
    arrive()
    step()
    gate_in, upper_in = clock.run(unit_grads, down_in, down_full, gate_pre, up_proj)
    arrive()
    step()
    normed_ffn_blocks = blocks_of(normed_ffn)
    send(model_first, normed_ffn_blocks, gate_in[:, :half])
    arrive()
    step()
    ffn_sum = TpTotal(
        clock.run(
            lambda a, b, c, d: matmul_nt(a, b) + matmul_nt(c, d), gate_in, gate_full, upper_in, up_full
        )
    )
    send(model_first, normed_ffn_blocks, gate_in[:, half:])
    ffn_sum.across(*clock.last)
    arrive()
    step()
    send(model_first, normed_ffn_blocks, upper_in[:, :half])
    ffn_sum.back(*clock.last)

    def hidden_grads(ffn_norm_grad, hidden, scale_ffn, upstream, ffn_gain_full):
        ffn_norm_grad = ffn_norm_grad.astype(wide)
        unit_ffn = hidden * scale_ffn
        hidden_back = upstream + norm_back(ffn_norm_grad, unit_ffn, scale_ffn, ffn_gain_full)
        return (
            (resid_scale * hidden_back).astype(low),
            hidden_back,
            jnp.sum(ffn_norm_grad * unit_ffn, axis=0),
        )

    attn_in, hidden_back, ffn_gain_part = clock.run(
        hidden_grads, ffn_sum.value(), hidden, scale_ffn, upstream, ffn_gain_full
    )
    attn_in_blocks = blocks_of(attn_in)
    mix_grad = clock.run(lambda a, b: matmul_nt(a, b).astype(low), attn_in, out_full)

    def attention_grads(tree):
        here = slice(tree * rows, (tree + 1) * rows)
        lse = lses[tree][:, ::HD].T.reshape(-1, 2, rows)
        dq, dk, dv = clock.run(
            lambda grad, q, kv, lse: attend_back(
                q,
                kv[:, :kv_width],
                kv[:, kv_width:],
                grad,
                lse,
                row_meta_t[tree],
                key_meta_t[tree],
                per_kv,
            ),
            mix_grad[here],
            query_low[here],
            kv_sets[tree],
            lse,
        )
        dkv = jnp.concatenate([dk, dv], axis=1)
        got = [
            cp_deliver(lane, dkv[s * rows : (s + 1) * rows].astype(low), s)
            for s in range(1, cp_count)
        ]
        return dq, dkv[:rows], got

    tree_grads = [attention_grads(0)]
    arrive()
    step()
    tree_grads += [attention_grads(tree) for tree in range(1, trees)]
    send(model_first, normed_ffn_blocks, upper_in[:, half:])
    arrive()
    step()
    send(model_last, attn_in_blocks, mixture_all)

    def qkv_grads(cos_qk, sin_qk, *parts):
        queries, own, got = parts[:trees], parts[trees : 2 * trees], parts[2 * trees :]
        each = len(got) // trees
        sums = []
        for tree in range(trees):
            total = own[tree]
            for piece in got[tree * each : (tree + 1) * each]:
                total = total + piece.astype(wide)
            sums.append(total)
        kv_turned = jnp.concatenate(sums, axis=0)
        qk_turned = jnp.concatenate(
            [jnp.concatenate(queries, axis=0), kv_turned[:, :kv_width]], axis=1
        )
        qk_in = qk_turned * cos_qk - turn(qk_turned) * sin_qk
        return jnp.concatenate([qk_in, kv_turned[:, kv_width:]], axis=1).astype(low)

    qkv_in = clock.run(
        qkv_grads,
        cos_qk,
        sin_qk,
        *[g[0] for g in tree_grads],
        *[g[1] for g in tree_grads],
        *[piece for g in tree_grads for piece in g[2]],
    )
    normed_attn_blocks = blocks_of(normed_attn)
    send(model_last, normed_attn_blocks, qkv_in[:, :q_width])
    arrive()
    step()
    attn_sum = TpTotal(clock.run(matmul_nt, qkv_in, qkv_full))
    send(model_last, normed_attn_blocks, qkv_in[:, q_width:])
    attn_sum.across(*clock.last)
    arrive()
    step()
    attn_sum.back(*clock.last)

    def input_grads(attn_norm_grad, input_wide, scale_attn, hidden_back, attn_gain_full):
        attn_norm_grad = attn_norm_grad.astype(wide)
        unit_attn = input_wide * scale_attn
        input_back = hidden_back + norm_back(attn_norm_grad, unit_attn, scale_attn, attn_gain_full)
        return width_part(input_back, tp_here), jnp.sum(attn_norm_grad * unit_attn, axis=0)

    arrive()
    step()
    input_mine, attn_gain_part = clock.run(
        input_grads, attn_sum.value(), input_wide, scale_attn, hidden_back, attn_gain_full
    )
    gain_rows = 16
    gain_part = jnp.concatenate(
        [attn_gain_part[None], ffn_gain_part[None], jnp.zeros((gain_rows - 2, model_width), wide)]
    )
    send(lambda m, o: m, blocks_of(gain_part), gain_part)
    arrive()
    step()
    down_mine = tp_scatter(clock.run(matmul, activation, down_full))
    result = (width_part(hidden, tp_here) + resid_scale * down_mine).astype(low)
    arrive()
    step()
    for _ in range(LineSum.lag):
        sums_line.load(None)
        step()
    finals = [sums_line.final(index) for index in range(len(keeps))]
    down_grad = jnp.concatenate(finals[0:4], axis=0)
    gate_grad = jnp.concatenate(finals[4:6], axis=1)
    up_grad = jnp.concatenate(finals[6:8], axis=1)
    out_grad, query_grad, kv_grad, gain_grads = finals[8], finals[9].T, finals[10].T, finals[11]
    return (
        result.reshape(inputs.shape),
        input_mine.reshape(inputs.shape),
        gain_grads[0],
        query_grad,
        kv_grad[:, :kv_width],
        kv_grad[:, kv_width:],
        out_grad,
        gain_grads[1],
        gate_grad,
        up_grad,
        down_grad,
    )


def solution(mesh):
    in_specs = (
        P("grp", "cp", "tp"),
        P("grp", "cp", "tp"),
        P("cp"),
        P("cp", "tp"),
        P("cp", "tp"),
        P("cp", "tp"),
        P("tp", "cp"),
        P("cp"),
        P("cp", "tp"),
        P("cp", "tp"),
        P("tp", "cp"),
        P("grp", None),
        P("grp", None),
        P("grp", None),
        P("grp", None),
    )
    out_specs = (
        P("grp", "cp", "tp"),
        P("grp", "cp", "tp"),
        P("cp"),
        P("cp", "tp"),
        P("cp", "tp"),
        P("cp", "tp"),
        P("tp", "cp"),
        P("cp"),
        P("cp", "tp"),
        P("cp", "tp"),
        P("tp", "cp"),
    )
    return jax.shard_map(
        per_device, mesh=mesh, in_specs=in_specs, out_specs=out_specs, check_vma=False
    )
```

time: 2080 us -> 967 us (0.46)
  waiting for transfers between devices: 1340 us -> 323 us
  matrix products: 280 us -> 154 us
  blocking collectives: 124 us -> 0 us
  starting transfers between devices: 2.49 us -> 109 us
  Pallas kernels: 0 us -> 89.2 us
  local copies, waits for them, and re-layouts: 170 us -> 105 us
  other arithmetic: 133 us -> 176 us
    reduce_scatter x13 -> x0, waiting for transfers between devices: 589 us -> none  [the longest x1 151 us: per_device(): lax.psum_scatter(totals[8].astype(jnp.bfloat16), ('grp', 'cp'), scatter_d...]
    all_gather x12 -> x0, waiting for transfers between devices: 564 us -> none  [the longest x1 106 us: per_device(): lax.all_gather(down_weight, 'cp', axis=1, tiled=True)]
    ppermute x0 -> x78, waiting for transfers between devices: none -> 323 us  [the longest x33 193 us: move(): self.done.append(lax.ppermute(tie(block, *earlier), axis, pairs))]
    psum x3 -> x0, waiting for transfers between devices: 182 us -> none  [the longest x1 77 us: per_device(): lax.psum(attn_norm_part.astype(jnp.bfloat16), 'tp').astype(jnp.float32)]
    dot_general x94 -> x33, matrix products: 280 us -> 154 us  [the longest x22 62.1 us: matmul_tn(): lax.dot_general(a, b, (((0,), (0,)), ((), ())), preferred_element_type=wide)]
    ppermute x0 -> x78, starting transfers between devices: none -> 109 us  [the longest x9 34.3 us: step(): lax.ppermute(tie(load, *before), 'grp', [(0, 1), (1, 0), (2, 3), (3, 2)])]
    all_gather x12 -> x0, blocking collectives: 101 us -> none  [the longest x2 15 us: per_device(): lax.all_gather(value_low, 'cp', axis=1, tiled=True)]
    pallas_call x0 -> x7, Pallas kernels: none -> 89.2 us  [the longest x3 35 us: assemble_shared(): pl.pallas_call(functools.partial(assemble_kernel, own_blocks=own_blocks,...]
  transfers between devices with their start and end apart: 28 -> 78, of which waited for: 20 -> 32; matrix products, arithmetic and copies ran while one was open for 22% -> 39% of each run, Pallas kernels for 0% -> 9%
where the time goes in v1:
time: 967 us; the launch traced here: 961 us
  waiting for transfers between devices  323 us (33%)
  other arithmetic  176 us (18%)
  matrix products  154 us (16%)
  starting transfers between devices  109 us (11%)
  local copies, waits for them, and re-layouts  105 us (11%)
  Pallas kernels  89.2 us (9%)
    ppermute x33, waiting for transfers between devices, move(): self.done.append(lax.ppermute(tie(block, *earlier), axis, pairs))  193 us
    ppermute x9, waiting for transfers between devices, step(): lax.ppermute(tie(load, *before), 'grp', [(0, 1), (1, 0), (2, 3), (3, 2)])  98.8 us
    dot_general x22, matrix products, matmul_tn(): lax.dot_general(a, b, (((0,), (0,)), ((), ())), preferred_element_type=wide)  62.1 us
    dot_general x5, matrix products, matmul_nt(): lax.dot_general(a, b, (((1,), (1,)), ((), ())), preferred_element_type=wide)  46.9 us
    dot_general x6, matrix products, matmul(): return jnp.dot(a, b, preferred_element_type=wide)  45.1 us
    unnamed x319, local copies, waits for them, and re-layouts  35.6 us
    pallas_call x3, Pallas kernels, assemble_shared(): pl.pallas_call(functools.partial(assemble_kernel, own_blocks=own_blocks,...  35 us
    ppermute x9, starting transfers between devices, step(): lax.ppermute(tie(load, *before), 'grp', [(0, 1), (1, 0), (2, 3), (3, 2)])  34.3 us
  transfers between devices with their start and end apart: 78, of which 32 were waited for; matrix products, arithmetic and copies ran while one was open for 39% of the time, Pallas kernels for 9%

profile of v1, /device:TPU:0, one launch (start us, length us, event | category | flops | bytes accessed | tf_op | source)
XLA Modules:
  0.0 960.8 jit_solution(9624340563327827735)
XLA Ops:
  21.9 11.7 %collective-permute-done.9.refs_0_ = bf16[256,2048]{1,0:T(8,128)(2,1)S(1)} collective-permute-done((bf16[256,2048]{1,0:T(8,128)(2,1)}, bf16[256,2048]{1,0:T(8,128)(2,1)S(1)}, u32[]{:S(2)}, u32[]{:S(2)}) %collective-permute-start.9) | collective-permute-done | bytes 1048608 | tf_op jit(solution)/shard_map/ppermute | solution.py:35
  69.8 22.2 %collective-permute-done.3 = bf16[1024,768]{1,0:T(8,128)(2,1)S(1)} collective-permute-done((bf16[1024,768]{1,0:T(8,128)(2,1)}, bf16[1024,768]{1,0:T(8,128)(2,1)S(1)}, u32[]{:S(2)}, u32[]{:S(2)}) %collective-permute-start.3) | collective-permute-done | bytes 1572896 | tf_op jit(solution)/shard_map/ppermute | solution.py:35
  115.1 10.9 %attend.2 = (bf16[448,512]{1,0:T(8,128)(2,1)}, f32[448,512]{1,0:T(8,128)}) custom-call(bf16[448,512]{1,0:T(8,128)(2,1)} %get-tuple-element.357.q_ref, bf16[896,128]{1,0:T(8,128)(2,1)} %get-tuple-element.621.k_ref, bf16[896,128]{1,0:T(8,128)(2,1)} %get-tuple-element.620.v_ref, s32[448,4]{1,0:T(8,128)} %copy.105.row_ref, s32[2,896]{1,0:T(2,128)} %copy.106.col_ref), custom_call_target="tpu_custom_call" | custom-call | flops 3288334336 | bytes 2293760 | tf_op jit(solution)/shard_map/attend/pallas_call | solution.py:305
  141.2 10.4 %attend.3 = (bf16[448,512]{1,0:T(8,128)(2,1)}, f32[448,512]{1,0:T(8,128)}) custom-call(bf16[448,512]{1,0:T(8,128)(2,1)} %get-tuple-element.376.q_ref, bf16[896,128]{1,0:T(8,128)(2,1)} %get-tuple-element.619.k_ref, bf16[896,128]{1,0:T(8,128)(2,1)} %get-tuple-element.618.v_ref, s32[448,4]{1,0:T(8,128)} %copy.107.row_ref, s32[2,896]{1,0:T(2,128)} %copy.108.col_ref), custom_call_target="tpu_custom_call" | custom-call | flops 3288334336 | bytes 2293760 | tf_op jit(solution)/shard_map/attend/pallas_call | solution.py:305
  161.6 19.5 %collective-permute-done.18.refs_0_ = bf16[512,2048]{1,0:T(8,128)(2,1)} collective-permute-done((bf16[512,2048]{1,0:T(8,128)(2,1)}, bf16[512,2048]{1,0:T(8,128)(2,1)}, u32[]{:S(2)}, u32[]{:S(2)}) %collective-permute-start.18) | collective-permute-done | bytes 2097184 | tf_op jit(solution)/shard_map/ppermute | solution.py:35
  204.3 41.4 %collective-permute-done.24.refs_2_ = bf16[384,1024]{1,0:T(8,128)(2,1)S(1)} collective-permute-done((bf16[384,1024]{1,0:T(8,128)(2,1)S(1)}, bf16[384,1024]{1,0:T(8,128)(2,1)S(1)}, u32[]{:S(2)}, u32[]{:S(2)}) %collective-permute-start.24) | collective-permute-done | bytes 786464 | tf_op jit(solution)/shard_map/ppermute | solution.py:35
  257.6 9.7 %assemble.3 = bf16[2048,2048]{1,0:T(8,128)(2,1)} custom-call(s32[1]{0:T(128)} %bitcast.18.here_ref, bf16[1024,2048]{1,0:T(8,128)(2,1)} %own_ref.3, bf16[256,2048]{1,0:T(8,128)(2,1)} %copy-done.62, bf16[256,2048]{1,0:T(8,128)(2,1)} %collective-permute-done.15.refs_1_, bf16[512,2048]{1,0:T(8,128)(2,1)} %collective-permute-done.16.refs_2_, ...), custom_call_target="tpu_custom_call" | custom-call | bytes 17825792 | tf_op jit(solution)/shard_map/assemble/pallas_call | solution.py:145
  267.3 13.2 %fusion.63 = f32[896,2048]{1,0:T(8,128)} fusion(bf16[896,2048]{1,0:T(8,128)(2,1)} %multiply_convert_fusion.5, bf16[2048,2048]{1,0:T(8,128)(2,1)} %assemble.3), kind=kOutput, calls=%fused_computation.277 | convolution fusion | flops 7516192768 | bytes 19398656 | tf_op jit(solution)/shard_map/dot_general | solution.py:441
  282.9 12.9 %assemble.4 = bf16[2048,2048]{1,0:T(8,128)(2,1)} custom-call(s32[1]{0:T(128)} %bitcast.18.here_ref, bf16[1024,2048]{1,0:T(8,128)(2,1)} %own_ref.4, bf16[512,2048]{1,0:T(8,128)(2,1)} %collective-permute-done.18.refs_0_, bf16[128,2048]{1,0:T(8,128)(2,1)} %collective-permute-done.10.refs_1_, bf16[128,2048]{1,0:T(8,128)(2,1)} %collective-permute-done.19.refs_2_, ...), custom_call_target="tpu_custom_call" | custom-call | bytes 17301504 | tf_op jit(solution)/shard_map/assemble/pallas_call | solution.py:145
  295.8 15.1 %multiply_convert_fusion.4 = (bf16[896,2048]{1,0:T(8,128)(2,1)S(1)}, f32[896,2048]{1,0:T(8,128)}) fusion(f32[896,2048]{1,0:T(8,128)} %fusion.63, bf16[896,2048]{1,0:T(8,128)(2,1)} %multiply_convert_fusion.5, bf16[2048,2048]{1,0:T(8,128)(2,1)} %assemble.4), kind=kOutput, calls=%fused_computation.17 | convolution fusion | flops 7527202816 | bytes 30408704 | tf_op jit(solution)/shard_map/dot_general | solution.py:441
  354.6 12.5 %assemble.5 = bf16[2048,2048]{1,0:T(8,128)(2,1)} custom-call(s32[1]{0:T(128)} %bitcast.18.here_ref, bf16[2048,1024]{1,0:T(8,128)(2,1)} %own_ref.5, bf16[512,1024]{1,0:T(8,128)(2,1)} %collective-permute-done.22.refs_0_, bf16[384,1024]{1,0:T(8,128)(2,1)} %copy-done.81, bf16[384,1024]{1,0:T(8,128)(2,1)} %copy-done.82, ...), custom_call_target="tpu_custom_call" | custom-call | bytes 17563648 | tf_op jit(solution)/shard_map/assemble/pallas_call | solution.py:145
  367.0 18.8 %multiply_convert_fusion.1 = (bf16[896,2048]{1,0:T(8,128)(2,1)}, bf16[896,2048]{1,0:T(8,128)(2,1)}) fusion(f32[896,2048]{1,0:T(8,128)} %fusion.63, f32[896,2048]{1,0:T(8,128)} %get-tuple-element.300, bf16[896,2048]{1,0:T(8,128)(2,1)} %copy-done.23, bf16[2048,2048]{1,0:T(8,128)(2,1)} %assemble.5), kind=kOutput, calls=%fused_computation.13 | convolution fusion | flops 7540047872 | bytes 34078720 | tf_op jit(solution)/shard_map/dot_general | solution.py:445
  413.6 10.0 %fusion.64 = f32[896,2048]{1,0:T(8,128)} fusion(bf16[896,2048]{1,0:T(8,128)(2,1)S(1)} %copy-done.74, bf16[2048,2048]{1,0:T(8,128)(2,1)S(1)} %bitcast.179), kind=kOutput, calls=%fused_computation.278 | convolution fusion | flops 7516192768 | bytes 19398656 | tf_op jit(solution)/shard_map/dot_general | solution.py:445
  423.6 13.0 %convolution_add_fusion = f32[896,2048]{1,0:T(8,128)} fusion(f32[896,2048]{1,0:T(8,128)} %fusion.64, bf16[896,2048]{1,0:T(8,128)(2,1)} %get-tuple-element.325, bf16[2048,2048]{1,0:T(8,128)(2,1)S(1)} %bitcast.181), kind=kOutput, calls=%fused_computation.44 | convolution fusion | flops 7518027776 | bytes 26738688 | tf_op jit(solution)/shard_map/dot_general | solution.py:445
  459.1 29.5 %collective-permute-done.42 = bf16[1024,1024]{1,0:T(8,128)(2,1)} collective-permute-done((bf16[1024,1024]{1,0:T(8,128)(2,1)}, bf16[1024,1024]{1,0:T(8,128)(2,1)}, u32[]{:S(2)}, u32[]{:S(2)}) %collective-permute-start.42) | collective-permute-done | bytes 2097184 | tf_op jit(solution)/shard_map/ppermute | solution.py:35
  557.0 16.5 %attend_back.2 = (f32[448,512]{1,0:T(8,128)}, f32[896,128]{1,0:T(8,128)}, f32[896,128]{1,0:T(8,128)}) custom-call(bf16[448,512]{1,0:T(8,128)(2,1)} %get-tuple-element.357.q_ref, bf16[896,128]{1,0:T(8,128)(2,1)} %get-tuple-element.617.k_ref, bf16[896,128]{1,0:T(8,128)(2,1)} %get-tuple-element.616.v_ref, bf16[448,512]{1,0:T(8,128)(2,1)} %get-tuple-element.359.g_ref, ...), custom_call_target="tpu_custom_call" | custom-call | flops 8220835840 | bytes 3211264 | tf_op jit(solution)/shard_map/attend_back/pallas_call | solution.py:384
  596.7 16.4 %attend_back.3 = (f32[448,512]{1,0:T(8,128)}, f32[896,128]{1,0:T(8,128)}, f32[896,128]{1,0:T(8,128)}) custom-call(bf16[448,512]{1,0:T(8,128)(2,1)} %get-tuple-element.376.q_ref, bf16[896,128]{1,0:T(8,128)(2,1)} %get-tuple-element.615.k_ref, bf16[896,128]{1,0:T(8,128)(2,1)} %get-tuple-element.614.v_ref, bf16[448,512]{1,0:T(8,128)(2,1)} %get-tuple-element.378.g_ref, ...), custom_call_target="tpu_custom_call" | custom-call | flops 8220835840 | bytes 3211264 | tf_op jit(solution)/shard_map/attend_back/pallas_call | solution.py:384
  718.1 20.4 %collective-permute-done.51 = bf16[512,1024]{1,0:T(8,128)(2,1)} collective-permute-done((bf16[512,1024]{1,0:T(8,128)(2,1)}, bf16[512,1024]{1,0:T(8,128)(2,1)}, u32[]{:S(2)}, u32[]{:S(2)}) %collective-permute-start.51) | collective-permute-done | bytes 1048608 | tf_op jit(solution)/shard_map/ppermute | solution.py:35
  742.5 10.8 %collective-permute-done.56 = bf16[1024,1024]{1,0:T(8,128)(2,1)} collective-permute-done((bf16[1024,1024]{1,0:T(8,128)(2,1)}, bf16[1024,1024]{1,0:T(8,128)(2,1)}, u32[]{:S(2)}, u32[]{:S(2)}) %collective-permute-start.56) | collective-permute-done | bytes 2097184 | tf_op jit(solution)/shard_map/ppermute | solution.py:211
  774.5 28.8 %collective-permute-done.57 = bf16[1024,1024]{1,0:T(8,128)(2,1)S(1)} collective-permute-done((bf16[1024,1024]{1,0:T(8,128)(2,1)S(1)}, bf16[1024,1024]{1,0:T(8,128)(2,1)S(1)}, u32[]{:S(2)}, u32[]{:S(2)}) %collective-permute-start.57) | collective-permute-done | bytes 2097184 | tf_op jit(solution)/shard_map/ppermute | solution.py:211
  826.1 24.2 %collective-permute-done.62 = bf16[1024,1024]{1,0:T(8,128)(2,1)} collective-permute-done((bf16[1024,1024]{1,0:T(8,128)(2,1)}, bf16[1024,1024]{1,0:T(8,128)(2,1)}, u32[]{:S(2)}, u32[]{:S(2)}) %collective-permute-start.62) | collective-permute-done | bytes 2097184 | tf_op jit(solution)/shard_map/ppermute | solution.py:211
  873.7 22.6 %collective-permute-done.70 = bf16[1024,1024]{1,0:T(8,128)(2,1)} collective-permute-done((bf16[1024,1024]{1,0:T(8,128)(2,1)}, bf16[1024,1024]{1,0:T(8,128)(2,1)}, u32[]{:S(2)}, u32[]{:S(2)}) %collective-permute-start.70) | collective-permute-done | bytes 2097184 | tf_op jit(solution)/shard_map/ppermute | solution.py:211
  906.8 12.1 %collective-permute-done.71 = bf16[512,1024]{1,0:T(8,128)(2,1)S(1)} collective-permute-done((bf16[512,1024]{1,0:T(8,128)(2,1)}, bf16[512,1024]{1,0:T(8,128)(2,1)S(1)}, u32[]{:S(2)}, u32[]{:S(2)}) %collective-permute-start.71) | collective-permute-done | bytes 1048608 | tf_op jit(solution)/shard_map/ppermute | solution.py:211
  931.1 11.3 %collective-permute-done.75 = bf16[512,1024]{1,0:T(8,128)(2,1)S(1)} collective-permute-done((bf16[512,1024]{1,0:T(8,128)(2,1)S(1)}, bf16[512,1024]{1,0:T(8,128)(2,1)S(1)}, u32[]{:S(2)}, u32[]{:S(2)}) %collective-permute-start.75) | collective-permute-done | bytes 1048608 | tf_op jit(solution)/shard_map/ppermute | solution.py:209
  (703 shorter events, 543.4 us)
Async XLA Ops:
  5.1 49.4 %collective-permute-start.2 = (bf16[2,1024]{1,0:T(2,128)(2,1)S(1)}, bf16[2,1024]{1,0:T(2,128)(2,1)S(1)}, u32[]{:S(2)}, u32[]{:S(2)}) collective-permute-start(bf16[2,1024]{1,0:T(2,128)(2,1)S(1)} %pad_maximum_fusion.15), channel_id=1, source_target_pairs={{4,0},{0,4},{5,1},{1,5},{6,2},{2,6},{7,3},{3,7},{12,8},{8,12},{13,... | collective-permute-start | bytes 12296 | tf_op jit(solution)/shard_map/ppermute | solution.py:35
  55.1 48.2 %collective-permute-start.10 = (bf16[128,2048]{1,0:T(8,128)(2,1)}, bf16[128,2048]{1,0:T(8,128)(2,1)}, u32[]{:S(2)}, u32[]{:S(2)}) collective-permute-start(bf16[128,2048]{1,0:T(8,128)(2,1)} %constant_dynamic-slice_fusion.3), channel_id=1, source_target_pairs={{4,0},{0,4},{5,1},{1,5},{6,2},{2,6},{7,3},{3,7},{12,8},{8,12},{13,... | collective-permute-start | bytes 1572872 | tf_op jit(solution)/shard_map/ppermute | solution.py:35
  113.5 67.5 %collective-permute-start.18 = (bf16[512,2048]{1,0:T(8,128)(2,1)}, bf16[512,2048]{1,0:T(8,128)(2,1)}, u32[]{:S(2)}, u32[]{:S(2)}) collective-permute-start(bf16[512,2048]{1,0:T(8,128)(2,1)} %slice.302), channel_id=1, source_target_pairs={{4,0},{0,4},{5,1},{1,5},{6,2},{2,6},{7,3},{3,7},{12,8},{8,12},{13,... | collective-permute-start | bytes 6291464 | tf_op jit(solution)/shard_map/ppermute | solution.py:35
  128.3 54.2 %collective-permute-start.28 = (bf16[2,896,512]{2,1,0:T(8,128)(2,1)}, bf16[2,896,512]{2,1,0:T(8,128)(2,1)S(1)}, u32[]{:S(2)}, u32[]{:S(2)}) collective-permute-start(bf16[2,896,512]{2,1,0:T(8,128)(2,1)} %pad_maximum_fusion.6), channel_id=1, source_target_pairs={{0,1},{1,0},{2,3},{3,2},{4,5},{5,4},{6,7},{7,6},{8,9},{9,8},{10,11... | collective-permute-start | bytes 5505032 | tf_op jit(solution)/shard_map/ppermute | solution.py:233
  181.0 73.9 %collective-permute-start.17 = (bf16[512,2048]{1,0:T(8,128)(2,1)}, bf16[512,2048]{1,0:T(8,128)(2,1)S(1)}, u32[]{:S(2)}, u32[]{:S(2)}) collective-permute-start(bf16[512,2048]{1,0:T(8,128)(2,1)} %collective-permute-done.16.refs_2_), channel_id=1, source_target_pairs={{8,0},{16,24},{9,1},{17,25},{10,2},{18,26},{11,3},{19,27},{12,4},{... | collective-permute-start | bytes 6291464 | tf_op jit(solution)/shard_map/ppermute | solution.py:35
  196.8 119.0 %collective-permute-start.22 = (bf16[512,1024]{1,0:T(8,128)(2,1)}, bf16[512,1024]{1,0:T(8,128)(2,1)}, u32[]{:S(2)}, u32[]{:S(2)}) collective-permute-start(bf16[512,1024]{1,0:T(8,128)(2,1)} %slice.303), channel_id=1, source_target_pairs={{4,0},{0,4},{5,1},{1,5},{6,2},{2,6},{7,3},{3,7},{12,8},{8,12},{13,... | collective-permute-start | bytes 3145736 | tf_op jit(solution)/shard_map/ppermute | solution.py:35
  197.4 48.3 %collective-permute-start.24 = (bf16[384,1024]{1,0:T(8,128)(2,1)S(1)}, bf16[384,1024]{1,0:T(8,128)(2,1)S(1)}, u32[]{:S(2)}, u32[]{:S(2)}) collective-permute-start(bf16[384,1024]{1,0:T(8,128)(2,1)S(1)} %collective-permute-done.23.refs_1_), channel_id=1, source_target_pairs={{0,8},{8,0},{16,24},{24,16},{1,9},{9,1},{17,25},{25,17},{2,10},{10... | collective-permute-start | bytes 2359304 | tf_op jit(solution)/shard_map/ppermute | solution.py:35
  340.5 64.3 %collective-permute-start.37 = (bf16[1024,1024]{1,0:T(8,128)(2,1)}, bf16[1024,1024]{1,0:T(8,128)(2,1)}, u32[]{:S(2)}, u32[]{:S(2)}) collective-permute-start(bf16[1024,1024]{1,0:T(8,128)(2,1)} %convolution_convert_fusion.4), channel_id=1, source_target_pairs={{0,4},{4,0},{1,5},{5,1},{2,6},{6,2},{3,7},{7,3},{8,12},{12,8},{9,1... | collective-permute-start | bytes 6291464 | tf_op jit(solution)/shard_map/ppermute | solution.py:35
  440.2 48.4 %collective-permute-start.42 = (bf16[1024,1024]{1,0:T(8,128)(2,1)}, bf16[1024,1024]{1,0:T(8,128)(2,1)}, u32[]{:S(2)}, u32[]{:S(2)}) collective-permute-start(bf16[1024,1024]{1,0:T(8,128)(2,1)} %convolution_convert_fusion.3), channel_id=1, source_target_pairs={{0,4},{4,0},{1,5},{5,1},{2,6},{6,2},{3,7},{7,3},{8,12},{12,8},{9,1... | collective-permute-start | bytes 6291464 | tf_op jit(solution)/shard_map/ppermute | solution.py:35
  440.8 54.0 %collective-permute-start.41 = (bf16[1024,1024]{1,0:T(8,128)(2,1)}, bf16[1024,1024]{1,0:T(8,128)(2,1)S(1)}, u32[]{:S(2)}, u32[]{:S(2)}) collective-permute-start(bf16[1024,1024]{1,0:T(8,128)(2,1)} %pad_select_fusion.5), channel_id=1, source_target_pairs={{0,8},{8,0},{16,24},{24,16},{1,9},{9,1},{17,25},{25,17},{2,10},{10... | collective-permute-start | bytes 6291464 | tf_op jit(solution)/shard_map/ppermute | solution.py:211
  523.7 53.6 %collective-permute-start.45 = (bf16[1024,1024]{1,0:T(8,128)(2,1)}, bf16[1024,1024]{1,0:T(8,128)(2,1)}, u32[]{:S(2)}, u32[]{:S(2)}) collective-permute-start(bf16[1024,1024]{1,0:T(8,128)(2,1)} %convolution_convert_fusion.2), channel_id=1, source_target_pairs={{0,4},{4,0},{1,5},{5,1},{2,6},{6,2},{3,7},{7,3},{8,12},{12,8},{9,1... | collective-permute-start | bytes 6291464 | tf_op jit(solution)/shard_map/ppermute | solution.py:35
  524.4 59.2 %collective-permute-start.44 = (bf16[1024,1024]{1,0:T(8,128)(2,1)}, bf16[1024,1024]{1,0:T(8,128)(2,1)}, u32[]{:S(2)}, u32[]{:S(2)}) collective-permute-start(bf16[1024,1024]{1,0:T(8,128)(2,1)} %pad_select_fusion.4), channel_id=1, source_target_pairs={{0,8},{8,0},{16,24},{24,16},{1,9},{9,1},{17,25},{25,17},{2,10},{10... | collective-permute-start | bytes 6291464 | tf_op jit(solution)/shard_map/ppermute | solution.py:211
  532.1 58.5 %collective-permute-start.46 = (bf16[1024,1024]{1,0:T(8,128)(2,1)}, bf16[1024,1024]{1,0:T(8,128)(2,1)}, u32[]{:S(2)}, u32[]{:S(2)}) collective-permute-start(bf16[1024,1024]{1,0:T(8,128)(2,1)} %add.355), channel_id=1, source_target_pairs={{8,16},{16,8},{9,17},{17,9},{10,18},{18,10},{11,19},{19,11},{12,20... | collective-permute-start | bytes 6291464 | tf_op jit(solution)/shard_map/ppermute | solution.py:219
  534.5 86.3 %collective-permute-start.49 = (bf16[1024,1024]{1,0:T(8,128)(2,1)}, bf16[1024,1024]{1,0:T(8,128)(2,1)}, u32[]{:S(2)}, u32[]{:S(2)}) collective-permute-start(bf16[1024,1024]{1,0:T(8,128)(2,1)} %convolution_convert_fusion.1), channel_id=1, source_target_pairs={{0,4},{4,0},{1,5},{5,1},{2,6},{6,2},{3,7},{7,3},{8,12},{12,8},{9,1... | collective-permute-start | bytes 6291464 | tf_op jit(solution)/shard_map/ppermute | solution.py:35
  583.6 50.4 %collective-permute-start.48 = (bf16[1024,1024]{1,0:T(8,128)(2,1)}, bf16[1024,1024]{1,0:T(8,128)(2,1)}, u32[]{:S(2)}, u32[]{:S(2)}) collective-permute-start(bf16[1024,1024]{1,0:T(8,128)(2,1)} %pad_select_fusion.3), channel_id=1, source_target_pairs={{0,8},{8,0},{16,24},{24,16},{1,9},{9,1},{17,25},{25,17},{2,10},{10... | collective-permute-start | bytes 6291464 | tf_op jit(solution)/shard_map/ppermute | solution.py:211
  593.9 48.0 %collective-permute-start.47 = (bf16[1024,1024]{1,0:T(8,128)(2,1)}, bf16[1024,1024]{1,0:T(8,128)(2,1)}, u32[]{:S(2)}, u32[]{:S(2)}) collective-permute-start(bf16[1024,1024]{1,0:T(8,128)(2,1)} %add.359), channel_id=1, source_target_pairs={{8,16},{16,8},{9,17},{17,9},{10,18},{18,10},{11,19},{19,11},{12,20... | collective-permute-start | bytes 6291464 | tf_op jit(solution)/shard_map/ppermute | solution.py:219
  633.5 47.8 %collective-permute-start.55 = (bf16[1024,1024]{1,0:T(8,128)(2,1)}, bf16[1024,1024]{1,0:T(8,128)(2,1)}, u32[]{:S(2)}, u32[]{:S(2)}) collective-permute-start(bf16[1024,1024]{1,0:T(8,128)(2,1)} %convolution_convert_fusion), channel_id=1, source_target_pairs={{0,4},{4,0},{1,5},{5,1},{2,6},{6,2},{3,7},{7,3},{8,12},{12,8},{9,1... | collective-permute-start | bytes 6291464 | tf_op jit(solution)/shard_map/ppermute | solution.py:35
  634.0 53.5 %collective-permute-start.54 = (bf16[1024,1024]{1,0:T(8,128)(2,1)}, bf16[1024,1024]{1,0:T(8,128)(2,1)}, u32[]{:S(2)}, u32[]{:S(2)}) collective-permute-start(bf16[1024,1024]{1,0:T(8,128)(2,1)} %broadcast_select_fusion.6), channel_id=1, source_target_pairs={{0,8},{8,0},{16,24},{24,16},{1,9},{9,1},{17,25},{25,17},{2,10},{10... | collective-permute-start | bytes 6291464 | tf_op jit(solution)/shard_map/ppermute | solution.py:211
  700.5 52.8 %collective-permute-start.56 = (bf16[1024,1024]{1,0:T(8,128)(2,1)}, bf16[1024,1024]{1,0:T(8,128)(2,1)}, u32[]{:S(2)}, u32[]{:S(2)}) collective-permute-start(bf16[1024,1024]{1,0:T(8,128)(2,1)} %broadcast_select_fusion.5), channel_id=1, source_target_pairs={{0,8},{8,0},{16,24},{24,16},{1,9},{9,1},{17,25},{25,17},{2,10},{10... | collective-permute-start | bytes 6291464 | tf_op jit(solution)/shard_map/ppermute | solution.py:211
  706.7 49.2 %collective-permute-start.59 = (bf16[1024,1024]{1,0:T(8,128)(2,1)}, bf16[1024,1024]{1,0:T(8,128)(2,1)}, u32[]{:S(2)}, u32[]{:S(2)}) collective-permute-start(bf16[1024,1024]{1,0:T(8,128)(2,1)} %add.367), channel_id=1, source_target_pairs={{8,16},{16,8},{9,17},{17,9},{10,18},{18,10},{11,19},{19,11},{12,20... | collective-permute-start | bytes 6291464 | tf_op jit(solution)/shard_map/ppermute | solution.py:219
  712.2 49.5 %collective-permute-start.65 = (bf16[448,2048]{1,0:T(8,128)(2,1)}, bf16[448,2048]{1,0:T(8,128)(2,1)}, u32[]{:S(2)}, u32[]{:S(2)}) collective-permute-start(bf16[448,2048]{1,0:T(8,128)(2,1)} %add_convert_fusion.6), channel_id=1, source_target_pairs={{0,2},{1,3},{2,0},{3,1},{4,6},{5,7},{6,4},{7,5},{8,10},{9,11},{10,... | collective-permute-start | bytes 5505032 | tf_op jit(solution)/shard_map/ppermute | solution.py:233
  716.5 54.6 %collective-permute-start.58 = (bf16[512,1024]{1,0:T(8,128)(2,1)S(1)}, bf16[512,1024]{1,0:T(8,128)(2,1)S(1)}, u32[]{:S(2)}, u32[]{:S(2)}) collective-permute-start(bf16[512,1024]{1,0:T(8,128)(2,1)S(1)} %copy-done.137), channel_id=1, source_target_pairs={{0,4},{4,0},{1,5},{5,1},{2,6},{6,2},{3,7},{7,3},{8,12},{12,8},{9,1... | collective-permute-start | bytes 3145736 | tf_op jit(solution)/shard_map/ppermute | solution.py:35
  741.2 81.0 %collective-permute-start.63 = (bf16[256,1024]{1,0:T(8,128)(2,1)}, bf16[256,1024]{1,0:T(8,128)(2,1)}, u32[]{:S(2)}, u32[]{:S(2)}) collective-permute-start(bf16[256,1024]{1,0:T(8,128)(2,1)} %convolution_convert_fusion.9), channel_id=1, source_target_pairs={{0,4},{4,0},{1,5},{5,1},{2,6},{6,2},{3,7},{7,3},{8,12},{12,8},{9,1... | collective-permute-start | bytes 1572872 | tf_op jit(solution)/shard_map/ppermute | solution.py:35
  804.9 48.0 %collective-permute-start.61 = (bf16[512,1024]{1,0:T(8,128)(2,1)S(1)}, bf16[512,1024]{1,0:T(8,128)(2,1)}, u32[]{:S(2)}, u32[]{:S(2)}) collective-permute-start(bf16[512,1024]{1,0:T(8,128)(2,1)S(1)} %slice_add_fusion.3), channel_id=1, source_target_pairs={{8,16},{16,8},{9,17},{17,9},{10,18},{18,10},{11,19},{19,11},{12,20... | collective-permute-start | bytes 3145736 | tf_op jit(solution)/shard_map/ppermute | solution.py:219
  (202 other events, 3285.9 us)

commit v2 on v1

--- a/solution.py
+++ b/solution.py
@@ -65,90 +65,62 @@
 
 
 class LineGather:
-    def __init__(self, lane, block, *earlier):
-        self.lane, self.block = lane, block
-        self.near = lane.move(block, "grp", [(0, 1), (1, 0), (2, 3), (3, 2)], *earlier)
-        self.pair = jnp.concatenate(in_order(lax.axis_index("grp") % 2 == 0, block, self.near), axis=0)
-
-    def across(self, *earlier):
-        self.far = self.lane.move(self.pair, "grp", [(1, 2), (2, 1)], *earlier)
-
-    def out(self, *earlier):
-        self.passed = self.lane.move(self.far, "grp", [(1, 0), (2, 3)], *earlier)
-
-
-def assemble_kernel(here_ref, own_ref, *refs, own_blocks, straight_blocks, share_blocks, beside):
+    def __init__(self, block):
+        self.right, self.left = [block], [block]
+
+    def step(self, *earlier):
+        last = lax.axis_size("grp") - 1
+        self.right.append(
+            lax.ppermute(tie(self.right[-1], *earlier), "grp", [(i, i + 1) for i in range(last)])
+        )
+        self.left.append(
+            lax.ppermute(tie(self.left[-1], *earlier), "grp", [(i + 1, i) for i in range(last)])
+        )
+
+    def got(self):
+        return self.right[-1], self.left[-1]
+
+
+def assemble_kernel(here_ref, own_ref, *refs, own_blocks, share_blocks, beside):
     step, here = pl.program_id(0), here_ref[0]
-    straight = refs[:1] if straight_blocks else ()
-    share_ref, near_ref, far_ref, passed_ref, out_ref = refs[len(straight) :]
+    share_ref, *moved_refs, out_ref = refs
     width = own_ref.shape[1]
-    at = step if beside else step - own_blocks
+    place = step if beside else step - own_blocks
     target = out_ref.at[:, width:] if beside else out_ref
     if beside:
         out_ref[:, :width] = own_ref[...]
     else:
 
-        @pl.when(at < 0)
+        @pl.when(place < 0)
         def _():
             target[...] = own_ref[...]
 
-    if straight:
-
-        @pl.when((at >= 0) & (at < straight_blocks))
+    owner = lax.div(jnp.maximum(place, 0), share_blocks)
+    away = len(moved_refs) // 2
+    for shift, ref in zip([0, *range(1, away + 1), *range(-1, -away - 1, -1)], [share_ref, *moved_refs]):
+
+        @pl.when((place >= 0) & (owner == here - shift))
         def _():
-            target[...] = straight[0][...]
-
-    place = at - straight_blocks
-    owner = lax.div(jnp.maximum(place, 0), share_blocks)
-    there = place >= 0
-    near = owner == here + 1 - 2 * lax.rem(here, 2)
-    apart = lax.div(owner, 2) != lax.div(here, 2)
-    inner = (here == 1) | (here == 2)
-
-    @pl.when(there & (owner == here))
-    def _():
-        target[...] = share_ref[...]
-
-    @pl.when(there & near)
-    def _():
-        target[...] = near_ref[...]
-
-    @pl.when(there & apart & inner)
-    def _():
-        target[...] = far_ref[...]
-
-    @pl.when(there & apart & jnp.logical_not(inner))
-    def _():
-        target[...] = passed_ref[...]
-
-
-def assemble_shared(weight, straight, line, beside):
-    share = line.block.shape[0]
+            target[...] = ref[...]
+
+
+def assemble_shared(weight, line, beside):
+    share = line.right[0].shape[0]
     rows, width = weight.shape
-    direct = straight[0].shape[0] if straight else 0
-    unit = math.gcd(math.gcd(rows, direct), share)
-    own_blocks, straight_blocks, share_blocks = rows // unit, direct // unit, share // unit
-    offset = straight_blocks + (0 if beside else own_blocks)
+    unit = math.gcd(rows, share)
+    own_blocks, share_blocks = rows // unit, share // unit
+    offset = 0 if beside else own_blocks
     spec = lambda first, count: pl.BlockSpec(
         (unit, width), lambda i, here: (jnp.clip(i - first(here[0]), 0, count - 1), 0)
     )
-    own_spec = spec(lambda z: 0, own_blocks)
-    straight_spec = [spec(lambda z: offset - straight_blocks, straight_blocks)] if direct else []
-    pair_first = lambda z: offset + (2 - 2 * lax.div(z, 2)) * share_blocks
-    specs = [own_spec] + straight_spec + [
-        spec(lambda z: offset + z * share_blocks, share_blocks),
-        spec(lambda z: offset + (z + 1 - 2 * lax.rem(z, 2)) * share_blocks, share_blocks),
-        spec(pair_first, 2 * share_blocks),
-        spec(pair_first, 2 * share_blocks),
-    ]
+    moved = lambda shift: spec(lambda z: offset + (z - shift) * share_blocks, share_blocks)
+    away = len(line.right) - 1
+    specs = [spec(lambda z: 0, own_blocks)]
+    specs += [moved(shift) for shift in [*range(away + 1), *range(-1, -away - 1, -1)]]
     out_shape = (rows, 2 * width) if beside else (2 * rows, width)
     return pl.pallas_call(
         functools.partial(
-            assemble_kernel,
-            own_blocks=own_blocks,
-            straight_blocks=straight_blocks,
-            share_blocks=share_blocks,
-            beside=beside,
+            assemble_kernel, own_blocks=own_blocks, share_blocks=share_blocks, beside=beside
         ),
         grid_spec=pltpu.PrefetchScalarGridSpec(
             num_scalar_prefetch=1,
@@ -164,11 +136,8 @@
     )(
         lax.axis_index("grp").astype(jnp.int32).reshape(1),
         weight,
-        *straight,
-        line.block,
-        line.near,
-        line.far,
-        line.passed,
+        *line.right,
+        *line.left[1:],
     )
 
 
@@ -532,37 +501,31 @@
         passed = width_part(part, tp_here ^ 2) + got[:, part_width:]
         return kept + tp_swap(passed.astype(low), 2).astype(wide)
 
-    lane, line = Lane(2), Lane(2)
+    free, lane = Lane(64), Lane(2)
     shared = cp_count == 2 and grp_count == 4
 
-    def share_of(weight, direct):
+    def share_of(weight, *earlier):
         if not shared:
             return None
-        share = (weight.shape[0] - direct) // grp_count
-        start = direct + lax.axis_index("grp") * share
-        return cp_fetch(lane, lax.dynamic_slice_in_dim(weight, start, share, 0))[0]
-
-    def direct_of(weight, direct):
-        if not shared:
-            return cp_fetch(lane, weight)
-        return cp_fetch(lane, weight[:direct]) if direct else []
-
-    def assemble(weight, straight, gathered, beside):
+        share = weight.shape[0] // grp_count
+        part = lax.dynamic_slice_in_dim(weight, lax.axis_index("grp") * share, share, 0)
+        return LineGather(cp_fetch(free, tie(part, *earlier))[0])
+
+    def assemble(weight, others, gathered, beside):
         if shared:
-            return assemble_shared(weight, straight, gathered, beside)
-        return jnp.concatenate([weight] + straight, axis=1 if beside else 0)
+            return assemble_shared(weight, gathered, beside)
+        return jnp.concatenate([weight] + others, axis=1 if beside else 0)
 
     qkv_own = jnp.concatenate([query_weight, key_weight, value_weight], axis=1)
     gains_own = jnp.stack([attn_gain, ffn_gain])
-    up_direct, down_direct = up_weight.shape[0] // 2, down_weight.shape[0] // 4
+    qkv_others = cp_fetch(free, qkv_own)
+    gains = jnp.concatenate([gains_own] + cp_fetch(free, gains_own), axis=1).astype(wide)
+    attn_gain_full, ffn_gain_full = gains[0:1], gains[1:2]
+    qkv_full = jnp.concatenate([qkv_own] + qkv_others, axis=0)
     input_rows, input_far = tp_width(inputs)
-    gains = jnp.concatenate([gains_own] + cp_fetch(lane, gains_own), axis=1).astype(wide)
-    attn_gain_full, ffn_gain_full = gains[0:1], gains[1:2]
-    gate_share = share_of(gate_weight, 0)
-    qkv_full = jnp.concatenate([qkv_own] + cp_fetch(lane, qkv_own), axis=0)
-    up_share = share_of(up_weight, up_direct)
-    gate_line = LineGather(line, gate_share) if shared else None
-    cot_rows, _ = tp_width(cotangent, input_rows)
+    input_rows = tie(input_rows, *qkv_others)
+    gate_line = share_of(gate_weight)
+    cot_rows, _ = tp_width(cotangent, input_far)
 
     seg, parent, grand = tree_segments(seg_parent, seg_start, seg_len, keys)
     meta = jnp.stack([seg, parent, grand, positions], axis=1)
@@ -587,55 +550,65 @@
     key_low = qk_rot[:, q_width:].astype(low)
     kv_own = jnp.concatenate([key_low, qkv_raw[:, q_width + kv_width :].astype(low)], axis=1)
     kv_sets = [
-        jnp.concatenate([own] + cp_fetch(lane, own), axis=0)
+        jnp.concatenate([own] + cp_fetch(free, own), axis=0)
         for own in (kv_own[t * rows : (t + 1) * rows] for t in range(trees))
     ]
-    out_full = jnp.concatenate([out_weight] + cp_fetch(lane, out_weight), axis=1)
-    up_straight = direct_of(up_weight, up_direct)
-    down_share = share_of(down_weight, down_direct)
-    down_straight = direct_of(down_weight, down_direct)
-    gate_straight = [] if shared else direct_of(gate_weight, 0)
+    out_others = cp_fetch(free, tie(out_weight, query_low))
+    out_full = jnp.concatenate([out_weight] + out_others, axis=1)
     clock = Clock()
-    up_line = down_line = None
+    mixtures, lses, sums = [], [], []
     if shared:
-        gate_line.across(query_low)
-        up_line = LineGather(line, up_share, query_low)
-    mixtures, lses, sums = [], [], []
+        gate_line.step(query_low)
     for tree in range(trees):
         here = slice(tree * rows, (tree + 1) * rows)
         mixture, lse = clock.run(
-            lambda q, kv: attend(
+            lambda q, kv, *_: attend(
                 q, kv[:, :kv_width], kv[:, kv_width:], row_meta[tree], key_meta[tree], per_kv
             ),
             query_low[here],
             kv_sets[tree],
+            cot_rows,
         )
         mixtures.append(mixture)
         lses.append(lse)
-        sums.append(TpTotal(clock.run(matmul, mixture, out_full)))
+    gate_first = gate_line.got() if shared else ()
+    for mixture in mixtures:
+        sums.append(TpTotal(clock.run(lambda a, b, *_: matmul(a, b), mixture, out_full, *gate_first)))
     mixture_all = jnp.concatenate(mixtures, axis=0)
+    if shared:
+        gate_line.step()
+    half_rows = up_weight.shape[0] // 2
+    up_top = cp_fetch(free, tie(up_weight[:half_rows], *kv_sets, *out_others))
     for one in sums:
         one.across()
+    gate_second = gate_line.got() if shared else ()
+    sums[0].back(*gate_second)
+    for one in sums[1:]:
+        one.back(*gate_second, *up_top)
+    up_bottom = cp_fetch(free, tie(up_weight[half_rows:], *up_top))
+    up_others = [piece for pair in zip(up_top, up_bottom) for piece in pair]
     if shared:
-        gate_line.out(sums[-1].pair)
-        up_line.across(sums[-1].pair)
-        up_line.out()
-        down_line = LineGather(line, down_share, sums[-1].pair)
-        down_line.across()
-        down_line.out()
-    for one in sums:
-        one.back()
-    gate_full = assemble(gate_weight, gate_straight, gate_line, False)
-    up_full = assemble(up_weight, up_straight, up_line, False)
-    down_full = assemble(down_weight, down_straight, down_line, True)
+        gate_line.step()
+    down_line = share_of(down_weight, *up_top)
+    gate_others = [] if shared else cp_fetch(free, gate_weight)
+    down_others = [] if shared else cp_fetch(free, down_weight)
+    gate_full = clock.run(lambda w: assemble(w, gate_others, gate_line, False), gate_weight)
     hidden = input_wide + resid_scale * jnp.concatenate([one.value() for one in sums], axis=0).astype(wide)
 
     scale_ffn = lax.rsqrt(jnp.mean(hidden * hidden, axis=-1, keepdims=True) + norm_eps)
     unit_ffn = hidden * scale_ffn
     normed_ffn = (unit_ffn * ffn_gain_full).astype(low)
-    gate_pre = matmul(normed_ffn, gate_full)
-    up_proj = matmul(normed_ffn, up_full)
+    gate_pre = clock.run(matmul, normed_ffn, gate_full)
+    up_proj = clock.run(matmul, normed_ffn[:, :block], up_weight)
+    for index, piece in enumerate(up_others):
+        first = block + index * half_rows
+        up_proj = up_proj + matmul(normed_ffn[:, first : first + half_rows], piece)
+    up_full = jnp.concatenate([up_weight] + up_others, axis=0)
     activation = (gate_pre * jax.nn.sigmoid(gate_pre) * up_proj).astype(low)
+    if shared:
+        for _ in range(grp_count - 1):
+            down_line.step()
+    down_full = assemble(down_weight, down_others, down_line, True)
 
     sums_line = LineSum(clock)
     arrivals, keeps = [], []

time: 967 us -> 951 us (0.983)
  waiting for transfers between devices: 323 us -> 291 us
  starting transfers between devices: 109 us -> 128 us
  Pallas kernels: 89.2 us -> 71.2 us
  other arithmetic: 176 us -> 188 us
    ppermute x33 -> x23, waiting for transfers between devices: 193 us -> 110 us  [move(): self.done.append(lax.ppermute(tie(block, *earlier), axis, pairs))]
    ppermute x0 -> x12, starting transfers between devices: none -> 39.3 us  [the longest x6 30.8 us: step(): lax.ppermute(tie(self.right[-1], *earlier), 'grp', [(i, i + 1) for i in r...]
    ppermute x0 -> x12, waiting for transfers between devices: none -> 31.1 us  [the longest x6 29.1 us: step(): lax.ppermute(tie(self.right[-1], *earlier), 'grp', [(i, i + 1) for i in r...]
    ppermute x18, waiting for transfers between devices: 5.6 us -> 25.5 us  [tp_swap(): lax.ppermute(tie(block, *earlier), 'tp', [(i, i ^ bit) for i in range(cou...]
    ppermute x9, starting transfers between devices: 34.3 us -> 15.2 us  [step(): lax.ppermute(tie(load, *before), 'grp', [(0, 1), (1, 0), (2, 3), (3, 2)])]
    pallas_call x3 -> x2, Pallas kernels: 35 us -> 17.3 us  [assemble_shared(): pl.pallas_call(functools.partial(assemble_kernel, own_blocks=own_blocks,...]
    ppermute x33 -> x23, starting transfers between devices: 32.5 us -> 23.4 us  [move(): self.done.append(lax.ppermute(tie(block, *earlier), axis, pairs))]
    dot_general x6 -> x8, matrix products: 45.1 us -> 51.9 us  [matmul(): return jnp.dot(a, b, preferred_element_type=wide)]
  transfers between devices with their start and end apart: 78 -> 80, of which waited for: 32 -> 27; matrix products, arithmetic and copies ran while one was open for 39% -> 42% of each run, Pallas kernels for 9% -> 8%
where the time goes in v2:
time: 951 us; the launch traced here: 940 us
  waiting for transfers between devices  291 us (31%)
  other arithmetic  188 us (20%)
  matrix products  161 us (17%)
  starting transfers between devices  128 us (13%)
  local copies, waits for them, and re-layouts  97.7 us (10%)
  Pallas kernels  71.2 us (7%)
    ppermute x23, waiting for transfers between devices, move(): self.done.append(lax.ppermute(tie(block, *earlier), axis, pairs))  110 us
    ppermute x9, waiting for transfers between devices, step(): lax.ppermute(tie(load, *before), 'grp', [(0, 1), (1, 0), (2, 3), (3, 2)])  95.9 us
    dot_general x22, matrix products, matmul_tn(): lax.dot_general(a, b, (((0,), (0,)), ((), ())), preferred_element_type=wide)  62.1 us
    dot_general x8, matrix products, matmul(): return jnp.dot(a, b, preferred_element_type=wide)  51.9 us
    dot_general x5, matrix products, matmul_nt(): lax.dot_general(a, b, (((1,), (1,)), ((), ())), preferred_element_type=wide)  46.7 us
    pallas_call x2, Pallas kernels, attend_back(): pl.pallas_call(functools.partial(attend_back_kernel, per_kv=per_kv), grid...  33 us
    unnamed x317, local copies, waits for them, and re-layouts  31 us
    ppermute x6, starting transfers between devices, step(): lax.ppermute(tie(self.right[-1], *earlier), 'grp', [(i, i + 1) for i in r...  30.8 us
  transfers between devices with their start and end apart: 80, of which 27 were waited for; matrix products, arithmetic and copies ran while one was open for 42% of the time, Pallas kernels for 8%

profile of v2, /device:TPU:0, one launch (start us, length us, event | category | flops | bytes accessed | tf_op | source)
XLA Modules:
  0.0 939.9 jit_solution(9914891099417648595)
XLA Ops:
  13.9 10.4 %collective-permute-done = bf16[896,512]{1,0:T(8,128)(2,1)S(1)} collective-permute-done((bf16[896,512]{1,0:T(8,128)(2,1)}, bf16[896,512]{1,0:T(8,128)(2,1)S(1)}, u32[]{:S(2)}, u32[]{:S(2)}) %collective-permute-start) | collective-permute-done | bytes 917536 | tf_op jit(solution)/shard_map/ppermute | solution.py:202
  89.8 10.4 %attend.2 = (bf16[448,512]{1,0:T(8,128)(2,1)}, f32[448,512]{1,0:T(8,128)}) custom-call(bf16[448,512]{1,0:T(8,128)(2,1)} %get-tuple-element.347.q_ref, bf16[896,128]{1,0:T(8,128)(2,1)} %get-tuple-element.607.k_ref, bf16[896,128]{1,0:T(8,128)(2,1)} %get-tuple-element.606.v_ref, s32[448,4]{1,0:T(8,128)} %copy.105.row_ref, s32[2,896]{1,0:T(2,128)} %copy.106.col_ref), custom_call_target="tpu_custom_call" | custom-call | flops 3288334336 | bytes 2293760 | tf_op jit(solution)/shard_map/attend/pallas_call | solution.py:274
  101.0 10.5 %attend.3 = (bf16[448,512]{1,0:T(8,128)(2,1)}, f32[448,512]{1,0:T(8,128)}) custom-call(bf16[448,512]{1,0:T(8,128)(2,1)} %get-tuple-element.366.q_ref, bf16[896,128]{1,0:T(8,128)(2,1)} %get-tuple-element.605.k_ref, bf16[896,128]{1,0:T(8,128)(2,1)} %get-tuple-element.604.v_ref, s32[448,4]{1,0:T(8,128)} %copy.107.row_ref, s32[2,896]{1,0:T(2,128)} %copy.108.col_ref), custom_call_target="tpu_custom_call" | custom-call | flops 3288334336 | bytes 2293760 | tf_op jit(solution)/shard_map/attend/pallas_call | solution.py:274
  132.3 15.7 %collective-permute-done.14.refs_2_ = bf16[256,2048]{1,0:T(8,128)(2,1)} collective-permute-done((bf16[256,2048]{1,0:T(8,128)(2,1)}, bf16[256,2048]{1,0:T(8,128)(2,1)}, u32[]{:S(2)}, u32[]{:S(2)}) %collective-permute-start.14) | collective-permute-done | bytes 1048608 | tf_op jit(solution)/shard_map/ppermute | solution.py:74
  156.3 13.4 %collective-permute-done.18 = bf16[224,2048]{1,0:T(8,128)(2,1)} collective-permute-done((bf16[224,2048]{1,0:T(8,128)(2,1)S(1)}, bf16[224,2048]{1,0:T(8,128)(2,1)}, u32[]{:S(2)}, u32[]{:S(2)}) %collective-permute-start.18) | collective-permute-done | bytes 917536 | tf_op jit(solution)/shard_map/ppermute | solution.py:202
  197.3 12.1 %fusion.67 = f32[896,2048]{1,0:T(8,128)} fusion(bf16[896,2048]{1,0:T(8,128)(2,1)S(1)} %multiply_convert_fusion.5, bf16[2048,2048]{1,0:T(8,128)(2,1)} %assemble.2), kind=kOutput, calls=%fused_computation.273 | convolution fusion | flops 7516192768 | bytes 19398656 | tf_op jit(solution)/shard_map/dot_general | solution.py:410
  216.1 30.4 %collective-permute-done.24.refs_0_ = bf16[512,1024]{1,0:T(8,128)(2,1)} collective-permute-done((bf16[512,1024]{1,0:T(8,128)(2,1)}, bf16[512,1024]{1,0:T(8,128)(2,1)}, u32[]{:S(2)}, u32[]{:S(2)}) %collective-permute-start.24) | collective-permute-done | bytes 1048608 | tf_op jit(solution)/shard_map/ppermute | solution.py:35
  259.9 13.4 %collective-permute-done.25.refs_1_ = bf16[512,1024]{1,0:T(8,128)(2,1)S(1)} collective-permute-done((bf16[512,1024]{1,0:T(8,128)(2,1)}, bf16[512,1024]{1,0:T(8,128)(2,1)S(1)}, u32[]{:S(2)}, u32[]{:S(2)}) %collective-permute-start.25) | collective-permute-done | bytes 1048608 | tf_op jit(solution)/shard_map/ppermute | solution.py:74
  279.8 11.5 %multiply_convert_fusion.4 = (bf16[896,2048]{1,0:T(8,128)(2,1)S(1)}, f32[896,2048]{1,0:T(8,128)}) fusion(f32[896,2048]{1,0:T(8,128)} %fusion.67, bf16[512,2048]{1,0:T(8,128)(2,1)} %collective-permute-done.23, bf16[896,2048]{1,0:T(8,128)(2,1)S(1)} %multiply_convert_fusion.5, f32[896,2048]{1,0:T(8,128)} %fusion.68, f32[896,2048]{1,0:T(8,128)} %fusion.28), kind=kOutput, calls=%fused_computation.18 | convolution fusion | flops 1893728256 | bytes 36044800 | tf_op jit(solution)/shard_map/dot_general | solution.py:410
  322.3 11.9 %pad_maximum_fusion = bf16[2048,2048]{1,0:T(8,128)(2,1)} fusion(bf16[512,2048]{1,0:T(8,128)(2,1)} %collective-permute-done.23, bf16[512,2048]{1,0:T(8,128)(2,1)} %collective-permute-done.19, bf16[1024,2048]{1,0:T(8,128)(2,1)S(1)} %copy-done.15), kind=kLoop, calls=%fused_computation.6 | loop fusion | flops 25165824 | bytes 16777216 | tf_op jit(solution)/shard_map/concatenate | solution.py:606
  358.9 18.8 %multiply_convert_fusion.1 = (bf16[896,2048]{1,0:T(8,128)(2,1)}, bf16[896,2048]{1,0:T(8,128)(2,1)}) fusion(f32[896,2048]{1,0:T(8,128)} %fusion.67, f32[896,2048]{1,0:T(8,128)} %get-tuple-element.290, bf16[896,2048]{1,0:T(8,128)(2,1)} %copy-done.19, bf16[2048,2048]{1,0:T(8,128)(2,1)} %assemble.3), kind=kOutput, calls=%fused_computation.14 | convolution fusion | flops 7540047872 | bytes 34078720 | tf_op jit(solution)/shard_map/dot_general | solution.py:414
  406.4 9.8 %fusion.69 = f32[896,2048]{1,0:T(8,128)} fusion(bf16[896,2048]{1,0:T(8,128)(2,1)S(1)} %copy-done.70, bf16[2048,2048]{1,0:T(8,128)(2,1)S(1)} %bitcast.185), kind=kOutput, calls=%fused_computation.275 | convolution fusion | flops 7516192768 | bytes 19398656 | tf_op jit(solution)/shard_map/dot_general | solution.py:414
  416.2 13.0 %convolution_add_fusion = f32[896,2048]{1,0:T(8,128)} fusion(f32[896,2048]{1,0:T(8,128)} %fusion.69, bf16[896,2048]{1,0:T(8,128)(2,1)} %get-tuple-element.315, bf16[2048,2048]{1,0:T(8,128)(2,1)S(1)} %bitcast.183), kind=kOutput, calls=%fused_computation.45 | convolution fusion | flops 7518027776 | bytes 26738688 | tf_op jit(solution)/shard_map/dot_general | solution.py:414
  446.7 34.6 %collective-permute-done.44 = bf16[1024,1024]{1,0:T(8,128)(2,1)} collective-permute-done((bf16[1024,1024]{1,0:T(8,128)(2,1)}, bf16[1024,1024]{1,0:T(8,128)(2,1)}, u32[]{:S(2)}, u32[]{:S(2)}) %collective-permute-start.44) | collective-permute-done | bytes 2097184 | tf_op jit(solution)/shard_map/ppermute | solution.py:35
  536.1 16.5 %attend_back.2 = (f32[448,512]{1,0:T(8,128)}, f32[896,128]{1,0:T(8,128)}, f32[896,128]{1,0:T(8,128)}) custom-call(bf16[448,512]{1,0:T(8,128)(2,1)} %get-tuple-element.347.q_ref, bf16[896,128]{1,0:T(8,128)(2,1)} %get-tuple-element.603.k_ref, bf16[896,128]{1,0:T(8,128)(2,1)} %get-tuple-element.602.v_ref, bf16[448,512]{1,0:T(8,128)(2,1)} %get-tuple-element.349.g_ref, ...), custom_call_target="tpu_custom_call" | custom-call | flops 8220835840 | bytes 3211264 | tf_op jit(solution)/shard_map/attend_back/pallas_call | solution.py:353
  575.7 16.5 %attend_back.3 = (f32[448,512]{1,0:T(8,128)}, f32[896,128]{1,0:T(8,128)}, f32[896,128]{1,0:T(8,128)}) custom-call(bf16[448,512]{1,0:T(8,128)(2,1)} %get-tuple-element.366.q_ref, bf16[896,128]{1,0:T(8,128)(2,1)} %get-tuple-element.601.k_ref, bf16[896,128]{1,0:T(8,128)(2,1)} %get-tuple-element.600.v_ref, bf16[448,512]{1,0:T(8,128)(2,1)} %get-tuple-element.368.g_ref, ...), custom_call_target="tpu_custom_call" | custom-call | flops 8220835840 | bytes 3211264 | tf_op jit(solution)/shard_map/attend_back/pallas_call | solution.py:353
  652.2 11.3 %collective-permute-done.57 = bf16[1024,1024]{1,0:T(8,128)(2,1)} collective-permute-done((bf16[1024,1024]{1,0:T(8,128)(2,1)}, bf16[1024,1024]{1,0:T(8,128)(2,1)}, u32[]{:S(2)}, u32[]{:S(2)}) %collective-permute-start.57) | collective-permute-done | bytes 2097184 | tf_op jit(solution)/shard_map/ppermute | solution.py:35
  704.7 14.4 %collective-permute-done.53 = bf16[512,1024]{1,0:T(8,128)(2,1)} collective-permute-done((bf16[512,1024]{1,0:T(8,128)(2,1)}, bf16[512,1024]{1,0:T(8,128)(2,1)}, u32[]{:S(2)}, u32[]{:S(2)}) %collective-permute-start.53) | collective-permute-done | bytes 1048608 | tf_op jit(solution)/shard_map/ppermute | solution.py:35
  722.9 9.4 %collective-permute-done.58 = bf16[1024,1024]{1,0:T(8,128)(2,1)} collective-permute-done((bf16[1024,1024]{1,0:T(8,128)(2,1)}, bf16[1024,1024]{1,0:T(8,128)(2,1)}, u32[]{:S(2)}, u32[]{:S(2)}) %collective-permute-start.58) | collective-permute-done | bytes 2097184 | tf_op jit(solution)/shard_map/ppermute | solution.py:180
  753.5 28.8 %collective-permute-done.59 = bf16[1024,1024]{1,0:T(8,128)(2,1)S(1)} collective-permute-done((bf16[1024,1024]{1,0:T(8,128)(2,1)S(1)}, bf16[1024,1024]{1,0:T(8,128)(2,1)S(1)}, u32[]{:S(2)}, u32[]{:S(2)}) %collective-permute-start.59) | collective-permute-done | bytes 2097184 | tf_op jit(solution)/shard_map/ppermute | solution.py:180
  804.9 24.3 %collective-permute-done.64 = bf16[1024,1024]{1,0:T(8,128)(2,1)} collective-permute-done((bf16[1024,1024]{1,0:T(8,128)(2,1)}, bf16[1024,1024]{1,0:T(8,128)(2,1)}, u32[]{:S(2)}, u32[]{:S(2)}) %collective-permute-start.64) | collective-permute-done | bytes 2097184 | tf_op jit(solution)/shard_map/ppermute | solution.py:180
  852.7 22.6 %collective-permute-done.72 = bf16[1024,1024]{1,0:T(8,128)(2,1)} collective-permute-done((bf16[1024,1024]{1,0:T(8,128)(2,1)}, bf16[1024,1024]{1,0:T(8,128)(2,1)}, u32[]{:S(2)}, u32[]{:S(2)}) %collective-permute-start.72) | collective-permute-done | bytes 2097184 | tf_op jit(solution)/shard_map/ppermute | solution.py:180
  887.3 10.6 %collective-permute-done.73 = bf16[512,1024]{1,0:T(8,128)(2,1)S(1)} collective-permute-done((bf16[512,1024]{1,0:T(8,128)(2,1)}, bf16[512,1024]{1,0:T(8,128)(2,1)S(1)}, u32[]{:S(2)}, u32[]{:S(2)}) %collective-permute-start.73) | collective-permute-done | bytes 1048608 | tf_op jit(solution)/shard_map/ppermute | solution.py:180
  910.1 11.3 %collective-permute-done.77 = bf16[512,1024]{1,0:T(8,128)(2,1)S(1)} collective-permute-done((bf16[512,1024]{1,0:T(8,128)(2,1)S(1)}, bf16[512,1024]{1,0:T(8,128)(2,1)S(1)}, u32[]{:S(2)}, u32[]{:S(2)}) %collective-permute-start.77) | collective-permute-done | bytes 1048608 | tf_op jit(solution)/shard_map/ppermute | solution.py:178
  (700 shorter events, 554.6 us)
Async XLA Ops:
  6.2 50.6 %collective-permute-start.2 = (bf16[1024,768]{1,0:T(8,128)(2,1)S(1)}, bf16[1024,768]{1,0:T(8,128)(2,1)}, u32[]{:S(2)}, u32[]{:S(2)}) collective-permute-start(bf16[1024,768]{1,0:T(8,128)(2,1)S(1)} %constant_dynamic-update-slice_fusion.8), channel_id=1, source_target_pairs={{4,0},{0,4},{5,1},{1,5},{6,2},{2,6},{7,3},{3,7},{12,8},{8,12},{13,... | collective-permute-start | bytes 4718600 | tf_op jit(solution)/shard_map/ppermute | solution.py:35
  11.2 59.8 %collective-permute-start.8 = (bf16[256,2048]{1,0:T(8,128)(2,1)}, bf16[256,2048]{1,0:T(8,128)(2,1)}, u32[]{:S(2)}, u32[]{:S(2)}) collective-permute-start(bf16[256,2048]{1,0:T(8,128)(2,1)} %constant_dynamic-slice_fusion.2), channel_id=1, source_target_pairs={{4,0},{0,4},{5,1},{1,5},{6,2},{2,6},{7,3},{3,7},{12,8},{8,12},{13,... | collective-permute-start | bytes 3145736 | tf_op jit(solution)/shard_map/ppermute | solution.py:35
  119.1 53.0 %collective-permute-start.19 = (bf16[512,2048]{1,0:T(8,128)(2,1)}, bf16[512,2048]{1,0:T(8,128)(2,1)}, u32[]{:S(2)}, u32[]{:S(2)}) collective-permute-start(bf16[512,2048]{1,0:T(8,128)(2,1)} %get-tuple-element.263), channel_id=1, source_target_pairs={{4,0},{0,4},{5,1},{1,5},{6,2},{2,6},{7,3},{3,7},{12,8},{8,12},{13,... | collective-permute-start | bytes 6291464 | tf_op jit(solution)/shard_map/ppermute | solution.py:35
  175.6 104.2 %collective-permute-start.23 = (bf16[512,2048]{1,0:T(8,128)(2,1)}, bf16[512,2048]{1,0:T(8,128)(2,1)}, u32[]{:S(2)}, u32[]{:S(2)}) collective-permute-start(bf16[512,2048]{1,0:T(8,128)(2,1)} %get-tuple-element.270), channel_id=1, source_target_pairs={{4,0},{0,4},{5,1},{1,5},{6,2},{2,6},{7,3},{3,7},{12,8},{8,12},{13,... | collective-permute-start | bytes 6291464 | tf_op jit(solution)/shard_map/ppermute | solution.py:35
  175.9 70.5 %collective-permute-start.24 = (bf16[512,1024]{1,0:T(8,128)(2,1)}, bf16[512,1024]{1,0:T(8,128)(2,1)}, u32[]{:S(2)}, u32[]{:S(2)}) collective-permute-start(bf16[512,1024]{1,0:T(8,128)(2,1)} %constant_dynamic-slice_fusion.1), channel_id=1, source_target_pairs={{4,0},{0,4},{5,1},{1,5},{6,2},{2,6},{7,3},{3,7},{12,8},{8,12},{13,... | collective-permute-start | bytes 3145736 | tf_op jit(solution)/shard_map/ppermute | solution.py:35
  334.5 63.8 %collective-permute-start.39 = (bf16[1024,1024]{1,0:T(8,128)(2,1)}, bf16[1024,1024]{1,0:T(8,128)(2,1)}, u32[]{:S(2)}, u32[]{:S(2)}) collective-permute-start(bf16[1024,1024]{1,0:T(8,128)(2,1)} %convolution_convert_fusion.4), channel_id=1, source_target_pairs={{0,4},{4,0},{1,5},{5,1},{2,6},{6,2},{3,7},{7,3},{8,12},{12,8},{9,1... | collective-permute-start | bytes 6291464 | tf_op jit(solution)/shard_map/ppermute | solution.py:35
  432.9 48.4 %collective-permute-start.44 = (bf16[1024,1024]{1,0:T(8,128)(2,1)}, bf16[1024,1024]{1,0:T(8,128)(2,1)}, u32[]{:S(2)}, u32[]{:S(2)}) collective-permute-start(bf16[1024,1024]{1,0:T(8,128)(2,1)} %convolution_convert_fusion.3), channel_id=1, source_target_pairs={{0,4},{4,0},{1,5},{5,1},{2,6},{6,2},{3,7},{7,3},{8,12},{12,8},{9,1... | collective-permute-start | bytes 6291464 | tf_op jit(solution)/shard_map/ppermute | solution.py:35
  433.2 54.2 %collective-permute-start.43 = (bf16[1024,1024]{1,0:T(8,128)(2,1)}, bf16[1024,1024]{1,0:T(8,128)(2,1)S(1)}, u32[]{:S(2)}, u32[]{:S(2)}) collective-permute-start(bf16[1024,1024]{1,0:T(8,128)(2,1)} %pad_select_fusion.5), channel_id=1, source_target_pairs={{0,8},{8,0},{16,24},{24,16},{1,9},{9,1},{17,25},{25,17},{2,10},{10... | collective-permute-start | bytes 6291464 | tf_op jit(solution)/shard_map/ppermute | solution.py:180
  442.5 53.4 %collective-permute-start.41 = (bf16[448,2048]{1,0:T(8,128)(2,1)S(1)}, bf16[448,2048]{1,0:T(8,128)(2,1)S(1)}, u32[]{:S(2)}, u32[]{:S(2)}) collective-permute-start(bf16[448,2048]{1,0:T(8,128)(2,1)S(1)} %add_convert_fusion.8), channel_id=1, source_target_pairs={{0,2},{1,3},{2,0},{3,1},{4,6},{5,7},{6,4},{7,5},{8,10},{9,11},{10,... | collective-permute-start | bytes 5505032 | tf_op jit(solution)/shard_map/ppermute | solution.py:202
  508.9 48.9 %collective-permute-start.47 = (bf16[1024,1024]{1,0:T(8,128)(2,1)}, bf16[1024,1024]{1,0:T(8,128)(2,1)}, u32[]{:S(2)}, u32[]{:S(2)}) collective-permute-start(bf16[1024,1024]{1,0:T(8,128)(2,1)} %convolution_convert_fusion.2), channel_id=1, source_target_pairs={{0,4},{4,0},{1,5},{5,1},{2,6},{6,2},{3,7},{7,3},{8,12},{12,8},{9,1... | collective-permute-start | bytes 6291464 | tf_op jit(solution)/shard_map/ppermute | solution.py:35
  509.3 54.8 %collective-permute-start.46 = (bf16[1024,1024]{1,0:T(8,128)(2,1)}, bf16[1024,1024]{1,0:T(8,128)(2,1)}, u32[]{:S(2)}, u32[]{:S(2)}) collective-permute-start(bf16[1024,1024]{1,0:T(8,128)(2,1)} %pad_select_fusion.4), channel_id=1, source_target_pairs={{0,8},{8,0},{16,24},{24,16},{1,9},{9,1},{17,25},{25,17},{2,10},{10... | collective-permute-start | bytes 6291464 | tf_op jit(solution)/shard_map/ppermute | solution.py:180
  510.9 58.7 %collective-permute-start.48 = (bf16[1024,1024]{1,0:T(8,128)(2,1)}, bf16[1024,1024]{1,0:T(8,128)(2,1)}, u32[]{:S(2)}, u32[]{:S(2)}) collective-permute-start(bf16[1024,1024]{1,0:T(8,128)(2,1)} %add.341), channel_id=1, source_target_pairs={{8,16},{16,8},{9,17},{17,9},{10,18},{18,10},{11,19},{19,11},{12,20... | collective-permute-start | bytes 6291464 | tf_op jit(solution)/shard_map/ppermute | solution.py:188
  513.3 88.9 %collective-permute-start.51 = (bf16[1024,1024]{1,0:T(8,128)(2,1)}, bf16[1024,1024]{1,0:T(8,128)(2,1)}, u32[]{:S(2)}, u32[]{:S(2)}) collective-permute-start(bf16[1024,1024]{1,0:T(8,128)(2,1)} %convolution_convert_fusion.1), channel_id=1, source_target_pairs={{0,4},{4,0},{1,5},{5,1},{2,6},{6,2},{3,7},{7,3},{8,12},{12,8},{9,1... | collective-permute-start | bytes 6291464 | tf_op jit(solution)/shard_map/ppermute | solution.py:35
  564.1 51.1 %collective-permute-start.50 = (bf16[1024,1024]{1,0:T(8,128)(2,1)}, bf16[1024,1024]{1,0:T(8,128)(2,1)}, u32[]{:S(2)}, u32[]{:S(2)}) collective-permute-start(bf16[1024,1024]{1,0:T(8,128)(2,1)} %pad_select_fusion.3), channel_id=1, source_target_pairs={{0,8},{8,0},{16,24},{24,16},{1,9},{9,1},{17,25},{25,17},{2,10},{10... | collective-permute-start | bytes 6291464 | tf_op jit(solution)/shard_map/ppermute | solution.py:180
  572.9 47.8 %collective-permute-start.49 = (bf16[1024,1024]{1,0:T(8,128)(2,1)}, bf16[1024,1024]{1,0:T(8,128)(2,1)}, u32[]{:S(2)}, u32[]{:S(2)}) collective-permute-start(bf16[1024,1024]{1,0:T(8,128)(2,1)} %add.345), channel_id=1, source_target_pairs={{8,16},{16,8},{9,17},{17,9},{10,18},{18,10},{11,19},{19,11},{12,20... | collective-permute-start | bytes 6291464 | tf_op jit(solution)/shard_map/ppermute | solution.py:188
  614.8 48.6 %collective-permute-start.57 = (bf16[1024,1024]{1,0:T(8,128)(2,1)}, bf16[1024,1024]{1,0:T(8,128)(2,1)}, u32[]{:S(2)}, u32[]{:S(2)}) collective-permute-start(bf16[1024,1024]{1,0:T(8,128)(2,1)} %convolution_convert_fusion), channel_id=1, source_target_pairs={{0,4},{4,0},{1,5},{5,1},{2,6},{6,2},{3,7},{7,3},{8,12},{12,8},{9,1... | collective-permute-start | bytes 6291464 | tf_op jit(solution)/shard_map/ppermute | solution.py:35
  615.1 54.5 %collective-permute-start.56 = (bf16[1024,1024]{1,0:T(8,128)(2,1)}, bf16[1024,1024]{1,0:T(8,128)(2,1)}, u32[]{:S(2)}, u32[]{:S(2)}) collective-permute-start(bf16[1024,1024]{1,0:T(8,128)(2,1)} %broadcast_select_fusion.6), channel_id=1, source_target_pairs={{0,8},{8,0},{16,24},{24,16},{1,9},{9,1},{17,25},{25,17},{2,10},{10... | collective-permute-start | bytes 6291464 | tf_op jit(solution)/shard_map/ppermute | solution.py:180
  682.6 49.7 %collective-permute-start.58 = (bf16[1024,1024]{1,0:T(8,128)(2,1)}, bf16[1024,1024]{1,0:T(8,128)(2,1)}, u32[]{:S(2)}, u32[]{:S(2)}) collective-permute-start(bf16[1024,1024]{1,0:T(8,128)(2,1)} %broadcast_select_fusion.5), channel_id=1, source_target_pairs={{0,8},{8,0},{16,24},{24,16},{1,9},{9,1},{17,25},{25,17},{2,10},{10... | collective-permute-start | bytes 6291464 | tf_op jit(solution)/shard_map/ppermute | solution.py:180
  685.7 49.2 %collective-permute-start.61 = (bf16[1024,1024]{1,0:T(8,128)(2,1)}, bf16[1024,1024]{1,0:T(8,128)(2,1)}, u32[]{:S(2)}, u32[]{:S(2)}) collective-permute-start(bf16[1024,1024]{1,0:T(8,128)(2,1)} %add.353), channel_id=1, source_target_pairs={{8,16},{16,8},{9,17},{17,9},{10,18},{18,10},{11,19},{19,11},{12,20... | collective-permute-start | bytes 6291464 | tf_op jit(solution)/shard_map/ppermute | solution.py:188
  691.2 49.4 %collective-permute-start.67 = (bf16[448,2048]{1,0:T(8,128)(2,1)}, bf16[448,2048]{1,0:T(8,128)(2,1)}, u32[]{:S(2)}, u32[]{:S(2)}) collective-permute-start(bf16[448,2048]{1,0:T(8,128)(2,1)} %add_convert_fusion.6), channel_id=1, source_target_pairs={{0,2},{1,3},{2,0},{3,1},{4,6},{5,7},{6,4},{7,5},{8,10},{9,11},{10,... | collective-permute-start | bytes 5505032 | tf_op jit(solution)/shard_map/ppermute | solution.py:202
  721.8 79.2 %collective-permute-start.65 = (bf16[256,1024]{1,0:T(8,128)(2,1)}, bf16[256,1024]{1,0:T(8,128)(2,1)}, u32[]{:S(2)}, u32[]{:S(2)}) collective-permute-start(bf16[256,1024]{1,0:T(8,128)(2,1)} %convolution_convert_fusion.9), channel_id=1, source_target_pairs={{0,4},{4,0},{1,5},{5,1},{2,6},{6,2},{3,7},{7,3},{8,12},{12,8},{9,1... | collective-permute-start | bytes 1572872 | tf_op jit(solution)/shard_map/ppermute | solution.py:35
  734.9 47.5 %collective-permute-start.59 = (bf16[1024,1024]{1,0:T(8,128)(2,1)S(1)}, bf16[1024,1024]{1,0:T(8,128)(2,1)S(1)}, u32[]{:S(2)}, u32[]{:S(2)}) collective-permute-start(bf16[1024,1024]{1,0:T(8,128)(2,1)S(1)} %pad_select_fusion.2), channel_id=1, source_target_pairs={{0,8},{8,0},{16,24},{24,16},{1,9},{9,1},{17,25},{25,17},{2,10},{10... | collective-permute-start | bytes 6291464 | tf_op jit(solution)/shard_map/ppermute | solution.py:180
  736.7 47.3 %collective-permute-start.62 = (bf16[1024,1024]{1,0:T(8,128)(2,1)S(1)}, bf16[1024,1024]{1,0:T(8,128)(2,1)S(1)}, u32[]{:S(2)}, u32[]{:S(2)}) collective-permute-start(bf16[1024,1024]{1,0:T(8,128)(2,1)S(1)} %add.356), channel_id=1, source_target_pairs={{8,16},{16,8},{9,17},{17,9},{10,18},{18,10},{11,19},{19,11},{12,20... | collective-permute-start | bytes 6291464 | tf_op jit(solution)/shard_map/ppermute | solution.py:188
  783.9 48.0 %collective-permute-start.63 = (bf16[512,1024]{1,0:T(8,128)(2,1)S(1)}, bf16[512,1024]{1,0:T(8,128)(2,1)}, u32[]{:S(2)}, u32[]{:S(2)}) collective-permute-start(bf16[512,1024]{1,0:T(8,128)(2,1)S(1)} %slice_add_fusion.3), channel_id=1, source_target_pairs={{8,16},{16,8},{9,17},{17,9},{10,18},{18,10},{11,19},{19,11},{12,20... | collective-permute-start | bytes 3145736 | tf_op jit(solution)/shard_map/ppermute | solution.py:188
  (203 other events, 3127.7 us)

commit v3 on v2

--- a/solution.py
+++ b/solution.py
@@ -585,11 +585,12 @@
     sums[0].back(*gate_second)
     for one in sums[1:]:
         one.back(*gate_second, *up_top)
-    up_bottom = cp_fetch(free, tie(up_weight[half_rows:], *up_top))
-    up_others = [piece for pair in zip(up_top, up_bottom) for piece in pair]
     if shared:
         gate_line.step()
     down_line = share_of(down_weight, *up_top)
+    up_after = [down_line.right[0]] if shared else up_top
+    up_bottom = cp_fetch(free, tie(up_weight[half_rows:], *up_after))
+    up_others = [piece for pair in zip(up_top, up_bottom) for piece in pair]
     gate_others = [] if shared else cp_fetch(free, gate_weight)
     down_others = [] if shared else cp_fetch(free, down_weight)
     gate_full = clock.run(lambda w: assemble(w, gate_others, gate_line, False), gate_weight)
@@ -671,17 +672,19 @@
     send(model_first, normed_ffn_blocks, gate_in[:, :half])
     arrive()
     step()
-    ffn_sum = TpTotal(
-        clock.run(
-            lambda a, b, c, d: matmul_nt(a, b) + matmul_nt(c, d), gate_in, gate_full, upper_in, up_full
-        )
+    ffn_part = clock.run(
+        lambda a, b, c, d: matmul_nt(a, b) + matmul_nt(c, d), gate_in, gate_full, upper_in, up_full
     )
     send(model_first, normed_ffn_blocks, gate_in[:, half:])
+    arrive()
+    step()
+    ffn_sum = TpTotal(tie(ffn_part, *clock.last))
+    send(model_first, normed_ffn_blocks, upper_in[:, :half])
     ffn_sum.across(*clock.last)
     arrive()
     step()
-    send(model_first, normed_ffn_blocks, upper_in[:, :half])
     ffn_sum.back(*clock.last)
+    send(model_first, normed_ffn_blocks, upper_in[:, half:])
 
     def hidden_grads(ffn_norm_grad, hidden, scale_ffn, upstream, ffn_gain_full):
         ffn_norm_grad = ffn_norm_grad.astype(wide)
@@ -729,10 +732,9 @@
     arrive()
     step()
     tree_grads += [attention_grads(tree) for tree in range(1, trees)]
-    send(model_first, normed_ffn_blocks, upper_in[:, half:])
-    arrive()
-    step()
     send(model_last, attn_in_blocks, mixture_all)
+    arrive()
+    step()
 
     def qkv_grads(cos_qk, sin_qk, *parts):
         queries, own, got = parts[:trees], parts[trees : 2 * trees], parts[2 * trees :]
@@ -760,9 +762,10 @@
     )
     normed_attn_blocks = blocks_of(normed_attn)
     send(model_last, normed_attn_blocks, qkv_in[:, :q_width])
-    arrive()
-    step()
-    attn_sum = TpTotal(clock.run(matmul_nt, qkv_in, qkv_full))
+    attn_part = clock.run(matmul_nt, qkv_in, qkv_full)
+    arrive()
+    step()
+    attn_sum = TpTotal(tie(attn_part, *clock.last))
     send(model_last, normed_attn_blocks, qkv_in[:, q_width:])
     attn_sum.across(*clock.last)
     arrive()
@@ -789,8 +792,6 @@
     step()
     down_mine = tp_scatter(clock.run(matmul, activation, down_full))
     result = (width_part(hidden, tp_here) + resid_scale * down_mine).astype(low)
-    arrive()
-    step()
     for _ in range(LineSum.lag):
         sums_line.load(None)
         step()

time: 951 us -> 925 us (0.973)
  waiting for transfers between devices: 291 us -> 269 us
    ppermute x23, waiting for transfers between devices: 110 us -> 93.1 us  [move(): self.done.append(lax.ppermute(tie(block, *earlier), axis, pairs))]
    unnamed x317 -> x333, local copies, waits for them, and re-layouts: 31 us -> 31.4 us
  transfers between devices with their start and end apart: 80 -> 80, of which waited for: 27 -> 27; matrix products, arithmetic and copies ran while one was open for 42% -> 45% of each run, Pallas kernels for 8% -> 8%
where the time goes in v3:
time: 925 us; the launch traced here: 914 us
  waiting for transfers between devices  269 us (29%)
  other arithmetic  189 us (20%)
  matrix products  160 us (17%)
  starting transfers between devices  121 us (13%)
  local copies, waits for them, and re-layouts  101 us (11%)
  Pallas kernels  70.9 us (8%)
    ppermute x9, waiting for transfers between devices, step(): lax.ppermute(tie(load, *before), 'grp', [(0, 1), (1, 0), (2, 3), (3, 2)])  97.5 us
    ppermute x23, waiting for transfers between devices, move(): self.done.append(lax.ppermute(tie(block, *earlier), axis, pairs))  93.1 us
    dot_general x22, matrix products, matmul_tn(): lax.dot_general(a, b, (((0,), (0,)), ((), ())), preferred_element_type=wide)  60.2 us
    dot_general x8, matrix products, matmul(): return jnp.dot(a, b, preferred_element_type=wide)  52.3 us
    dot_general x5, matrix products, matmul_nt(): lax.dot_general(a, b, (((1,), (1,)), ((), ())), preferred_element_type=wide)  47.2 us
    pallas_call x2, Pallas kernels, attend_back(): pl.pallas_call(functools.partial(attend_back_kernel, per_kv=per_kv), grid...  32.7 us
    unnamed x333, local copies, waits for them, and re-layouts  31.4 us
    ppermute x6, starting transfers between devices, step(): lax.ppermute(tie(self.right[-1], *earlier), 'grp', [(i, i + 1) for i in r...  30.5 us
  transfers between devices with their start and end apart: 80, of which 27 were waited for; matrix products, arithmetic and copies ran while one was open for 45% of the time, Pallas kernels for 8%

profile of v3, /device:TPU:0, one launch (start us, length us, event | category | flops | bytes accessed | tf_op | source)
XLA Modules:
  0.0 913.9 jit_solution(2555719600370511602)
XLA Ops:
  13.9 10.4 %collective-permute-done = bf16[896,512]{1,0:T(8,128)(2,1)S(1)} collective-permute-done((bf16[896,512]{1,0:T(8,128)(2,1)}, bf16[896,512]{1,0:T(8,128)(2,1)S(1)}, u32[]{:S(2)}, u32[]{:S(2)}) %collective-permute-start) | collective-permute-done | bytes 917536 | tf_op jit(solution)/shard_map/ppermute | solution.py:202
  90.1 10.4 %attend.2 = (bf16[448,512]{1,0:T(8,128)(2,1)}, f32[448,512]{1,0:T(8,128)}) custom-call(bf16[448,512]{1,0:T(8,128)(2,1)} %get-tuple-element.362.q_ref, bf16[896,128]{1,0:T(8,128)(2,1)} %get-tuple-element.611.k_ref, bf16[896,128]{1,0:T(8,128)(2,1)} %get-tuple-element.610.v_ref, s32[448,4]{1,0:T(8,128)} %copy.105.row_ref, s32[2,896]{1,0:T(2,128)} %copy.106.col_ref), custom_call_target="tpu_custom_call" | custom-call | flops 3288334336 | bytes 2293760 | tf_op jit(solution)/shard_map/attend/pallas_call | solution.py:274
  101.2 10.5 %attend.3 = (bf16[448,512]{1,0:T(8,128)(2,1)}, f32[448,512]{1,0:T(8,128)}) custom-call(bf16[448,512]{1,0:T(8,128)(2,1)} %get-tuple-element.380.q_ref, bf16[896,128]{1,0:T(8,128)(2,1)} %get-tuple-element.609.k_ref, bf16[896,128]{1,0:T(8,128)(2,1)} %get-tuple-element.608.v_ref, s32[448,4]{1,0:T(8,128)} %copy.107.row_ref, s32[2,896]{1,0:T(2,128)} %copy.108.col_ref), custom_call_target="tpu_custom_call" | custom-call | flops 3288334336 | bytes 2293760 | tf_op jit(solution)/shard_map/attend/pallas_call | solution.py:274
  132.3 15.7 %collective-permute-done.14.refs_2_ = bf16[256,2048]{1,0:T(8,128)(2,1)} collective-permute-done((bf16[256,2048]{1,0:T(8,128)(2,1)}, bf16[256,2048]{1,0:T(8,128)(2,1)}, u32[]{:S(2)}, u32[]{:S(2)}) %collective-permute-start.14) | collective-permute-done | bytes 1048608 | tf_op jit(solution)/shard_map/ppermute | solution.py:74
  156.2 13.4 %collective-permute-done.18 = bf16[224,2048]{1,0:T(8,128)(2,1)} collective-permute-done((bf16[224,2048]{1,0:T(8,128)(2,1)S(1)}, bf16[224,2048]{1,0:T(8,128)(2,1)}, u32[]{:S(2)}, u32[]{:S(2)}) %collective-permute-start.18) | collective-permute-done | bytes 917536 | tf_op jit(solution)/shard_map/ppermute | solution.py:202
  179.6 9.1 assemble.2
  207.4 12.1 %fusion.67 = f32[896,2048]{1,0:T(8,128)} fusion(bf16[896,2048]{1,0:T(8,128)(2,1)S(1)} %multiply_convert_fusion.5, bf16[2048,2048]{1,0:T(8,128)(2,1)} %assemble.2), kind=kOutput, calls=%fused_computation.273 | convolution fusion | flops 7516192768 | bytes 19398656 | tf_op jit(solution)/shard_map/dot_general | solution.py:410
  242.8 10.8 %collective-permute-done.26.refs_2_ = bf16[512,1024]{1,0:T(8,128)(2,1)} collective-permute-done((bf16[512,1024]{1,0:T(8,128)(2,1)S(1)}, bf16[512,1024]{1,0:T(8,128)(2,1)}, u32[]{:S(2)}, u32[]{:S(2)}) %collective-permute-start.26) | collective-permute-done | bytes 1048608 | tf_op jit(solution)/shard_map/ppermute | solution.py:74
  260.4 11.8 %multiply_convert_fusion.4 = (bf16[896,2048]{1,0:T(8,128)(2,1)S(1)}, f32[896,2048]{1,0:T(8,128)}) fusion(f32[896,2048]{1,0:T(8,128)} %fusion.67, bf16[512,2048]{1,0:T(8,128)(2,1)S(1)} %collective-permute-done.24, bf16[896,2048]{1,0:T(8,128)(2,1)S(1)} %multiply_convert_fusion.5, f32[896,2048]{1,0:T(8,128)} %fusion.68, f32[896,2048]{1,0:T(8,128)} %fusion.28), kind=kOutput, calls=%fused_computation.18 | convolution fusion | flops 1893728256 | bytes 36044800 | tf_op jit(solution)/shard_map/dot_general | solution.py:410
  296.9 14.0 %pad_maximum_fusion = bf16[2048,2048]{1,0:T(8,128)(2,1)} fusion(bf16[512,2048]{1,0:T(8,128)(2,1)S(1)} %collective-permute-done.24, bf16[512,2048]{1,0:T(8,128)(2,1)} %collective-permute-done.19, bf16[1024,2048]{1,0:T(8,128)(2,1)S(1)} %copy-done.15), kind=kLoop, calls=%fused_computation.6 | loop fusion | flops 25165824 | bytes 16777216 | tf_op jit(solution)/shard_map/concatenate | solution.py:607
  326.6 18.9 %multiply_convert_fusion.1 = (bf16[896,2048]{1,0:T(8,128)(2,1)}, bf16[896,2048]{1,0:T(8,128)(2,1)}) fusion(f32[896,2048]{1,0:T(8,128)} %fusion.67, f32[896,2048]{1,0:T(8,128)} %get-tuple-element.292, bf16[896,2048]{1,0:T(8,128)(2,1)} %copy-done.19, bf16[2048,2048]{1,0:T(8,128)(2,1)} %assemble.3), kind=kOutput, calls=%fused_computation.14 | convolution fusion | flops 7540047872 | bytes 34078720 | tf_op jit(solution)/shard_map/dot_general | solution.py:414
  362.0 20.2 %collective-permute-done.39 = bf16[1024,1024]{1,0:T(8,128)(2,1)} collective-permute-done((bf16[1024,1024]{1,0:T(8,128)(2,1)}, bf16[1024,1024]{1,0:T(8,128)(2,1)}, u32[]{:S(2)}, u32[]{:S(2)}) %collective-permute-start.39) | collective-permute-done | bytes 2097184 | tf_op jit(solution)/shard_map/ppermute | solution.py:35
  390.6 10.1 %fusion.69 = f32[896,2048]{1,0:T(8,128)} fusion(bf16[896,2048]{1,0:T(8,128)(2,1)S(1)} %copy-done.77, bf16[2048,2048]{1,0:T(8,128)(2,1)S(1)} %bitcast.185), kind=kOutput, calls=%fused_computation.275 | convolution fusion | flops 7516192768 | bytes 19398656 | tf_op jit(solution)/shard_map/dot_general | solution.py:414
  400.7 13.1 %convolution_add_fusion = f32[896,2048]{1,0:T(8,128)} fusion(f32[896,2048]{1,0:T(8,128)} %fusion.69, bf16[896,2048]{1,0:T(8,128)(2,1)} %get-tuple-element.317, bf16[2048,2048]{1,0:T(8,128)(2,1)S(1)} %bitcast.183), kind=kOutput, calls=%fused_computation.45 | convolution fusion | flops 7518027776 | bytes 26738688 | tf_op jit(solution)/shard_map/dot_general | solution.py:414
  454.1 30.1 %collective-permute-done.47 = bf16[1024,1024]{1,0:T(8,128)(2,1)S(1)} collective-permute-done((bf16[1024,1024]{1,0:T(8,128)(2,1)}, bf16[1024,1024]{1,0:T(8,128)(2,1)S(1)}, u32[]{:S(2)}, u32[]{:S(2)}) %collective-permute-start.47) | collective-permute-done | bytes 2097184 | tf_op jit(solution)/shard_map/ppermute | solution.py:35
  542.8 16.4 %attend_back.2 = (f32[448,512]{1,0:T(8,128)}, f32[896,128]{1,0:T(8,128)}, f32[896,128]{1,0:T(8,128)}) custom-call(bf16[448,512]{1,0:T(8,128)(2,1)} %get-tuple-element.362.q_ref, bf16[896,128]{1,0:T(8,128)(2,1)} %get-tuple-element.607.k_ref, bf16[896,128]{1,0:T(8,128)(2,1)} %get-tuple-element.606.v_ref, bf16[448,512]{1,0:T(8,128)(2,1)} %get-tuple-element.364.g_ref, ...), custom_call_target="tpu_custom_call" | custom-call | flops 8220835840 | bytes 3211264 | tf_op jit(solution)/shard_map/attend_back/pallas_call | solution.py:353
  577.7 16.4 %attend_back.3 = (f32[448,512]{1,0:T(8,128)}, f32[896,128]{1,0:T(8,128)}, f32[896,128]{1,0:T(8,128)}) custom-call(bf16[448,512]{1,0:T(8,128)(2,1)} %get-tuple-element.380.q_ref, bf16[896,128]{1,0:T(8,128)(2,1)} %get-tuple-element.605.k_ref, bf16[896,128]{1,0:T(8,128)(2,1)} %get-tuple-element.604.v_ref, bf16[448,512]{1,0:T(8,128)(2,1)} %get-tuple-element.382.g_ref, ...), custom_call_target="tpu_custom_call" | custom-call | flops 8220835840 | bytes 3211264 | tf_op jit(solution)/shard_map/attend_back/pallas_call | solution.py:353
  611.0 8.4 collective-permute-done.52
  662.7 24.3 %collective-permute-done.59 = bf16[1024,1024]{1,0:T(8,128)(2,1)S(1)} collective-permute-done((bf16[1024,1024]{1,0:T(8,128)(2,1)}, bf16[1024,1024]{1,0:T(8,128)(2,1)S(1)}, u32[]{:S(2)}, u32[]{:S(2)}) %collective-permute-start.59) | collective-permute-done | bytes 2097184 | tf_op jit(solution)/shard_map/ppermute | solution.py:180
  711.4 13.1 %collective-permute-done.57 = bf16[512,1024]{1,0:T(8,128)(2,1)S(1)} collective-permute-done((bf16[512,1024]{1,0:T(8,128)(2,1)S(1)}, bf16[512,1024]{1,0:T(8,128)(2,1)S(1)}, u32[]{:S(2)}, u32[]{:S(2)}) %collective-permute-start.57) | collective-permute-done | bytes 1048608 | tf_op jit(solution)/shard_map/ppermute | solution.py:35
  726.5 21.6 %collective-permute-done.61 = bf16[1024,1024]{1,0:T(8,128)(2,1)S(1)} collective-permute-done((bf16[1024,1024]{1,0:T(8,128)(2,1)}, bf16[1024,1024]{1,0:T(8,128)(2,1)S(1)}, u32[]{:S(2)}, u32[]{:S(2)}) %collective-permute-start.61) | collective-permute-done | bytes 2097184 | tf_op jit(solution)/shard_map/ppermute | solution.py:180
  770.7 24.3 %collective-permute-done.62 = bf16[1024,1024]{1,0:T(8,128)(2,1)S(1)} collective-permute-done((bf16[1024,1024]{1,0:T(8,128)(2,1)S(1)}, bf16[1024,1024]{1,0:T(8,128)(2,1)S(1)}, u32[]{:S(2)}, u32[]{:S(2)}) %collective-permute-start.62) | collective-permute-done | bytes 2097184 | tf_op jit(solution)/shard_map/ppermute | solution.py:180
  818.3 23.1 %collective-permute-done.67 = bf16[1024,1024]{1,0:T(8,128)(2,1)} collective-permute-done((bf16[1024,1024]{1,0:T(8,128)(2,1)}, bf16[1024,1024]{1,0:T(8,128)(2,1)}, u32[]{:S(2)}, u32[]{:S(2)}) %collective-permute-start.67) | collective-permute-done | bytes 2097184 | tf_op jit(solution)/shard_map/ppermute | solution.py:180
  877.6 10.7 %collective-permute-done.77 = bf16[512,1024]{1,0:T(8,128)(2,1)S(1)} collective-permute-done((bf16[512,1024]{1,0:T(8,128)(2,1)S(1)}, bf16[512,1024]{1,0:T(8,128)(2,1)S(1)}, u32[]{:S(2)}, u32[]{:S(2)}) %collective-permute-start.77) | collective-permute-done | bytes 1048608 | tf_op jit(solution)/shard_map/ppermute | solution.py:178
  (716 shorter events, 541.4 us)
Async XLA Ops:
  6.2 50.6 %collective-permute-start.2 = (bf16[1024,768]{1,0:T(8,128)(2,1)S(1)}, bf16[1024,768]{1,0:T(8,128)(2,1)}, u32[]{:S(2)}, u32[]{:S(2)}) collective-permute-start(bf16[1024,768]{1,0:T(8,128)(2,1)S(1)} %constant_dynamic-update-slice_fusion.8), channel_id=1, source_target_pairs={{4,0},{0,4},{5,1},{1,5},{6,2},{2,6},{7,3},{3,7},{12,8},{8,12},{13,... | collective-permute-start | bytes 4718600 | tf_op jit(solution)/shard_map/ppermute | solution.py:35
  11.2 59.7 %collective-permute-start.8 = (bf16[256,2048]{1,0:T(8,128)(2,1)}, bf16[256,2048]{1,0:T(8,128)(2,1)}, u32[]{:S(2)}, u32[]{:S(2)}) collective-permute-start(bf16[256,2048]{1,0:T(8,128)(2,1)} %constant_dynamic-slice_fusion.2), channel_id=1, source_target_pairs={{4,0},{0,4},{5,1},{1,5},{6,2},{2,6},{7,3},{3,7},{12,8},{8,12},{13,... | collective-permute-start | bytes 3145736 | tf_op jit(solution)/shard_map/ppermute | solution.py:35
  119.3 52.7 %collective-permute-start.19 = (bf16[512,2048]{1,0:T(8,128)(2,1)}, bf16[512,2048]{1,0:T(8,128)(2,1)}, u32[]{:S(2)}, u32[]{:S(2)}) collective-permute-start(bf16[512,2048]{1,0:T(8,128)(2,1)} %get-tuple-element.265), channel_id=1, source_target_pairs={{4,0},{0,4},{5,1},{1,5},{6,2},{2,6},{7,3},{3,7},{12,8},{8,12},{13,... | collective-permute-start | bytes 6291464 | tf_op jit(solution)/shard_map/ppermute | solution.py:35
  201.5 58.9 %collective-permute-start.24 = (bf16[512,2048]{1,0:T(8,128)(2,1)S(1)}, bf16[512,2048]{1,0:T(8,128)(2,1)S(1)}, u32[]{:S(2)}, u32[]{:S(2)}) collective-permute-start(bf16[512,2048]{1,0:T(8,128)(2,1)S(1)} %copy-done.89), channel_id=1, source_target_pairs={{4,0},{0,4},{5,1},{1,5},{6,2},{2,6},{7,3},{3,7},{12,8},{8,12},{13,... | collective-permute-start | bytes 6291464 | tf_op jit(solution)/shard_map/ppermute | solution.py:35
  253.6 60.1 %collective-permute-start.27 = (bf16[512,1024]{1,0:T(8,128)(2,1)}, bf16[512,1024]{1,0:T(8,128)(2,1)}, u32[]{:S(2)}, u32[]{:S(2)}) collective-permute-start(bf16[512,1024]{1,0:T(8,128)(2,1)} %collective-permute-done.26.refs_2_), channel_id=1, source_target_pairs={{0,8},{8,16},{16,24},{1,9},{9,17},{17,25},{2,10},{10,18},{18,26},{... | collective-permute-start | bytes 3145736 | tf_op jit(solution)/shard_map/ppermute | solution.py:74
  259.1 54.6 %collective-permute-start.30 = (bf16[512,1024]{1,0:T(8,128)(2,1)}, bf16[512,1024]{1,0:T(8,128)(2,1)}, u32[]{:S(2)}, u32[]{:S(2)}) collective-permute-start(bf16[512,1024]{1,0:T(8,128)(2,1)} %collective-permute-done.29.refs_5_), channel_id=1, source_target_pairs={{8,0},{16,8},{24,16},{9,1},{17,9},{25,17},{10,2},{18,10},{26,18},{... | collective-permute-start | bytes 3145736 | tf_op jit(solution)/shard_map/ppermute | solution.py:77
  312.7 69.5 %collective-permute-start.39 = (bf16[1024,1024]{1,0:T(8,128)(2,1)}, bf16[1024,1024]{1,0:T(8,128)(2,1)}, u32[]{:S(2)}, u32[]{:S(2)}) collective-permute-start(bf16[1024,1024]{1,0:T(8,128)(2,1)} %convolution_convert_fusion.4), channel_id=1, source_target_pairs={{0,4},{4,0},{1,5},{5,1},{2,6},{6,2},{3,7},{7,3},{8,12},{12,8},{9,1... | collective-permute-start | bytes 6291464 | tf_op jit(solution)/shard_map/ppermute | solution.py:35
  360.2 60.1 %collective-permute-start.42 = (bf16[1024,1024]{1,0:T(8,128)(2,1)}, bf16[1024,1024]{1,0:T(8,128)(2,1)}, u32[]{:S(2)}, u32[]{:S(2)}) collective-permute-start(bf16[1024,1024]{1,0:T(8,128)(2,1)} %convolution_convert_fusion.3), channel_id=1, source_target_pairs={{0,4},{4,0},{1,5},{5,1},{2,6},{6,2},{3,7},{7,3},{8,12},{12,8},{9,1... | collective-permute-start | bytes 6291464 | tf_op jit(solution)/shard_map/ppermute | solution.py:35
  435.8 48.3 %collective-permute-start.47 = (bf16[1024,1024]{1,0:T(8,128)(2,1)}, bf16[1024,1024]{1,0:T(8,128)(2,1)S(1)}, u32[]{:S(2)}, u32[]{:S(2)}) collective-permute-start(bf16[1024,1024]{1,0:T(8,128)(2,1)} %convolution_convert_fusion.2), channel_id=1, source_target_pairs={{0,4},{4,0},{1,5},{5,1},{2,6},{6,2},{3,7},{7,3},{8,12},{12,8},{9,1... | collective-permute-start | bytes 6291464 | tf_op jit(solution)/shard_map/ppermute | solution.py:35
  441.5 50.0 %collective-permute-start.46 = (bf16[1024,1024]{1,0:T(8,128)(2,1)S(1)}, bf16[1024,1024]{1,0:T(8,128)(2,1)S(1)}, u32[]{:S(2)}, u32[]{:S(2)}) collective-permute-start(bf16[1024,1024]{1,0:T(8,128)(2,1)S(1)} %copy-done.88), channel_id=1, source_target_pairs={{0,8},{8,0},{16,24},{24,16},{1,9},{9,1},{17,25},{25,17},{2,10},{10... | collective-permute-start | bytes 6291464 | tf_op jit(solution)/shard_map/ppermute | solution.py:180
  445.3 48.4 %collective-permute-start.45 = (bf16[1024,1024]{1,0:T(8,128)(2,1)S(1)}, bf16[1024,1024]{1,0:T(8,128)(2,1)S(1)}, u32[]{:S(2)}, u32[]{:S(2)}) collective-permute-start(bf16[1024,1024]{1,0:T(8,128)(2,1)S(1)} %copy-done.40), channel_id=1, source_target_pairs={{8,16},{16,8},{9,17},{17,9},{10,18},{18,10},{11,19},{19,11},{12,20... | collective-permute-start | bytes 6291464 | tf_op jit(solution)/shard_map/ppermute | solution.py:188
  510.0 49.2 %collective-permute-start.51 = (bf16[1024,1024]{1,0:T(8,128)(2,1)}, bf16[1024,1024]{1,0:T(8,128)(2,1)}, u32[]{:S(2)}, u32[]{:S(2)}) collective-permute-start(bf16[1024,1024]{1,0:T(8,128)(2,1)} %convolution_convert_fusion.1), channel_id=1, source_target_pairs={{0,4},{4,0},{1,5},{5,1},{2,6},{6,2},{3,7},{7,3},{8,12},{12,8},{9,1... | collective-permute-start | bytes 6291464 | tf_op jit(solution)/shard_map/ppermute | solution.py:35
  510.1 56.0 %collective-permute-start.50 = (bf16[1024,1024]{1,0:T(8,128)(2,1)}, bf16[1024,1024]{1,0:T(8,128)(2,1)}, u32[]{:S(2)}, u32[]{:S(2)}) collective-permute-start(bf16[1024,1024]{1,0:T(8,128)(2,1)} %pad_select_fusion.3), channel_id=1, source_target_pairs={{0,8},{8,0},{16,24},{24,16},{1,9},{9,1},{17,25},{25,17},{2,10},{10... | collective-permute-start | bytes 6291464 | tf_op jit(solution)/shard_map/ppermute | solution.py:180
  512.7 58.9 %collective-permute-start.49 = (bf16[1024,1024]{1,0:T(8,128)(2,1)}, bf16[1024,1024]{1,0:T(8,128)(2,1)}, u32[]{:S(2)}, u32[]{:S(2)}) collective-permute-start(bf16[1024,1024]{1,0:T(8,128)(2,1)} %add.344), channel_id=1, source_target_pairs={{8,16},{16,8},{9,17},{17,9},{10,18},{18,10},{11,19},{19,11},{12,20... | collective-permute-start | bytes 6291464 | tf_op jit(solution)/shard_map/ppermute | solution.py:188
  520.4 82.9 %collective-permute-start.53 = (bf16[1024,1024]{1,0:T(8,128)(2,1)}, bf16[1024,1024]{1,0:T(8,128)(2,1)}, u32[]{:S(2)}, u32[]{:S(2)}) collective-permute-start(bf16[1024,1024]{1,0:T(8,128)(2,1)} %convolution_convert_fusion), channel_id=1, source_target_pairs={{0,4},{4,0},{1,5},{5,1},{2,6},{6,2},{3,7},{7,3},{8,12},{12,8},{9,1... | collective-permute-start | bytes 6291464 | tf_op jit(solution)/shard_map/ppermute | solution.py:35
  566.0 53.8 %collective-permute-start.56 = (bf16[1024,1024]{1,0:T(8,128)(2,1)}, bf16[1024,1024]{1,0:T(8,128)(2,1)}, u32[]{:S(2)}, u32[]{:S(2)}) collective-permute-start(bf16[1024,1024]{1,0:T(8,128)(2,1)} %broadcast_select_fusion.6), channel_id=1, source_target_pairs={{0,8},{8,0},{16,24},{24,16},{1,9},{9,1},{17,25},{25,17},{2,10},{10... | collective-permute-start | bytes 6291464 | tf_op jit(solution)/shard_map/ppermute | solution.py:180
  574.8 48.9 %collective-permute-start.55 = (bf16[1024,1024]{1,0:T(8,128)(2,1)}, bf16[1024,1024]{1,0:T(8,128)(2,1)}, u32[]{:S(2)}, u32[]{:S(2)}) collective-permute-start(bf16[1024,1024]{1,0:T(8,128)(2,1)} %add.348), channel_id=1, source_target_pairs={{8,16},{16,8},{9,17},{17,9},{10,18},{18,10},{11,19},{19,11},{12,20... | collective-permute-start | bytes 6291464 | tf_op jit(solution)/shard_map/ppermute | solution.py:188
  640.2 46.8 %collective-permute-start.59 = (bf16[1024,1024]{1,0:T(8,128)(2,1)}, bf16[1024,1024]{1,0:T(8,128)(2,1)S(1)}, u32[]{:S(2)}, u32[]{:S(2)}) collective-permute-start(bf16[1024,1024]{1,0:T(8,128)(2,1)} %broadcast_select_fusion.5), channel_id=1, source_target_pairs={{0,8},{8,0},{16,24},{24,16},{1,9},{9,1},{17,25},{25,17},{2,10},{10... | collective-permute-start | bytes 6291464 | tf_op jit(solution)/shard_map/ppermute | solution.py:180
  642.4 46.9 %collective-permute-start.58 = (bf16[1024,1024]{1,0:T(8,128)(2,1)}, bf16[1024,1024]{1,0:T(8,128)(2,1)S(1)}, u32[]{:S(2)}, u32[]{:S(2)}) collective-permute-start(bf16[1024,1024]{1,0:T(8,128)(2,1)} %add.351), channel_id=1, source_target_pairs={{8,16},{16,8},{9,17},{17,9},{10,18},{18,10},{11,19},{19,11},{12,20... | collective-permute-start | bytes 6291464 | tf_op jit(solution)/shard_map/ppermute | solution.py:188
  700.1 48.0 %collective-permute-start.61 = (bf16[1024,1024]{1,0:T(8,128)(2,1)}, bf16[1024,1024]{1,0:T(8,128)(2,1)S(1)}, u32[]{:S(2)}, u32[]{:S(2)}) collective-permute-start(bf16[1024,1024]{1,0:T(8,128)(2,1)} %pad_select_fusion.2), channel_id=1, source_target_pairs={{0,8},{8,0},{16,24},{24,16},{1,9},{9,1},{17,25},{25,17},{2,10},{10... | collective-permute-start | bytes 6291464 | tf_op jit(solution)/shard_map/ppermute | solution.py:180
  701.9 48.1 %collective-permute-start.64 = (bf16[1024,1024]{1,0:T(8,128)(2,1)S(1)}, bf16[1024,1024]{1,0:T(8,128)(2,1)S(1)}, u32[]{:S(2)}, u32[]{:S(2)}) collective-permute-start(bf16[1024,1024]{1,0:T(8,128)(2,1)S(1)} %copy-done.34), channel_id=1, source_target_pairs={{8,16},{16,8},{9,17},{17,9},{10,18},{18,10},{11,19},{19,11},{12,20... | collective-permute-start | bytes 6291464 | tf_op jit(solution)/shard_map/ppermute | solution.py:188
  748.1 46.9 %collective-permute-start.62 = (bf16[1024,1024]{1,0:T(8,128)(2,1)S(1)}, bf16[1024,1024]{1,0:T(8,128)(2,1)S(1)}, u32[]{:S(2)}, u32[]{:S(2)}) collective-permute-start(bf16[1024,1024]{1,0:T(8,128)(2,1)S(1)} %pad_select_fusion.1), channel_id=1, source_target_pairs={{0,8},{8,0},{16,24},{24,16},{1,9},{9,1},{17,25},{25,17},{2,10},{10... | collective-permute-start | bytes 6291464 | tf_op jit(solution)/shard_map/ppermute | solution.py:180
  751.7 48.3 %collective-permute-start.70 = (bf16[448,2048]{1,0:T(8,128)(2,1)S(1)}, bf16[448,2048]{1,0:T(8,128)(2,1)S(1)}, u32[]{:S(2)}, u32[]{:S(2)}) collective-permute-start(bf16[448,2048]{1,0:T(8,128)(2,1)S(1)} %add_convert_fusion.5), channel_id=1, source_target_pairs={{0,1},{1,0},{2,3},{3,2},{4,5},{5,4},{6,7},{7,6},{8,9},{9,8},{10,11... | collective-permute-start | bytes 5505032 | tf_op jit(solution)/shard_map/ppermute | solution.py:202
  795.0 46.4 %collective-permute-start.67 = (bf16[1024,1024]{1,0:T(8,128)(2,1)}, bf16[1024,1024]{1,0:T(8,128)(2,1)}, u32[]{:S(2)}, u32[]{:S(2)}) collective-permute-start(bf16[1024,1024]{1,0:T(8,128)(2,1)} %pad_select_fusion), channel_id=1, source_target_pairs={{0,8},{8,0},{16,24},{24,16},{1,9},{9,1},{17,25},{25,17},{2,10},{10... | collective-permute-start | bytes 6291464 | tf_op jit(solution)/shard_map/ppermute | solution.py:180
  (211 other events, 3086.0 us)

commit v4 on v3

--- a/solution.py
+++ b/solution.py
@@ -168,7 +168,7 @@
 
     def step(self):
         count = len(self.loads) - 1
-        before = self.ins[-1:] + self.outs[-1:]
+        before = self.ins[-2:-1] + self.outs[-2:-1]
         load = self.loads[count]
         if isinstance(load, tuple):
             part, total = load

time: 925 us -> 930 us (level)
  waiting for transfers between devices: 269 us -> 228 us
  starting transfers between devices: 121 us -> 158 us
    ppermute x9, waiting for transfers between devices: 97.5 us -> 58.5 us  [step(): lax.ppermute(tie(load, *before), 'grp', [(0, 1), (1, 0), (2, 3), (3, 2)])]
    ppermute x9, starting transfers between devices: 17.3 us -> 52.2 us  [step(): lax.ppermute(tie(load, *before), 'grp', [(0, 1), (1, 0), (2, 3), (3, 2)])]
    ppermute x18, waiting for transfers between devices: 27.4 us -> 40.4 us  [tp_swap(): lax.ppermute(tie(block, *earlier), 'tp', [(i, i ^ bit) for i in range(cou...]
    ppermute x23, waiting for transfers between devices: 93.1 us -> 80.3 us  [move(): self.done.append(lax.ppermute(tie(block, *earlier), axis, pairs))]
    unnamed x333 -> x325, local copies, waits for them, and re-layouts: 31.4 us -> 31.8 us
  transfers between devices with their start and end apart: 80 -> 80, of which waited for: 27 -> 23; matrix products, arithmetic and copies ran while one was open for 45% -> 46% of each run, Pallas kernels for 8% -> 8%
where the time goes in v4:
time: 930 us; the launch traced here: 919 us
  waiting for transfers between devices  228 us (25%)
  other arithmetic  197 us (21%)
  matrix products  160 us (17%)
  starting transfers between devices  158 us (17%)
  local copies, waits for them, and re-layouts  102 us (11%)
  Pallas kernels  70.9 us (8%)
    ppermute x23, waiting for transfers between devices, move(): self.done.append(lax.ppermute(tie(block, *earlier), axis, pairs))  80.3 us
    dot_general x22, matrix products, matmul_tn(): lax.dot_general(a, b, (((0,), (0,)), ((), ())), preferred_element_type=wide)  60.3 us
    ppermute x9, waiting for transfers between devices, step(): lax.ppermute(tie(load, *before), 'grp', [(0, 1), (1, 0), (2, 3), (3, 2)])  58.5 us
    dot_general x8, matrix products, matmul(): return jnp.dot(a, b, preferred_element_type=wide)  52.2 us
    ppermute x9, starting transfers between devices, step(): lax.ppermute(tie(load, *before), 'grp', [(0, 1), (1, 0), (2, 3), (3, 2)])  52.2 us
    dot_general x5, matrix products, matmul_nt(): lax.dot_general(a, b, (((1,), (1,)), ((), ())), preferred_element_type=wide)  47.2 us
    ppermute x18, waiting for transfers between devices, tp_swap(): lax.ppermute(tie(block, *earlier), 'tp', [(i, i ^ bit) for i in range(cou...  40.4 us
    pallas_call x2, Pallas kernels, attend_back(): pl.pallas_call(functools.partial(attend_back_kernel, per_kv=per_kv), grid...  32.7 us
  transfers between devices with their start and end apart: 80, of which 23 were waited for; matrix products, arithmetic and copies ran while one was open for 46% of the time, Pallas kernels for 8%

profile of v4, /device:TPU:0, one launch (start us, length us, event | category | flops | bytes accessed | tf_op | source)
XLA Modules:
  0.0 918.9 jit_solution(15714636452061381643)
XLA Ops:
  13.9 10.4 %collective-permute-done = bf16[896,512]{1,0:T(8,128)(2,1)S(1)} collective-permute-done((bf16[896,512]{1,0:T(8,128)(2,1)}, bf16[896,512]{1,0:T(8,128)(2,1)S(1)}, u32[]{:S(2)}, u32[]{:S(2)}) %collective-permute-start) | collective-permute-done | bytes 917536 | tf_op jit(solution)/shard_map/ppermute | solution.py:202
  90.1 10.4 %attend.2 = (bf16[448,512]{1,0:T(8,128)(2,1)}, f32[448,512]{1,0:T(8,128)}) custom-call(bf16[448,512]{1,0:T(8,128)(2,1)} %get-tuple-element.360.q_ref, bf16[896,128]{1,0:T(8,128)(2,1)} %get-tuple-element.609.k_ref, bf16[896,128]{1,0:T(8,128)(2,1)} %get-tuple-element.608.v_ref, s32[448,4]{1,0:T(8,128)} %copy.105.row_ref, s32[2,896]{1,0:T(2,128)} %copy.106.col_ref), custom_call_target="tpu_custom_call" | custom-call | flops 3288334336 | bytes 2293760 | tf_op jit(solution)/shard_map/attend/pallas_call | solution.py:274
  101.2 10.5 %attend.3 = (bf16[448,512]{1,0:T(8,128)(2,1)}, f32[448,512]{1,0:T(8,128)}) custom-call(bf16[448,512]{1,0:T(8,128)(2,1)} %get-tuple-element.378.q_ref, bf16[896,128]{1,0:T(8,128)(2,1)} %get-tuple-element.607.k_ref, bf16[896,128]{1,0:T(8,128)(2,1)} %get-tuple-element.606.v_ref, s32[448,4]{1,0:T(8,128)} %copy.107.row_ref, s32[2,896]{1,0:T(2,128)} %copy.108.col_ref), custom_call_target="tpu_custom_call" | custom-call | flops 3288334336 | bytes 2293760 | tf_op jit(solution)/shard_map/attend/pallas_call | solution.py:274
  132.2 15.7 %collective-permute-done.14.refs_2_ = bf16[256,2048]{1,0:T(8,128)(2,1)} collective-permute-done((bf16[256,2048]{1,0:T(8,128)(2,1)}, bf16[256,2048]{1,0:T(8,128)(2,1)}, u32[]{:S(2)}, u32[]{:S(2)}) %collective-permute-start.14) | collective-permute-done | bytes 1048608 | tf_op jit(solution)/shard_map/ppermute | solution.py:74
  156.2 13.4 %collective-permute-done.18 = bf16[224,2048]{1,0:T(8,128)(2,1)} collective-permute-done((bf16[224,2048]{1,0:T(8,128)(2,1)S(1)}, bf16[224,2048]{1,0:T(8,128)(2,1)}, u32[]{:S(2)}, u32[]{:S(2)}) %collective-permute-start.18) | collective-permute-done | bytes 917536 | tf_op jit(solution)/shard_map/ppermute | solution.py:202
  179.6 9.1 assemble.2
  207.4 12.1 %fusion.67 = f32[896,2048]{1,0:T(8,128)} fusion(bf16[896,2048]{1,0:T(8,128)(2,1)S(1)} %multiply_convert_fusion.5, bf16[2048,2048]{1,0:T(8,128)(2,1)} %assemble.2), kind=kOutput, calls=%fused_computation.273 | convolution fusion | flops 7516192768 | bytes 19398656 | tf_op jit(solution)/shard_map/dot_general | solution.py:410
  242.8 10.8 %collective-permute-done.26.refs_2_ = bf16[512,1024]{1,0:T(8,128)(2,1)} collective-permute-done((bf16[512,1024]{1,0:T(8,128)(2,1)S(1)}, bf16[512,1024]{1,0:T(8,128)(2,1)}, u32[]{:S(2)}, u32[]{:S(2)}) %collective-permute-start.26) | collective-permute-done | bytes 1048608 | tf_op jit(solution)/shard_map/ppermute | solution.py:74
  260.4 11.7 %multiply_convert_fusion.4 = (bf16[896,2048]{1,0:T(8,128)(2,1)S(1)}, f32[896,2048]{1,0:T(8,128)}) fusion(f32[896,2048]{1,0:T(8,128)} %fusion.67, bf16[512,2048]{1,0:T(8,128)(2,1)S(1)} %collective-permute-done.24, bf16[896,2048]{1,0:T(8,128)(2,1)S(1)} %multiply_convert_fusion.5, f32[896,2048]{1,0:T(8,128)} %fusion.68, f32[896,2048]{1,0:T(8,128)} %fusion.28), kind=kOutput, calls=%fused_computation.18 | convolution fusion | flops 1893728256 | bytes 36044800 | tf_op jit(solution)/shard_map/dot_general | solution.py:410
  296.9 14.0 %pad_maximum_fusion = bf16[2048,2048]{1,0:T(8,128)(2,1)} fusion(bf16[512,2048]{1,0:T(8,128)(2,1)S(1)} %collective-permute-done.24, bf16[512,2048]{1,0:T(8,128)(2,1)} %collective-permute-done.19, bf16[1024,2048]{1,0:T(8,128)(2,1)S(1)} %copy-done.15), kind=kLoop, calls=%fused_computation.6 | loop fusion | flops 25165824 | bytes 16777216 | tf_op jit(solution)/shard_map/concatenate | solution.py:607
  325.9 18.8 %multiply_convert_fusion.1 = (bf16[896,2048]{1,0:T(8,128)(2,1)}, bf16[896,2048]{1,0:T(8,128)(2,1)}) fusion(f32[896,2048]{1,0:T(8,128)} %fusion.67, f32[896,2048]{1,0:T(8,128)} %get-tuple-element.291, bf16[896,2048]{1,0:T(8,128)(2,1)} %copy-done.19, bf16[2048,2048]{1,0:T(8,128)(2,1)} %assemble.3), kind=kOutput, calls=%fused_computation.14 | convolution fusion | flops 7540047872 | bytes 34078720 | tf_op jit(solution)/shard_map/dot_general | solution.py:414
  361.2 21.0 %collective-permute-done.39 = bf16[1024,1024]{1,0:T(8,128)(2,1)} collective-permute-done((bf16[1024,1024]{1,0:T(8,128)(2,1)}, bf16[1024,1024]{1,0:T(8,128)(2,1)}, u32[]{:S(2)}, u32[]{:S(2)}) %collective-permute-start.39) | collective-permute-done | bytes 2097184 | tf_op jit(solution)/shard_map/ppermute | solution.py:35
  390.6 10.1 %fusion.69 = f32[896,2048]{1,0:T(8,128)} fusion(bf16[896,2048]{1,0:T(8,128)(2,1)S(1)} %copy-done.74, bf16[2048,2048]{1,0:T(8,128)(2,1)S(1)} %bitcast.185), kind=kOutput, calls=%fused_computation.275 | convolution fusion | flops 7516192768 | bytes 19398656 | tf_op jit(solution)/shard_map/dot_general | solution.py:414
  400.7 13.1 %convolution_add_fusion = f32[896,2048]{1,0:T(8,128)} fusion(f32[896,2048]{1,0:T(8,128)} %fusion.69, bf16[896,2048]{1,0:T(8,128)(2,1)} %get-tuple-element.315, bf16[2048,2048]{1,0:T(8,128)(2,1)S(1)} %bitcast.183), kind=kOutput, calls=%fused_computation.45 | convolution fusion | flops 7518027776 | bytes 26738688 | tf_op jit(solution)/shard_map/dot_general | solution.py:414
  454.1 30.0 %collective-permute-done.47 = bf16[1024,1024]{1,0:T(8,128)(2,1)S(1)} collective-permute-done((bf16[1024,1024]{1,0:T(8,128)(2,1)}, bf16[1024,1024]{1,0:T(8,128)(2,1)S(1)}, u32[]{:S(2)}, u32[]{:S(2)}) %collective-permute-start.47) | collective-permute-done | bytes 2097184 | tf_op jit(solution)/shard_map/ppermute | solution.py:35
  542.8 16.4 %attend_back.2 = (f32[448,512]{1,0:T(8,128)}, f32[896,128]{1,0:T(8,128)}, f32[896,128]{1,0:T(8,128)}) custom-call(bf16[448,512]{1,0:T(8,128)(2,1)} %get-tuple-element.360.q_ref, bf16[896,128]{1,0:T(8,128)(2,1)} %get-tuple-element.605.k_ref, bf16[896,128]{1,0:T(8,128)(2,1)} %get-tuple-element.604.v_ref, bf16[448,512]{1,0:T(8,128)(2,1)} %get-tuple-element.362.g_ref, ...), custom_call_target="tpu_custom_call" | custom-call | flops 8220835840 | bytes 3211264 | tf_op jit(solution)/shard_map/attend_back/pallas_call | solution.py:353
  578.3 16.4 %attend_back.3 = (f32[448,512]{1,0:T(8,128)}, f32[896,128]{1,0:T(8,128)}, f32[896,128]{1,0:T(8,128)}) custom-call(bf16[448,512]{1,0:T(8,128)(2,1)} %get-tuple-element.378.q_ref, bf16[896,128]{1,0:T(8,128)(2,1)} %get-tuple-element.603.k_ref, bf16[896,128]{1,0:T(8,128)(2,1)} %get-tuple-element.602.v_ref, bf16[448,512]{1,0:T(8,128)(2,1)} %get-tuple-element.380.g_ref, ...), custom_call_target="tpu_custom_call" | custom-call | flops 8220835840 | bytes 3211264 | tf_op jit(solution)/shard_map/attend_back/pallas_call | solution.py:353
  678.5 23.8 %collective-permute-start.64 = (bf16[1024,1024]{1,0:T(8,128)(2,1)S(1)}, bf16[1024,1024]{1,0:T(8,128)(2,1)S(1)}, u32[]{:S(2)}, u32[]{:S(2)}) collective-permute-start(bf16[1024,1024]{1,0:T(8,128)(2,1)S(1)} %copy-done.86), channel_id=1, source_target_pairs={{0,8},{8,0},{16,24},{24,16},{1,9},{9,1},{17,25},{25,17},{2,10},{10... | collective-permute-start | bytes 6291464 | tf_op jit(solution)/shard_map/ppermute | solution.py:180
  715.1 14.4 %collective-permute-start.61 = (bf16[1024,1024]{1,0:T(8,128)(2,1)S(1)}, bf16[1024,1024]{1,0:T(8,128)(2,1)S(1)}, u32[]{:S(2)}, u32[]{:S(2)}) collective-permute-start(bf16[1024,1024]{1,0:T(8,128)(2,1)S(1)} %pad_select_fusion.1), channel_id=1, source_target_pairs={{0,8},{8,0},{16,24},{24,16},{1,9},{9,1},{17,25},{25,17},{2,10},{10... | collective-permute-start | bytes 6291464 | tf_op jit(solution)/shard_map/ppermute | solution.py:180
  729.5 19.3 %collective-permute-done.64 = bf16[1024,1024]{1,0:T(8,128)(2,1)S(1)} collective-permute-done((bf16[1024,1024]{1,0:T(8,128)(2,1)S(1)}, bf16[1024,1024]{1,0:T(8,128)(2,1)S(1)}, u32[]{:S(2)}, u32[]{:S(2)}) %collective-permute-start.64) | collective-permute-done | bytes 2097184 | tf_op jit(solution)/shard_map/ppermute | solution.py:180
  774.9 18.9 %collective-permute-done.61 = bf16[1024,1024]{1,0:T(8,128)(2,1)S(1)} collective-permute-done((bf16[1024,1024]{1,0:T(8,128)(2,1)S(1)}, bf16[1024,1024]{1,0:T(8,128)(2,1)S(1)}, u32[]{:S(2)}, u32[]{:S(2)}) %collective-permute-start.61) | collective-permute-done | bytes 2097184 | tf_op jit(solution)/shard_map/ppermute | solution.py:180
  821.4 17.4 %collective-permute-done.67 = bf16[1024,1024]{1,0:T(8,128)(2,1)} collective-permute-done((bf16[1024,1024]{1,0:T(8,128)(2,1)}, bf16[1024,1024]{1,0:T(8,128)(2,1)}, u32[]{:S(2)}, u32[]{:S(2)}) %collective-permute-start.67) | collective-permute-done | bytes 2097184 | tf_op jit(solution)/shard_map/ppermute | solution.py:180
  868.2 15.5 %collective-permute-done.77 = bf16[512,1024]{1,0:T(8,128)(2,1)S(1)} collective-permute-done((bf16[512,1024]{1,0:T(8,128)(2,1)S(1)}, bf16[512,1024]{1,0:T(8,128)(2,1)S(1)}, u32[]{:S(2)}, u32[]{:S(2)}) %collective-permute-start.77) | collective-permute-done | bytes 1048608 | tf_op jit(solution)/shard_map/ppermute | solution.py:178
  898.9 14.9 %collective-permute-done.73 = bf16[896,512]{1,0:T(8,128)(2,1)S(1)} collective-permute-done((bf16[896,512]{1,0:T(8,128)(2,1)S(1)}, bf16[896,512]{1,0:T(8,128)(2,1)S(1)}, u32[]{:S(2)}, u32[]{:S(2)}) %collective-permute-start.73) | collective-permute-done | bytes 917536 | tf_op jit(solution)/shard_map/ppermute | solution.py:202
  (708 shorter events, 547.1 us)
Async XLA Ops:
  6.2 50.6 %collective-permute-start.2 = (bf16[1024,768]{1,0:T(8,128)(2,1)S(1)}, bf16[1024,768]{1,0:T(8,128)(2,1)}, u32[]{:S(2)}, u32[]{:S(2)}) collective-permute-start(bf16[1024,768]{1,0:T(8,128)(2,1)S(1)} %constant_dynamic-update-slice_fusion.8), channel_id=1, source_target_pairs={{4,0},{0,4},{5,1},{1,5},{6,2},{2,6},{7,3},{3,7},{12,8},{8,12},{13,... | collective-permute-start | bytes 4718600 | tf_op jit(solution)/shard_map/ppermute | solution.py:35
  11.2 59.7 %collective-permute-start.8 = (bf16[256,2048]{1,0:T(8,128)(2,1)}, bf16[256,2048]{1,0:T(8,128)(2,1)}, u32[]{:S(2)}, u32[]{:S(2)}) collective-permute-start(bf16[256,2048]{1,0:T(8,128)(2,1)} %constant_dynamic-slice_fusion.2), channel_id=1, source_target_pairs={{4,0},{0,4},{5,1},{1,5},{6,2},{2,6},{7,3},{3,7},{12,8},{8,12},{13,... | collective-permute-start | bytes 3145736 | tf_op jit(solution)/shard_map/ppermute | solution.py:35
  119.3 52.7 %collective-permute-start.19 = (bf16[512,2048]{1,0:T(8,128)(2,1)}, bf16[512,2048]{1,0:T(8,128)(2,1)}, u32[]{:S(2)}, u32[]{:S(2)}) collective-permute-start(bf16[512,2048]{1,0:T(8,128)(2,1)} %get-tuple-element.264), channel_id=1, source_target_pairs={{4,0},{0,4},{5,1},{1,5},{6,2},{2,6},{7,3},{3,7},{12,8},{8,12},{13,... | collective-permute-start | bytes 6291464 | tf_op jit(solution)/shard_map/ppermute | solution.py:35
  201.4 58.9 %collective-permute-start.24 = (bf16[512,2048]{1,0:T(8,128)(2,1)S(1)}, bf16[512,2048]{1,0:T(8,128)(2,1)S(1)}, u32[]{:S(2)}, u32[]{:S(2)}) collective-permute-start(bf16[512,2048]{1,0:T(8,128)(2,1)S(1)} %copy-done.87), channel_id=1, source_target_pairs={{4,0},{0,4},{5,1},{1,5},{6,2},{2,6},{7,3},{3,7},{12,8},{8,12},{13,... | collective-permute-start | bytes 6291464 | tf_op jit(solution)/shard_map/ppermute | solution.py:35
  253.6 61.9 %collective-permute-start.27 = (bf16[512,1024]{1,0:T(8,128)(2,1)}, bf16[512,1024]{1,0:T(8,128)(2,1)}, u32[]{:S(2)}, u32[]{:S(2)}) collective-permute-start(bf16[512,1024]{1,0:T(8,128)(2,1)} %collective-permute-done.26.refs_2_), channel_id=1, source_target_pairs={{0,8},{8,16},{16,24},{1,9},{9,17},{17,25},{2,10},{10,18},{18,26},{... | collective-permute-start | bytes 3145736 | tf_op jit(solution)/shard_map/ppermute | solution.py:74
  259.1 56.7 %collective-permute-start.30 = (bf16[512,1024]{1,0:T(8,128)(2,1)}, bf16[512,1024]{1,0:T(8,128)(2,1)}, u32[]{:S(2)}, u32[]{:S(2)}) collective-permute-start(bf16[512,1024]{1,0:T(8,128)(2,1)} %collective-permute-done.29.refs_5_), channel_id=1, source_target_pairs={{8,0},{16,8},{24,16},{9,1},{17,9},{25,17},{10,2},{18,10},{26,18},{... | collective-permute-start | bytes 3145736 | tf_op jit(solution)/shard_map/ppermute | solution.py:77
  315.5 66.7 %collective-permute-start.39 = (bf16[1024,1024]{1,0:T(8,128)(2,1)}, bf16[1024,1024]{1,0:T(8,128)(2,1)}, u32[]{:S(2)}, u32[]{:S(2)}) collective-permute-start(bf16[1024,1024]{1,0:T(8,128)(2,1)} %convolution_convert_fusion.4), channel_id=1, source_target_pairs={{0,4},{4,0},{1,5},{5,1},{2,6},{6,2},{3,7},{7,3},{8,12},{12,8},{9,1... | collective-permute-start | bytes 6291464 | tf_op jit(solution)/shard_map/ppermute | solution.py:35
  359.5 60.8 %collective-permute-start.42 = (bf16[1024,1024]{1,0:T(8,128)(2,1)}, bf16[1024,1024]{1,0:T(8,128)(2,1)}, u32[]{:S(2)}, u32[]{:S(2)}) collective-permute-start(bf16[1024,1024]{1,0:T(8,128)(2,1)} %convolution_convert_fusion.3), channel_id=1, source_target_pairs={{0,4},{4,0},{1,5},{5,1},{2,6},{6,2},{3,7},{7,3},{8,12},{12,8},{9,1... | collective-permute-start | bytes 6291464 | tf_op jit(solution)/shard_map/ppermute | solution.py:35
  435.9 48.2 %collective-permute-start.47 = (bf16[1024,1024]{1,0:T(8,128)(2,1)}, bf16[1024,1024]{1,0:T(8,128)(2,1)S(1)}, u32[]{:S(2)}, u32[]{:S(2)}) collective-permute-start(bf16[1024,1024]{1,0:T(8,128)(2,1)} %convolution_convert_fusion.2), channel_id=1, source_target_pairs={{0,4},{4,0},{1,5},{5,1},{2,6},{6,2},{3,7},{7,3},{8,12},{12,8},{9,1... | collective-permute-start | bytes 6291464 | tf_op jit(solution)/shard_map/ppermute | solution.py:35
  441.4 50.0 %collective-permute-start.46 = (bf16[1024,1024]{1,0:T(8,128)(2,1)S(1)}, bf16[1024,1024]{1,0:T(8,128)(2,1)S(1)}, u32[]{:S(2)}, u32[]{:S(2)}) collective-permute-start(bf16[1024,1024]{1,0:T(8,128)(2,1)S(1)} %copy-done.85), channel_id=1, source_target_pairs={{0,8},{8,0},{16,24},{24,16},{1,9},{9,1},{17,25},{25,17},{2,10},{10... | collective-permute-start | bytes 6291464 | tf_op jit(solution)/shard_map/ppermute | solution.py:180
  445.3 48.4 %collective-permute-start.45 = (bf16[1024,1024]{1,0:T(8,128)(2,1)S(1)}, bf16[1024,1024]{1,0:T(8,128)(2,1)S(1)}, u32[]{:S(2)}, u32[]{:S(2)}) collective-permute-start(bf16[1024,1024]{1,0:T(8,128)(2,1)S(1)} %copy-done.38), channel_id=1, source_target_pairs={{8,16},{16,8},{9,17},{17,9},{10,18},{18,10},{11,19},{19,11},{12,20... | collective-permute-start | bytes 6291464 | tf_op jit(solution)/shard_map/ppermute | solution.py:188
  509.9 57.8 %collective-permute-start.50 = (bf16[1024,1024]{1,0:T(8,128)(2,1)}, bf16[1024,1024]{1,0:T(8,128)(2,1)}, u32[]{:S(2)}, u32[]{:S(2)}) collective-permute-start(bf16[1024,1024]{1,0:T(8,128)(2,1)} %pad_select_fusion.3), channel_id=1, source_target_pairs={{0,8},{8,0},{16,24},{24,16},{1,9},{9,1},{17,25},{25,17},{2,10},{10... | collective-permute-start | bytes 6291464 | tf_op jit(solution)/shard_map/ppermute | solution.py:180
  511.6 48.8 %collective-permute-start.51 = (bf16[1024,1024]{1,0:T(8,128)(2,1)}, bf16[1024,1024]{1,0:T(8,128)(2,1)}, u32[]{:S(2)}, u32[]{:S(2)}) collective-permute-start(bf16[1024,1024]{1,0:T(8,128)(2,1)} %convolution_convert_fusion.1), channel_id=1, source_target_pairs={{0,4},{4,0},{1,5},{5,1},{2,6},{6,2},{3,7},{7,3},{8,12},{12,8},{9,1... | collective-permute-start | bytes 6291464 | tf_op jit(solution)/shard_map/ppermute | solution.py:35
  512.6 59.5 %collective-permute-start.49 = (bf16[1024,1024]{1,0:T(8,128)(2,1)}, bf16[1024,1024]{1,0:T(8,128)(2,1)}, u32[]{:S(2)}, u32[]{:S(2)}) collective-permute-start(bf16[1024,1024]{1,0:T(8,128)(2,1)} %add.344), channel_id=1, source_target_pairs={{8,16},{16,8},{9,17},{17,9},{10,18},{18,10},{11,19},{19,11},{12,20... | collective-permute-start | bytes 6291464 | tf_op jit(solution)/shard_map/ppermute | solution.py:188
  520.4 84.2 %collective-permute-start.53 = (bf16[1024,1024]{1,0:T(8,128)(2,1)}, bf16[1024,1024]{1,0:T(8,128)(2,1)}, u32[]{:S(2)}, u32[]{:S(2)}) collective-permute-start(bf16[1024,1024]{1,0:T(8,128)(2,1)} %convolution_convert_fusion), channel_id=1, source_target_pairs={{0,4},{4,0},{1,5},{5,1},{2,6},{6,2},{3,7},{7,3},{8,12},{12,8},{9,1... | collective-permute-start | bytes 6291464 | tf_op jit(solution)/shard_map/ppermute | solution.py:35
  567.3 54.2 %collective-permute-start.56 = (bf16[1024,1024]{1,0:T(8,128)(2,1)}, bf16[1024,1024]{1,0:T(8,128)(2,1)}, u32[]{:S(2)}, u32[]{:S(2)}) collective-permute-start(bf16[1024,1024]{1,0:T(8,128)(2,1)} %broadcast_select_fusion.6), channel_id=1, source_target_pairs={{0,8},{8,0},{16,24},{24,16},{1,9},{9,1},{17,25},{25,17},{2,10},{10... | collective-permute-start | bytes 6291464 | tf_op jit(solution)/shard_map/ppermute | solution.py:180
  575.4 49.9 %collective-permute-start.55 = (bf16[1024,1024]{1,0:T(8,128)(2,1)}, bf16[1024,1024]{1,0:T(8,128)(2,1)}, u32[]{:S(2)}, u32[]{:S(2)}) collective-permute-start(bf16[1024,1024]{1,0:T(8,128)(2,1)} %add.348), channel_id=1, source_target_pairs={{8,16},{16,8},{9,17},{17,9},{10,18},{18,10},{11,19},{19,11},{12,20... | collective-permute-start | bytes 6291464 | tf_op jit(solution)/shard_map/ppermute | solution.py:188
  612.3 49.9 %collective-permute-start.59 = (bf16[1024,1024]{1,0:T(8,128)(2,1)}, bf16[1024,1024]{1,0:T(8,128)(2,1)}, u32[]{:S(2)}, u32[]{:S(2)}) collective-permute-start(bf16[1024,1024]{1,0:T(8,128)(2,1)} %broadcast_select_fusion.5), channel_id=1, source_target_pairs={{0,8},{8,0},{16,24},{24,16},{1,9},{9,1},{17,25},{25,17},{2,10},{10... | collective-permute-start | bytes 6291464 | tf_op jit(solution)/shard_map/ppermute | solution.py:180
  678.5 70.3 %collective-permute-start.64 = (bf16[1024,1024]{1,0:T(8,128)(2,1)S(1)}, bf16[1024,1024]{1,0:T(8,128)(2,1)S(1)}, u32[]{:S(2)}, u32[]{:S(2)}) collective-permute-start(bf16[1024,1024]{1,0:T(8,128)(2,1)S(1)} %copy-done.86), channel_id=1, source_target_pairs={{0,8},{8,0},{16,24},{24,16},{1,9},{9,1},{17,25},{25,17},{2,10},{10... | collective-permute-start | bytes 6291464 | tf_op jit(solution)/shard_map/ppermute | solution.py:180
  702.4 46.5 %collective-permute-start.63 = (bf16[1024,1024]{1,0:T(8,128)(2,1)S(1)}, bf16[1024,1024]{1,0:T(8,128)(2,1)S(1)}, u32[]{:S(2)}, u32[]{:S(2)}) collective-permute-start(bf16[1024,1024]{1,0:T(8,128)(2,1)S(1)} %copy-done.32), channel_id=1, source_target_pairs={{8,16},{16,8},{9,17},{17,9},{10,18},{18,10},{11,19},{19,11},{12,20... | collective-permute-start | bytes 6291464 | tf_op jit(solution)/shard_map/ppermute | solution.py:188
  715.1 78.7 %collective-permute-start.61 = (bf16[1024,1024]{1,0:T(8,128)(2,1)S(1)}, bf16[1024,1024]{1,0:T(8,128)(2,1)S(1)}, u32[]{:S(2)}, u32[]{:S(2)}) collective-permute-start(bf16[1024,1024]{1,0:T(8,128)(2,1)S(1)} %pad_select_fusion.1), channel_id=1, source_target_pairs={{0,8},{8,0},{16,24},{24,16},{1,9},{9,1},{17,25},{25,17},{2,10},{10... | collective-permute-start | bytes 6291464 | tf_op jit(solution)/shard_map/ppermute | solution.py:180
  750.6 46.7 %collective-permute-start.70 = (bf16[448,2048]{1,0:T(8,128)(2,1)S(1)}, bf16[448,2048]{1,0:T(8,128)(2,1)S(1)}, u32[]{:S(2)}, u32[]{:S(2)}) collective-permute-start(bf16[448,2048]{1,0:T(8,128)(2,1)S(1)} %add_convert_fusion.5), channel_id=1, source_target_pairs={{0,1},{1,0},{2,3},{3,2},{4,5},{5,4},{6,7},{7,6},{8,9},{9,8},{10,11... | collective-permute-start | bytes 5505032 | tf_op jit(solution)/shard_map/ppermute | solution.py:202
  771.6 67.2 %collective-permute-start.67 = (bf16[1024,1024]{1,0:T(8,128)(2,1)}, bf16[1024,1024]{1,0:T(8,128)(2,1)}, u32[]{:S(2)}, u32[]{:S(2)}) collective-permute-start(bf16[1024,1024]{1,0:T(8,128)(2,1)} %pad_select_fusion), channel_id=1, source_target_pairs={{0,8},{8,0},{16,24},{24,16},{1,9},{9,1},{17,25},{25,17},{2,10},{10... | collective-permute-start | bytes 6291464 | tf_op jit(solution)/shard_map/ppermute | solution.py:180
  817.5 46.3 %collective-permute-start.74 = (bf16[512,1024]{1,0:T(8,128)(2,1)}, bf16[512,1024]{1,0:T(8,128)(2,1)S(1)}, u32[]{:S(2)}, u32[]{:S(2)}) collective-permute-start(bf16[512,1024]{1,0:T(8,128)(2,1)} %pad_select_fusion.6), channel_id=1, source_target_pairs={{0,8},{8,0},{16,24},{24,16},{1,9},{9,1},{17,25},{25,17},{2,10},{10... | collective-permute-start | bytes 3145736 | tf_op jit(solution)/shard_map/ppermute | solution.py:180
  (207 other events, 3105.9 us)
